TPU v7x, 128 devices: a whole 4x4x4 slice. The times are simulated.
128 devices in a mesh: ctx: 8 (over z, y_hi), tp: 16 (over y_lo, x, core).
Axes of the slice: x: 4, y: 4 (y_hi: 2, y_lo: 2; y = y_hi * 2 + y_lo), z: 4, core: 2. Of those that a mesh axis runs over, the one named last changes fastest.
Arguments:
- byte_embeds: bfloat16 [24576, 1024], P(('ctx', 'tp')), may hold values from -6 to 6
- local_embeds: bfloat16 [24576, 1024], P(('ctx', 'tp')), may hold values from -6 to 6
- global_qkv: bfloat16 [3, 8192, 4096], P(None, None, 'tp'), may hold values from -0.0625 to 0.0625
- global_out: bfloat16 [4096, 8192], P('tp'), may hold values from -1.5 to 1.5
- local_qkv: bfloat16 [1, 1024, 3072], replicated, may hold values from -0.1875 to 0.1875
- local_out: bfloat16 [1, 1024, 1024], replicated, may hold values from -0.1875 to 0.1875
- cotangent: bfloat16 [24576, 1024], P(('ctx', 'tp')), may hold values from -6 to 6
Outputs:
- hidden: bfloat16 [24576, 1024], P(('ctx', 'tp'))
- grad_qkv: float32 [1, 1024, 3072], P(None, ('ctx', 'tp'))
- grad_out: float32 [1, 1024, 1024], P(None, ('ctx', 'tp'))
All inputs are finite; a program needn't handle non-finite values.
Results may differ from a plain program's by a relative error of at most 0.028.
Values may be sent and summed in bfloat16 or wider, within the bound.
A program may use at most 128 MiB of HBM per device.

v0:
```python
import math

import jax
import jax.numpy as jnp
from jax import lax
from jax.sharding import PartitionSpec as P

PATCH = 8
HEAD_DIM = 128
LOCAL_HEADS = 8
LOCAL_HEAD_DIM = 128


def from_behind(value, axis, steps):
    count = lax.axis_size(axis)
    initial, last = (max(0, -steps), min(count, count - steps))
    return lax.ppermute(value, axis, [(source, source + steps) for source in range(initial, last)])


def rms_norm(values):
    return values * lax.rsqrt(jnp.mean(values * values, axis=-1, keepdims=True) + 1e-06)


def local_core(qkv_rows):
    total = qkv_rows.shape[0]
    groups = total // PATCH
    width = qkv_rows.shape[1] // 3
    parts = qkv_rows.reshape(groups, PATCH, 3, LOCAL_HEADS, LOCAL_HEAD_DIM)
    queries = rms_norm(parts[:, :, 0])
    keys_all = rms_norm(parts[:, :, 1])
    values = parts[:, :, 2]
    scores = jnp.einsum("npha,nqha->nhpq", queries, keys_all) / math.sqrt(LOCAL_HEAD_DIM)
    causal = jnp.arange(PATCH)[:, None] >= jnp.arange(PATCH)[None, :]
    weights = jnp.where(causal[None, None], jnp.exp(scores), 0.0)
    numerator = jnp.einsum("nhpq,nqha->npha", weights, values)
    denominator = jnp.sum(weights, axis=-1).transpose(0, 2, 1)[..., None]
    return (numerator / denominator).reshape(total, width)


def local_pass(state, local_qkv, local_out, cotangent):
    layer = 0
    normed = rms_norm(state).astype(jnp.bfloat16)
    qkv_rows = jnp.dot(normed, local_qkv[layer], preferred_element_type=jnp.float32)
    core, core_back = jax.vjp(local_core, qkv_rows)
    attended = core.astype(jnp.bfloat16)
    saved = [(state, normed, core_back, attended)]
    state = state + jnp.dot(attended, local_out[layer], preferred_element_type=jnp.float32)
    hidden = state.astype(jnp.bfloat16)
    grad_state = cotangent.astype(jnp.float32)
    layer = 0
    before, normed, core_back, attended = saved[layer]
    grad_round = grad_state.astype(jnp.bfloat16)
    grads_out = [jnp.dot(attended.T, grad_round, preferred_element_type=jnp.float32)]
    grad_core = jnp.dot(grad_round, local_out[layer].T, preferred_element_type=jnp.float32)
    grad_rows = core_back(grad_core)[0].astype(jnp.bfloat16)
    grads_qkv = [jnp.dot(normed.T, grad_rows, preferred_element_type=jnp.float32)]
    return (hidden, jnp.stack(grads_qkv[::-1]), jnp.stack(grads_out[::-1]))


def per_device(byte_embeds, local_embeds, global_qkv, global_out, local_qkv, local_out, cotangent):
    byte_count = byte_embeds.shape[0]
    patch_count = byte_count // PATCH
    full_width = PATCH * byte_embeds.shape[1]
    patch_in = byte_embeds.reshape(patch_count, full_width).astype(jnp.float32)
    normed = rms_norm(patch_in).astype(jnp.bfloat16)
    projected = jnp.einsum(
        "nd,cdh->nch",
        lax.all_gather(normed, "tp", axis=0, tiled=True),
        global_qkv,
        preferred_element_type=jnp.float32,
    )
    shard_rows = projected.shape[0]
    head_width = global_qkv.shape[2]
    head_count = head_width // HEAD_DIM
    queries = rms_norm(projected[:, 0].reshape(shard_rows, head_count, HEAD_DIM)).astype(
        jnp.bfloat16
    )
    keys_mine = rms_norm(projected[:, 1].reshape(shard_rows, head_count, HEAD_DIM)).astype(
        jnp.bfloat16
    )
    values_mine = projected[:, 2].reshape(shard_rows, head_count, HEAD_DIM).astype(jnp.bfloat16)
    query_pos = lax.axis_index("ctx") * shard_rows + jnp.arange(shard_rows, dtype=jnp.int32)
    key_piece = lax.all_gather(keys_mine, "ctx", axis=0, tiled=True)
    value_piece = lax.all_gather(values_mine, "ctx", axis=0, tiled=True)
    key_count = key_piece.shape[0]
    scores = jnp.einsum(
        "rha,kha->rhk", queries, key_piece, preferred_element_type=jnp.float32
    ) / math.sqrt(HEAD_DIM)
    key_pos = jnp.arange(key_count, dtype=jnp.int32)
    allowed = key_pos[None, None, :] <= query_pos[:, None, None]
    expo = jnp.where(allowed, jnp.exp(scores), 0.0)
    numerator = jnp.einsum(
        "rhk,kha->rha", expo.astype(jnp.bfloat16), value_piece, preferred_element_type=jnp.float32
    )
    denominator = jnp.sum(expo, axis=-1)
    numerator, denominator = (numerator, denominator)
    attended = (
        (numerator / denominator[..., None]).reshape(shard_rows, head_width).astype(jnp.bfloat16)
    )
    patch_out = lax.psum_scatter(
        jnp.dot(attended, global_out, preferred_element_type=jnp.float32).astype(jnp.bfloat16),
        "tp",
        scatter_dimension=0,
        tiled=True,
    )
    earlier_row = from_behind(patch_out[-1:], ("ctx", "tp"), 1)
    patch_out = jnp.concatenate([earlier_row, patch_out[:-1]], axis=0)
    context = patch_out.reshape(byte_count, byte_embeds.shape[1])
    state = local_embeds.astype(jnp.float32) + context.astype(jnp.float32)
    hidden, grad_qkv, grad_out = local_pass(state, local_qkv, local_out, cotangent)
    grad_qkv, grad_out = (
        lax.psum_scatter(grad_qkv, ("ctx", "tp"), scatter_dimension=1, tiled=True),
        lax.psum_scatter(grad_out, ("ctx", "tp"), scatter_dimension=1, tiled=True),
    )
    return (hidden, grad_qkv, grad_out)


def solution(mesh):
    in_specs = (
        P(("ctx", "tp"), None),
        P(("ctx", "tp"), None),
        P(None, None, "tp"),
        P("tp", None),
        P(),
        P(),
        P(("ctx", "tp"), None),
    )
    out_specs = (P(("ctx", "tp"), None), P(None, ("ctx", "tp"), None), P(None, ("ctx", "tp"), None))
    return jax.shard_map(
        per_device, mesh=mesh, in_specs=in_specs, out_specs=out_specs, check_vma=False
    )
```

profile of v0, /device:TPU:1, one launch (start us, length us, event | category | flops | bytes accessed | tf_op | source)
XLA Modules:
  0.0 1155.5 jit_solution(7614287349965638369)
XLA Ops:
  7.2 1.3 reshape.139
  8.5 1.2 multiply_reduce_fusion.6
  10.8 46.0 %all-gather.4.cloned.1.call-done = bf16[384,8192]{1,0:T(8,128)(2,1)} async-done(((bf16[24,8192]{1,0:T(8,128)(2,1)}), bf16[384,8192]{1,0:T(8,128)(2,1)}) %all-gather.4.cloned.1.call-update) | async-done | bytes 6291472 | tf_op jit(solution)/shard_map/all_gather | solution.py:68
  56.9 11.2 fusion.2
  68.2 0.9 copy-done.16
  70.3 1.7 slice.71
  72.0 2.0 iota_compare_fusion
  75.0 44.3 %all-gather.8.cloned.1.call-done = bf16[3072,2,128]{2,0,1:T(8,128)(2,1)} async-done(((bf16[384,2,128]{2,0,1:T(8,128)(2,1)}), bf16[3072,2,128]{2,0,1:T(8,128)(2,1)}) %all-gather.8.cloned.1.call-update) | async-done | bytes 1572880 | tf_op jit(solution)/shard_map/all_gather | solution.py:83
  119.3 7.9 fusion
  127.2 42.9 %all-gather.6.cloned.1.call-done = bf16[3072,2,128]{0,2,1:T(8,128)(2,1)} async-done(((bf16[384,2,128]{0,2,1:T(8,128)(2,1)}), bf16[3072,2,128]{0,2,1:T(8,128)(2,1)}) %all-gather.6.cloned.1.call-update) | async-done | bytes 1572880 | tf_op jit(solution)/shard_map/all_gather | solution.py:84
  170.1 6.5 fusion.27
  176.6 4.5 convolution_convert_fusion
  182.1 1.7 fusion.38
  183.8 63.1 %reduce-scatter.4.cloned.1.call-done = bf16[24,8192]{1,0:T(8,128)(2,1)} async-done(((bf16[384,8192]{1,0:T(8,128)(2,1)}), bf16[24,8192]{1,0:T(8,128)(2,1)}) %reduce-scatter.4.cloned.1.call-update) | async-done | bytes 393232 | tf_op jit(solution)/shard_map/reduce_scatter | solution.py:100
  247.9 3.5 collective-permute-start
  251.4 8.7 copy.36
  260.1 1.0 maximum_convert_fusion
  261.1 1.3 reshape.140
  262.6 1.1 multiply_convert_fusion
  263.7 4.3 fusion.40
  269.9 1.3 multiply_reduce_fusion.2
  272.2 3.2 convolution_bitcast_fusion.1
  275.5 1.1 negate_bitcast_fusion
  276.5 2.1 fusion.16
  280.8 1.0 fusion.30
  282.1 1.2 copy.28
  283.3 3.0 convert_element_type.83
  286.3 7.6 convolution_bitcast_fusion
  294.0 1.0 copy-done.8
  295.0 2.5 fusion.18
  297.5 625.1 %reduce-scatter.8.cloned.1.call-done = f32[1,8,1024]{2,1,0:T(8,128)} async-done(((f32[1,1024,1024]{2,1,0:T(8,128)}), f32[1,8,1024]{2,1,0:T(8,128)}) %reduce-scatter.8.cloned.1.call-update) | async-done | bytes 32784 | tf_op jit(solution)/shard_map/reduce_scatter | solution.py:113
  922.6 226.1 %reduce-scatter.6.cloned.1.call-done = f32[1,8,3072]{2,1,0:T(8,128)} async-done(((f32[1,1024,3072]{2,1,0:T(8,128)}), f32[1,8,3072]{2,1,0:T(8,128)}) %reduce-scatter.6.cloned.1.call-update) | async-done | bytes 98320 | tf_op jit(solution)/shard_map/reduce_scatter | solution.py:112
  (84 shorter events, 10.6 us)
Async XLA Ops:
  7.2 174.0 %copy-start = (bf16[1,1024,1024]{2,1,0:T(8,128)(2,1)S(1)}, bf16[1,1024,1024]{2,1,0:T(8,128)(2,1)}, u32[]{:S(2)}) copy-start(bf16[1,1024,1024]{2,1,0:T(8,128)(2,1)} %param.12) | copy-start | bytes 6291460
  7.2 49.7 %all-gather.4.cloned.1.call-start = ((), (), s32[]{:S(2)}) async-start(), calls=%async_computation.3 | async-start | bytes 6684672 | tf_op jit(solution)/shard_map/all_gather | solution.py:68
  10.8 108.5 %all-gather.8.cloned.1.call-start = ((), (), s32[]{:S(2)}) async-start(), calls=%async_computation.5 | async-start | bytes 1769472 | tf_op jit(solution)/shard_map/all_gather | solution.py:83
  68.1 1.0 copy-start.16
  70.2 99.9 %all-gather.6.cloned.1.call-start = ((), (), s32[]{:S(2)}) async-start(), calls=%async_computation.4 | async-start | bytes 1769472 | tf_op jit(solution)/shard_map/all_gather | solution.py:84
  72.0 175.0 %reduce-scatter.4.cloned.1.call-start = ((), (), s32[]{:S(2)}) async-start(), calls=%async_computation.6 | async-start | bytes 6684672 | tf_op jit(solution)/shard_map/reduce_scatter | solution.py:100
  75.0 95.1 %copy-start.11 = (pred[384,3072]{0,1:T(8,128)(4,1)S(1)}, pred[384,3072]{0,1:T(8,128)(4,1)}, u32[]{:S(2)}) copy-start(pred[384,3072]{0,1:T(8,128)(4,1)} %iota_compare_fusion) | copy-start | bytes 3538948
  170.1 6.6 copy-start.3
  181.1 1.0 copy-start.9
  181.2 741.4 %reduce-scatter.8.cloned.1.call-start = ((), (), s32[]{:S(2)}) async-start(), calls=%async_computation.8 | async-start | bytes 4227072 | tf_op jit(solution)/shard_map/reduce_scatter | solution.py:113
  247.9 12.2 %collective-permute-start = (bf16[1,8192]{1,0:T(2,128)(2,1)S(1)}, bf16[1,8192]{1,0:T(2,128)(2,1)S(1)}, u32[]{:S(2)}, u32[]{:S(2)}) collective-permute-start(bf16[1,8192]{1,0:T(2,128)(2,1)S(1)} %slice.36), channel_id=1, source_target_pairs={{0,1},{1,2},{2,3},{3,4},{4,5},{5,6},{6,7},{7,8},{8,9},{9,10},{10,1... | collective-permute-start | bytes 49160 | tf_op jit(solution)/shard_map/ppermute | solution.py:17
  251.4 8.7 copy-start.19
  260.1 2.3 copy-start.7
  268.0 1.9 copy-start.1
  268.0 1.9 copy-start.4
  268.5 0.6 copy-start.14
  268.5 0.7 copy-start.12
  269.8 1.4 copy-start.17
  269.8 1.4 copy-start.20
  269.8 2.3 copy-start.10
  271.2 0.9 copy-start.6
  275.4 873.3 %reduce-scatter.6.cloned.1.call-start = ((), (), s32[]{:S(2)}) async-start(), calls=%async_computation.7 | async-start | bytes 12681216 | tf_op jit(solution)/shard_map/reduce_scatter | solution.py:112
  275.5 3.2 copy-start.2
  278.6 1.6 copy-start.13
  278.7 1.6 copy-start.15
  278.7 1.6 copy-start.5
  278.7 1.6 copy-start.18
  278.7 1.6 copy-start.21
  293.9 1.0 copy-start.8
  293.9 1.0 copy-start.22
Sparse Core Ops, SparseCore 0:
  10.9 45.9 all-gather.3
  70.3 48.8 all-gather.7
  121.5 48.5 all-gather.5
  181.3 65.6 reduce-scatter.3
  275.5 647.0 reduce-scatter.7
  928.0 220.6 reduce-scatter.5
where the time goes:
time: 1160 us
  waiting for transfers between devices  1050 us (91%)
  matrix products  55.6 us (5%)
  local copies, waits for them, and re-layouts  23.8 us (2%)
  between operations  14.5 us (1%)
    reduce_scatter x1, waiting for transfers between devices, per_device(): lax.psum_scatter(grad_out, ('ctx', 'tp'), scatter_dimension=1, tiled=True)  625 us
    reduce_scatter x1, waiting for transfers between devices, per_device(): lax.psum_scatter(grad_qkv, ('ctx', 'tp'), scatter_dimension=1, tiled=True)  226 us
    reduce_scatter x1, waiting for transfers between devices, per_device(): lax.psum_scatter(jnp.dot(attended, global_out, preferred_element_type=jnp...  63.1 us
    all_gather x1, waiting for transfers between devices, per_device(): lax.all_gather(normed, 'tp', axis=0, tiled=True)  46 us
    all_gather x1, waiting for transfers between devices, per_device(): key_piece = lax.all_gather(keys_mine, 'ctx', axis=0, tiled=True)  44.3 us
    all_gather x1, waiting for transfers between devices, per_device(): value_piece = lax.all_gather(values_mine, 'ctx', axis=0, tiled=True)  42.9 us
  transfers between devices with their start and end apart: 7, of which 6 were waited for; matrix products, arithmetic and copies ran while one was open for 4% of the time, Pallas kernels for 0%

commit v1 on v0

--- a/solution.py
+++ b/solution.py
@@ -80,8 +80,10 @@
     )
     values_mine = projected[:, 2].reshape(shard_rows, head_count, HEAD_DIM).astype(jnp.bfloat16)
     query_pos = lax.axis_index("ctx") * shard_rows + jnp.arange(shard_rows, dtype=jnp.int32)
-    key_piece = lax.all_gather(keys_mine, "ctx", axis=0, tiled=True)
-    value_piece = lax.all_gather(values_mine, "ctx", axis=0, tiled=True)
+    pieces = lax.all_gather(
+        jnp.concatenate([keys_mine, values_mine], axis=1), "ctx", axis=0, tiled=True
+    )
+    key_piece, value_piece = pieces[:, :head_count], pieces[:, head_count:]
     key_count = key_piece.shape[0]
     scores = jnp.einsum(
         "rha,kha->rhk", queries, key_piece, preferred_element_type=jnp.float32
@@ -108,10 +110,17 @@
     context = patch_out.reshape(byte_count, byte_embeds.shape[1])
     state = local_embeds.astype(jnp.float32) + context.astype(jnp.float32)
     hidden, grad_qkv, grad_out = local_pass(state, local_qkv, local_out, cotangent)
-    grad_qkv, grad_out = (
-        lax.psum_scatter(grad_qkv, ("ctx", "tp"), scatter_dimension=1, tiled=True),
-        lax.psum_scatter(grad_out, ("ctx", "tp"), scatter_dimension=1, tiled=True),
+    width = grad_qkv.shape[2]
+    grads = jnp.concatenate([grad_qkv[0], grad_out[0]], axis=1)
+    ctx_count, tp_count = lax.axis_size("ctx"), lax.axis_size("tp")
+    grads = grads.reshape(ctx_count, tp_count, -1, grads.shape[1]).transpose(1, 0, 2, 3)
+    grads = grads.reshape(-1, grads.shape[3]).astype(jnp.bfloat16)
+    grads = lax.psum_scatter(grads, "tp", scatter_dimension=0, tiled=True)
+    grads = lax.psum_scatter(
+        grads.astype(jnp.float32), "ctx", scatter_dimension=0, tiled=True
     )
+    grads = grads.reshape(1, -1, grads.shape[1])
+    grad_qkv, grad_out = grads[:, :, :width], grads[:, :, width:]
     return (hidden, grad_qkv, grad_out)
 
 

time: 1160 us -> 428 us (0.37)
  waiting for transfers between devices: 1050 us -> 316 us
  matrix products: 55.6 us -> 44 us
    reduce_scatter x2, waiting for transfers between devices: 851 us -> 147 us  [the longest x1 75.1 us: per_device(): grads = lax.psum_scatter(grads, 'tp', scatter_dimension=0, tiled=True)]
    all_gather x2 -> x1, waiting for transfers between devices: 87.2 us -> 59.2 us  [per_device(): lax.all_gather(jnp.concatenate([keys_mine, values_mine], axis=1), 'ctx',...]
  transfers between devices with their start and end apart: 7 -> 6, of which waited for: 6 -> 5; matrix products, arithmetic and copies ran while one was open for 4% -> 4% of each run, Pallas kernels for 0% -> 0%
where the time goes in v1:
time: 428 us; the launch traced here: 426 us
  waiting for transfers between devices  316 us (74%)
  matrix products  44 us (10%)
  local copies, waits for them, and re-layouts  29.3 us (7%)
  other arithmetic  18.9 us (4%)
  between operations  14.1 us (3%)
    reduce_scatter x1, waiting for transfers between devices, per_device(): grads = lax.psum_scatter(grads, 'tp', scatter_dimension=0, tiled=True)  75.1 us
    reduce_scatter x1, waiting for transfers between devices, per_device(): lax.psum_scatter(grads.astype(jnp.float32), 'ctx', scatter_dimension=0, t...  72.1 us
    reduce_scatter x1, waiting for transfers between devices, per_device(): lax.psum_scatter(jnp.dot(attended, global_out, preferred_element_type=jnp...  63.1 us
    all_gather x1, waiting for transfers between devices, per_device(): lax.all_gather(jnp.concatenate([keys_mine, values_mine], axis=1), 'ctx',...  59.2 us
    all_gather x1, waiting for transfers between devices, per_device(): lax.all_gather(normed, 'tp', axis=0, tiled=True)  46 us
    dot_general x1, matrix products, per_device(): jnp.einsum('nd,cdh->nch', lax.all_gather(normed, 'tp', axis=0, tiled=True...  11.2 us
    dot_general x1, local copies, waits for them, and re-layouts, local_pass(): jnp.dot(normed, local_qkv[layer], preferred_element_type=jnp.float32)  8.74 us
  transfers between devices with their start and end apart: 6, of which 5 were waited for; matrix products, arithmetic and copies ran while one was open for 4% of the time, Pallas kernels for 0%

profile of v1, /device:TPU:1, one launch (start us, length us, event | category | flops | bytes accessed | tf_op | source)
XLA Modules:
  0.0 425.7 jit_solution(14515467212190886574)
XLA Ops:
  7.2 1.3 reshape.147
  8.5 1.2 multiply_reduce_fusion.6
  10.8 46.0 %all-gather.3.cloned.1.call-done = bf16[384,8192]{1,0:T(8,128)(2,1)} async-done(((bf16[24,8192]{1,0:T(8,128)(2,1)}), bf16[384,8192]{1,0:T(8,128)(2,1)}) %all-gather.3.cloned.1.call-update) | async-done | bytes 6291472 | tf_op jit(solution)/shard_map/all_gather | solution.py:68
  56.9 11.2 %fusion.2 = f32[384,3,256]{0,2,1:T(8,128)S(1)} fusion(bf16[3,8192,256]{2,1,0:T(8,128)(2,1)} %param.9, bf16[384,8192]{1,0:T(8,128)(2,1)} %all-gather.3.cloned.1.call-done), kind=kOutput, calls=%fused_computation.5 | convolution fusion | flops 4831838208 | bytes 20054016 | tf_op jit(solution)/shard_map/nd,cdh->nch/dot_general | solution.py:66
  69.6 1.9 iota_compare_fusion
  72.5 59.2 %all-gather.5.cloned.1.call-done = bf16[3072,4,128]{2,0,1:T(8,128)(2,1)} async-done(((bf16[384,4,128]{2,0,1:T(8,128)(2,1)}), bf16[3072,4,128]{2,0,1:T(8,128)(2,1)}) %all-gather.5.cloned.1.call-update) | async-done | bytes 3145744 | tf_op jit(solution)/shard_map/all_gather | solution.py:83
  131.8 4.3 %fusion = (f32[384,2]{0,1:T(2,128)S(1)}, f32[2,3072,384]{2,1,0:T(8,128)S(1)}) fusion(pred[384,3072]{0,1:T(8,128)(4,1)} %iota_compare_fusion, bf16[3072,4,128]{2,0,1:T(8,128)(2,1)} %all-gather.5.cloned.1.call-done, f32[384,2,128]{2,0,1:T(8,128)} %copy.26, f32[384,2]{0,1:T(2,128)S(1)} %add_rsqrt_fusion), kind=kOutput, calls=%fused_computation.3 | convolution fusion | flops 611253504 | bytes 14161920 | tf_op jit(solution)/shard_map/rha,kha->rhk/dot_general | solution.py:88
  136.1 2.5 fusion.27
  138.6 4.5 %convolution_convert_fusion = bf16[384,8192]{1,0:T(8,128)(2,1)} fusion(bf16[384,256]{0,1:T(8,128)(2,1)S(1)} %bitcast.156, bf16[256,8192]{1,0:T(8,128)(2,1)S(1)} %copy-done.1), kind=kOutput, calls=%fused_computation | convolution fusion | flops 1613758464 | bytes 10682368 | tf_op jit(solution)/shard_map/dot_general | solution.py:103
  144.1 1.7 fusion.38
  145.8 63.1 %reduce-scatter.4.cloned.1.call-done = bf16[24,8192]{1,0:T(8,128)(2,1)} async-done(((bf16[384,8192]{1,0:T(8,128)(2,1)}), bf16[24,8192]{1,0:T(8,128)(2,1)}) %reduce-scatter.4.cloned.1.call-update) | async-done | bytes 393232 | tf_op jit(solution)/shard_map/reduce_scatter | solution.py:102
  209.0 0.9 slice.52
  209.9 3.3 collective-permute-start
  213.2 8.7 %copy.46 = bf16[3072,1024]{1,0:T(8,128)(2,1)} copy(bf16[3072,1024]{0,1:T(8,128)(2,1)} %bitcast.148) | data formatting | bytes 12582912 | tf_op jit(solution)/shard_map/dot_general | solution.py:43
  222.0 1.0 maximum_convert_fusion
  223.0 1.3 reshape.148
  224.5 1.1 multiply_convert_fusion
  225.6 4.3 %fusion.40 = f32[24,8,3,8,128]{4,1,3,2,0:T(8,128)S(1)} fusion(bf16[3,8,128,1024,1]{3,2,1,0,4:T(8,128)(2,1)} %bitcast.149, bf16[192,1024]{1,0:T(8,128)(2,1)S(1)} %multiply_convert_fusion), kind=kOutput, calls=%fused_computation.63 | convolution fusion | flops 1207959552 | bytes 9043968 | tf_op jit(solution)/shard_map/dot_general | solution.py:43
  231.6 1.4 multiply_reduce_fusion.2
  235.0 1.0 fusion.30
  236.3 1.3 copy.34
  237.5 3.0 convert_element_type.96
  240.5 5.9 %convolution_convert_fusion.1 = bf16[1024,3072]{1,0:T(8,128)(2,1)} fusion(bf16[192,1024]{1,0:T(8,128)(2,1)S(1)} %multiply_convert_fusion, bf16[192,3072]{1,0:T(8,128)(2,1)} %convert_element_type.96), kind=kOutput, calls=%fused_computation.7 | convolution fusion | flops 1211105280 | bytes 7864320 | tf_op jit(solution)/shard_map/dot_general | solution.py:56
  246.5 2.6 convolution_convert_fusion.2
  249.1 7.6 %pad_maximum_fusion = bf16[1024,4096]{1,0:T(8,128)(2,1)} fusion(bf16[1024,1024]{1,0:T(8,128)(2,1)} %convolution_convert_fusion.2, bf16[1024,3072]{1,0:T(8,128)(2,1)} %convolution_convert_fusion.1), kind=kLoop, calls=%fused_computation.2 | loop fusion | flops 16777216 | bytes 16777216 | tf_op jit(solution)/shard_map/concatenate | solution.py:114
  256.6 7.7 %copy.36 = bf16[16,8,8,4096]{3,2,1,0:T(8,128)(2,1)} copy(bf16[16,8,8,4096]{3,2,0,1:T(8,128)(2,1)} %bitcast.147) | data formatting | bytes 16777216 | tf_op jit(solution)/shard_map/convert_element_type | solution.py:117
  264.4 75.1 %reduce-scatter.6.cloned.1.call-done = bf16[64,4096]{1,0:T(8,128)(2,1)} async-done(((bf16[1024,4096]{1,0:T(8,128)(2,1)}), bf16[64,4096]{1,0:T(8,128)(2,1)}) %reduce-scatter.6.cloned.1.call-update) | async-done | bytes 524304 | tf_op jit(solution)/shard_map/reduce_scatter | solution.py:118
  339.5 2.1 convert_element_type.100
  341.6 2.5 fusion.18
  344.2 72.1 %reduce-scatter.8.cloned.1.call-done = f32[8,4096]{1,0:T(8,128)} async-done(((f32[64,4096]{1,0:T(8,128)}), f32[8,4096]{1,0:T(8,128)}) %reduce-scatter.8.cloned.1.call-update) | async-done | bytes 131088 | tf_op jit(solution)/shard_map/reduce_scatter | solution.py:119
  416.2 1.5 slice.57
  417.8 1.4 slice.58
  (64 shorter events, 8.9 us)
Async XLA Ops:
  7.2 136.2 %copy-start = (bf16[1,1024,1024]{2,1,0:T(8,128)(2,1)S(1)}, bf16[1,1024,1024]{2,1,0:T(8,128)(2,1)}, u32[]{:S(2)}) copy-start(bf16[1,1024,1024]{2,1,0:T(8,128)(2,1)} %param.12) | copy-start | bytes 6291460
  7.2 49.7 %all-gather.3.cloned.1.call-start = ((), (), s32[]{:S(2)}) async-start(), calls=%async_computation.3 | async-start | bytes 6684672 | tf_op jit(solution)/shard_map/all_gather | solution.py:68
  10.8 121.0 %all-gather.5.cloned.1.call-start = ((), (), s32[]{:S(2)}) async-start(), calls=%async_computation.4 | async-start | bytes 3538944 | tf_op jit(solution)/shard_map/all_gather | solution.py:83
  69.6 139.4 %reduce-scatter.4.cloned.1.call-start = ((), (), s32[]{:S(2)}) async-start(), calls=%async_computation.5 | async-start | bytes 6684672 | tf_op jit(solution)/shard_map/reduce_scatter | solution.py:102
  72.5 63.5 %copy-start.5 = (pred[384,3072]{0,1:T(8,128)(4,1)S(1)}, pred[384,3072]{0,1:T(8,128)(4,1)}, u32[]{:S(2)}) copy-start(pred[384,3072]{0,1:T(8,128)(4,1)} %iota_compare_fusion) | copy-start | bytes 3538948
  131.8 4.3 %copy-start.10 = (bf16[3072,4,128]{2,0,1:T(8,128)(2,1)S(1)}, bf16[3072,4,128]{2,0,1:T(8,128)(2,1)}, u32[]{:S(2)}) copy-start(bf16[3072,4,128]{2,0,1:T(8,128)(2,1)} %all-gather.5.cloned.1.call-done) | copy-start | bytes 9437188
  136.1 2.5 copy-start.1
  143.1 1.0 copy-start.8
  143.1 196.4 %reduce-scatter.6.cloned.1.call-start = ((), (), s32[]{:S(2)}) async-start(), calls=%async_computation.6 | async-start | bytes 8912896 | tf_op jit(solution)/shard_map/reduce_scatter | solution.py:118
  209.9 12.1 %collective-permute-start = (bf16[1,8192]{1,0:T(2,128)(2,1)S(1)}, bf16[1,8192]{1,0:T(2,128)(2,1)S(1)}, u32[]{:S(2)}, u32[]{:S(2)}) collective-permute-start(bf16[1,8192]{1,0:T(2,128)(2,1)S(1)} %slice.52), channel_id=1, source_target_pairs={{0,1},{1,2},{2,3},{3,4},{4,5},{5,6},{6,7},{7,8},{8,9},{9,10},{10,1... | collective-permute-start | bytes 49160 | tf_op jit(solution)/shard_map/ppermute | solution.py:17
  213.2 8.8 %copy-start.7 = (bf16[24,8192]{1,0:T(8,128)(2,1)S(1)}, bf16[24,8192]{1,0:T(8,128)(2,1)}, u32[]{:S(2)}) copy-start(bf16[24,8192]{1,0:T(8,128)(2,1)} %reduce-scatter.4.cloned.1.call-done) | copy-start | bytes 1179652
  213.2 11.0 %copy-start.3 = (bf16[192,1024]{1,0:T(8,128)(2,1)S(1)}, bf16[192,1024]{1,0:T(8,128)(2,1)}, u32[]{:S(2)}) copy-start(bf16[192,1024]{1,0:T(8,128)(2,1)} %param.8) | copy-start | bytes 1179652
  229.9 1.2 copy-start.2
  240.5 5.9 %copy-start.6 = (f32[24,8,8,128]{3,1,2,0:T(8,128)S(1)}, f32[24,8,8,128]{3,1,2,0:T(8,128)}, u32[]{:S(2)}) copy-start(f32[24,8,8,128]{3,1,2,0:T(8,128)} %get-tuple-element.16) | copy-start | bytes 2359300
  240.5 5.9 %copy-start.9 = (bf16[192,1024]{1,0:T(8,128)(2,1)S(1)}, bf16[192,1024]{1,0:T(8,128)(2,1)}, u32[]{:S(2)}) copy-start(bf16[192,1024]{1,0:T(8,128)(2,1)} %param.13) | copy-start | bytes 1179652
  264.3 77.3 %copy-start.4 = (bf16[192,1024]{1,0:T(8,128)(2,1)S(1)}, bf16[192,1024]{1,0:T(8,128)(2,1)}, u32[]{:S(2)}) copy-start(bf16[192,1024]{1,0:T(8,128)(2,1)} %param.8) | copy-start | bytes 1179652
  264.3 151.9 %reduce-scatter.8.cloned.1.call-start = ((), (), s32[]{:S(2)}) async-start(), calls=%async_computation.7 | async-start | bytes 1179648 | tf_op jit(solution)/shard_map/reduce_scatter | solution.py:119
Sparse Core Ops, SparseCore 0:
  10.9 45.9 all-gather.2
  69.7 62.0 all-gather.4
  143.3 65.6 reduce-scatter.3
  264.5 75.0 reduce-scatter.5
  342.9 73.2 reduce-scatter.7

commit v2 on v0

--- a/solution.py
+++ b/solution.py
@@ -3,6 +3,8 @@
 import jax
 import jax.numpy as jnp
 from jax import lax
+from jax.experimental import pallas as pl
+from jax.experimental.pallas import tpu as pltpu
 from jax.sharding import PartitionSpec as P
 
 PATCH = 8
@@ -15,6 +17,258 @@
     count = lax.axis_size(axis)
     initial, last = (max(0, -steps), min(count, count - steps))
     return lax.ppermute(value, axis, [(source, source + steps) for source in range(initial, last)])
+
+
+MESH = pl.DeviceIdType.MESH
+
+
+def coords():
+    ctx, tp = lax.axis_index("ctx"), lax.axis_index("tp")
+    x, core = lax.rem(lax.div(tp, 2), 4), lax.rem(tp, 2)
+    y = lax.rem(ctx, 2) * 2 + lax.div(tp, 8)
+    return x, y, lax.div(ctx, 2), core
+
+
+def device_at(x, y, z, core):
+    return {"ctx": z * 2 + lax.div(y, 2), "tp": lax.rem(y, 2) * 8 + x * 2 + core}
+
+
+def greet(peers):
+    barrier = pltpu.get_barrier_semaphore()
+    for peer in peers:
+        pl.semaphore_signal(barrier, inc=1, device_id=peer, device_id_type=MESH)
+    pl.semaphore_wait(barrier, len(peers))
+
+
+def remote(source, target, send_sem, recv_sem, peer):
+    return pltpu.make_async_remote_copy(
+        src_ref=source,
+        dst_ref=target,
+        send_sem=send_sem,
+        recv_sem=recv_sem,
+        device_id=peer,
+        device_id_type=MESH,
+    )
+
+
+PART_COLS = (640, 640, 768)
+PART_ORDERS = ((0, 1, 2), (1, 2, 0), (2, 0, 1))
+
+
+def grads_kernel(
+    xn_ref, gq_ref, ab_ref, gb_ref, out_q, out_o,
+    xn2, gq2, ab2, gb2,
+    part0, part1, part2, relay0, relay1, relay2, near0, near1, near2,
+    sum0, sum1, sum2, got0, got1, got2, low0, low1, low2, last0, last1, last2,
+    fin, other, pair_send, pair_recv, send1, recv1, send2, recv2, send3, recv3,
+    fin_send, fin_recv,
+):
+    place = coords()
+    core = place[3]
+
+    def peer_along(axis, step):
+        at = list(place)
+        at[axis] = lax.rem(at[axis] + step, 4)
+        return device_at(*at)
+
+    partner = device_at(place[0], place[1], place[2], 1 - core)
+    greet([partner] + [peer_along(axis, step) for axis in range(3) for step in (1, 2, 3)])
+
+    rows = xn_ref.shape[0]
+    qh, oh = gq2.shape[1], gb2.shape[1]
+    mine_q, mine_o = pl.multiple_of(core * qh, qh), pl.multiple_of(core * oh, oh)
+    its_q, its_o = pl.multiple_of((1 - core) * qh, qh), pl.multiple_of((1 - core) * oh, oh)
+    bottom = pl.ds(rows, rows)
+    swaps = [
+        remote(xn_ref, xn2.at[bottom], pair_send.at[0], pair_recv.at[0], partner),
+        remote(gq_ref.at[:, pl.ds(its_q, qh)], gq2.at[bottom], pair_send.at[1], pair_recv.at[1], partner),
+        remote(ab_ref, ab2.at[bottom], pair_send.at[2], pair_recv.at[2], partner),
+        remote(gb_ref.at[:, pl.ds(its_o, oh)], gb2.at[bottom], pair_send.at[3], pair_recv.at[3], partner),
+    ]
+    for swap in swaps:
+        swap.start()
+    top = pl.ds(0, rows)
+    xn2[top] = xn_ref[...]
+    gq2[top] = gq_ref[:, pl.ds(mine_q, qh)]
+    ab2[top] = ab_ref[...]
+    gb2[top] = gb_ref[:, pl.ds(mine_o, oh)]
+
+    parts = (part0, part1, part2)
+    relays, nears = (relay0, relay1, relay2), (near0, near1, near2)
+    sums, gots = (sum0, sum1, sum2), (got0, got1, got2)
+    lows, lasts = (low0, low1, low2), (last0, last1, last2)
+
+    def fill(part, order, left, right, columns, into):
+        width = columns[1] - columns[0]
+        for z in range(4):
+            block = lax.dot_general(
+                left[:, z * 256 : (z + 1) * 256],
+                right[:, columns[0] : columns[1]],
+                (((0,), (0,)), ((), ())),
+                preferred_element_type=jnp.float32,
+            ).astype(jnp.bfloat16)
+            for y in range(4):
+                for x in range(4):
+                    at = (x, y, z)
+                    row = (y * 4 + x) * 16
+                    part[at[order[0]], at[order[1]], at[order[2]], :, into : into + width] = block[
+                        row : row + 16
+                    ]
+
+    first = []
+
+    def stage1(k):
+        order = PART_ORDERS[k]
+        axis = order[0]
+        me = place[axis]
+        right, left, far = lax.rem(me + 1, 4), lax.rem(me + 3, 4), lax.rem(me + 2, 4)
+        to_right, to_left = peer_along(axis, 1), peer_along(axis, 3)
+        part, relay, near = parts[k], relays[k], nears[k]
+        lo, hi = pl.ds(0, 2), pl.ds(2, 2)
+
+        def copy(n, source, target, peer):
+            return remote(source, target, send1.at[k, n], recv1.at[k, n], peer)
+
+        copies = [
+            copy(0, part.at[far, lo], relay.at[0], to_right),
+            copy(1, part.at[far, hi], relay.at[1], to_left),
+            copy(2, part.at[right, hi], near.at[0, hi], to_right),
+            copy(3, part.at[left, lo], near.at[1, lo], to_left),
+            copy(4, part.at[right, lo], near.at[0, lo], to_right),
+            copy(5, part.at[left, hi], near.at[1, hi], to_left),
+        ]
+        for n in range(4):
+            copies[n].start()
+        return copies, (right, left)
+
+    def add_relay(k, copies, sides):
+        part, relay = parts[k], relays[k]
+        for n in range(2):
+            copies[n].wait_recv()
+            for j in range(2):
+                at = 2 * n + j
+                part[sides[n], at] = (
+                    part[sides[n], at].astype(jnp.float32) + relay[n, j].astype(jnp.float32)
+                ).astype(jnp.bfloat16)
+            copies[4 + n].start()
+
+    def stage2(k, copies):
+        order = PART_ORDERS[k]
+        for n in range(2, 6):
+            copies[n].wait_recv()
+        me = place[order[0]]
+        for j in range(4):
+            sums[k][j] = (
+                parts[k][me, j].astype(jnp.float32)
+                + nears[k][0, j].astype(jnp.float32)
+                + nears[k][1, j].astype(jnp.float32)
+            ).astype(jnp.bfloat16)
+        axis = order[1]
+        at = place[axis]
+        sends = []
+        for d in range(1, 4):
+            send = remote(
+                sums[k].at[lax.rem(at + d, 4)], gots[k].at[d - 1],
+                send2.at[k, d - 1], recv2.at[k, d - 1], peer_along(axis, d),
+            )
+            send.start()
+            sends.append(send)
+        return sends
+
+    def stage3(k, copies):
+        order = PART_ORDERS[k]
+        for copy in copies:
+            copy.wait_recv()
+        me = place[order[1]]
+        total = sums[k][me].astype(jnp.float32)
+        for d in range(3):
+            total = total + gots[k][d].astype(jnp.float32)
+        lows[k][...] = total.astype(jnp.bfloat16)
+        axis = order[2]
+        at = place[axis]
+        sends = []
+        for d in range(1, 4):
+            send = remote(
+                lows[k].at[lax.rem(at + d, 4)], lasts[k].at[d - 1],
+                send3.at[k, d - 1], recv3.at[k, d - 1], peer_along(axis, d),
+            )
+            send.start()
+            sends.append(send)
+        return sends
+
+    def finish(k, copies):
+        for copy in copies:
+            copy.wait_recv()
+        me = place[PART_ORDERS[k][2]]
+        total = lows[k][me].astype(jnp.float32)
+        for d in range(3):
+            total = total + lasts[k][d].astype(jnp.float32)
+        start = sum(PART_COLS[:k])
+        fin[:, start : start + PART_COLS[k]] = total
+
+    swaps[0].wait_recv()
+    swaps[1].wait_recv()
+    split = PART_COLS[0] + PART_COLS[1]
+    fill(part0, PART_ORDERS[0], xn2, gq2, (0, PART_COLS[0]), 0)
+    first.append(stage1(0))
+    fill(part1, PART_ORDERS[1], xn2, gq2, (PART_COLS[0], split), 0)
+    first.append(stage1(1))
+    swaps[2].wait_recv()
+    swaps[3].wait_recv()
+    fill(part2, PART_ORDERS[2], xn2, gq2, (split, qh), 0)
+    fill(part2, PART_ORDERS[2], ab2, gb2, (0, oh), qh - split)
+    first.append(stage1(2))
+    for k in range(3):
+        add_relay(k, *first[k])
+    second = [stage2(k, first[k][0]) for k in range(3)]
+    third = [stage3(k, second[k]) for k in range(3)]
+    for k in range(3):
+        finish(k, third[k])
+
+    keep, give = pl.multiple_of(core * 8, 8), pl.multiple_of((1 - core) * 8, 8)
+    end = remote(fin.at[pl.ds(give, 8)], other, fin_send, fin_recv, partner)
+    end.start()
+    out_q[:, pl.ds(mine_q, qh)] = fin[pl.ds(keep, 8), 0:qh]
+    out_o[:, pl.ds(mine_o, oh)] = fin[pl.ds(keep, 8), qh : qh + oh]
+    end.wait_recv()
+    out_q[:, pl.ds(its_q, qh)] = other[:, 0:qh]
+    out_o[:, pl.ds(its_o, oh)] = other[:, qh : qh + oh]
+    for copy in swaps + [c for f in first for c in f[0]] + [c for s in second + third for c in s] + [end]:
+        copy.wait_send()
+
+
+def reduce_grads(xn, gq, ab, gb):
+    rows, width = xn.shape
+    qw, ow = gq.shape[1], gb.shape[1]
+    bf, f32 = jnp.bfloat16, jnp.float32
+    vmem = pl.BlockSpec(memory_space=pltpu.VMEM)
+
+    def each(*lead):
+        return [pltpu.VMEM((*lead, 16, c), bf) for c in PART_COLS]
+
+    return pl.pallas_call(
+        grads_kernel,
+        name="reduce_grads",
+        out_shape=(jax.ShapeDtypeStruct((8, qw), f32), jax.ShapeDtypeStruct((8, ow), f32)),
+        in_specs=[vmem] * 4,
+        out_specs=(vmem, vmem),
+        scratch_shapes=[
+            pltpu.VMEM((2 * rows, width), bf),
+            pltpu.VMEM((2 * rows, qw // 2), bf),
+            pltpu.VMEM((2 * rows, width), bf),
+            pltpu.VMEM((2 * rows, ow // 2), bf),
+            *each(4, 4, 4), *each(2, 2, 4), *each(2, 4, 4),
+            *each(4, 4), *each(3, 4), *each(4), *each(3),
+            pltpu.VMEM((16, (qw + ow) // 2), f32),
+            pltpu.VMEM((8, (qw + ow) // 2), f32),
+            pltpu.SemaphoreType.DMA((4,)), pltpu.SemaphoreType.DMA((4,)),
+            pltpu.SemaphoreType.DMA((3, 6)), pltpu.SemaphoreType.DMA((3, 6)),
+            pltpu.SemaphoreType.DMA((3, 3)), pltpu.SemaphoreType.DMA((3, 3)),
+            pltpu.SemaphoreType.DMA((3, 3)), pltpu.SemaphoreType.DMA((3, 3)),
+            pltpu.SemaphoreType.DMA, pltpu.SemaphoreType.DMA,
+        ],
+        compiler_params=pltpu.CompilerParams(collective_id=5, has_side_effects=True, vmem_limit_bytes=48 << 20),
+    )(xn, gq, ab, gb)
 
 
 def rms_norm(values):
@@ -50,11 +304,9 @@
     layer = 0
     before, normed, core_back, attended = saved[layer]
     grad_round = grad_state.astype(jnp.bfloat16)
-    grads_out = [jnp.dot(attended.T, grad_round, preferred_element_type=jnp.float32)]
     grad_core = jnp.dot(grad_round, local_out[layer].T, preferred_element_type=jnp.float32)
     grad_rows = core_back(grad_core)[0].astype(jnp.bfloat16)
-    grads_qkv = [jnp.dot(normed.T, grad_rows, preferred_element_type=jnp.float32)]
-    return (hidden, jnp.stack(grads_qkv[::-1]), jnp.stack(grads_out[::-1]))
+    return hidden, normed, grad_rows, attended, grad_round
 
 
 def per_device(byte_embeds, local_embeds, global_qkv, global_out, local_qkv, local_out, cotangent):
@@ -80,8 +332,10 @@
     )
     values_mine = projected[:, 2].reshape(shard_rows, head_count, HEAD_DIM).astype(jnp.bfloat16)
     query_pos = lax.axis_index("ctx") * shard_rows + jnp.arange(shard_rows, dtype=jnp.int32)
-    key_piece = lax.all_gather(keys_mine, "ctx", axis=0, tiled=True)
-    value_piece = lax.all_gather(values_mine, "ctx", axis=0, tiled=True)
+    pieces = lax.all_gather(
+        jnp.concatenate([keys_mine, values_mine], axis=1), "ctx", axis=0, tiled=True
+    )
+    key_piece, value_piece = pieces[:, :head_count], pieces[:, head_count:]
     key_count = key_piece.shape[0]
     scores = jnp.einsum(
         "rha,kha->rhk", queries, key_piece, preferred_element_type=jnp.float32
@@ -107,12 +361,9 @@
     patch_out = jnp.concatenate([earlier_row, patch_out[:-1]], axis=0)
     context = patch_out.reshape(byte_count, byte_embeds.shape[1])
     state = local_embeds.astype(jnp.float32) + context.astype(jnp.float32)
-    hidden, grad_qkv, grad_out = local_pass(state, local_qkv, local_out, cotangent)
-    grad_qkv, grad_out = (
-        lax.psum_scatter(grad_qkv, ("ctx", "tp"), scatter_dimension=1, tiled=True),
-        lax.psum_scatter(grad_out, ("ctx", "tp"), scatter_dimension=1, tiled=True),
-    )
-    return (hidden, grad_qkv, grad_out)
+    hidden, *factors = local_pass(state, local_qkv, local_out, cotangent)
+    grad_qkv, grad_out = reduce_grads(*factors)
+    return (hidden, grad_qkv[None], grad_out[None])
 
 
 def solution(mesh):

time: 1160 us -> 290 us (0.25)
  waiting for transfers between devices: 1050 us -> 168 us
  Pallas kernels: 0 us -> 40.5 us
  matrix products: 55.6 us -> 33.8 us
    reduce_scatter x2 -> x0, waiting for transfers between devices: 851 us -> none  [the longest x1 625 us: per_device(): lax.psum_scatter(grad_out, ('ctx', 'tp'), scatter_dimension=1, tiled=True)]
    pallas_call x0 -> x1, Pallas kernels: none -> 40.5 us  [reduce_grads(): pl.pallas_call(grads_kernel, name='reduce_grads', out_shape=(jax.ShapeDty...]
    all_gather x2 -> x1, waiting for transfers between devices: 87.2 us -> 59 us  [per_device(): lax.all_gather(jnp.concatenate([keys_mine, values_mine], axis=1), 'ctx',...]
  transfers between devices with their start and end apart: 7 -> 4, of which waited for: 6 -> 3; matrix products, arithmetic and copies ran while one was open for 4% -> 5% of each run, Pallas kernels for 0% -> 0%
where the time goes in v2:
time: 290 us; the launch traced here: 289 us
  waiting for transfers between devices  168 us (58%)
  Pallas kernels  40.5 us (14%)
  matrix products  33.8 us (12%)
  local copies, waits for them, and re-layouts  18.6 us (6%)
  between operations  14.1 us (5%)
  other arithmetic  10.3 us (4%)
  starting transfers between devices  3.8 us (1%)
    reduce_scatter x1, waiting for transfers between devices, per_device(): lax.psum_scatter(jnp.dot(attended, global_out, preferred_element_type=jnp...  63.1 us
    all_gather x1, waiting for transfers between devices, per_device(): lax.all_gather(jnp.concatenate([keys_mine, values_mine], axis=1), 'ctx',...  59 us
    all_gather x1, waiting for transfers between devices, per_device(): lax.all_gather(normed, 'tp', axis=0, tiled=True)  46 us
    pallas_call x1, Pallas kernels, reduce_grads(): pl.pallas_call(grads_kernel, name='reduce_grads', out_shape=(jax.ShapeDty...  40.5 us
    dot_general x1, matrix products, per_device(): jnp.einsum('nd,cdh->nch', lax.all_gather(normed, 'tp', axis=0, tiled=True...  11.2 us
    dot_general x1, local copies, waits for them, and re-layouts, local_pass(): jnp.dot(normed, local_qkv[layer], preferred_element_type=jnp.float32)  8.72 us
  transfers between devices with their start and end apart: 4, of which 3 were waited for; matrix products, arithmetic and copies ran while one was open for 5% of the time, Pallas kernels for 0%

profile of v2, /device:TPU:1, one launch (start us, length us, event | category | flops | bytes accessed | tf_op | source)
XLA Modules:
  0.0 289.3 jit_solution(3359376056625075472)
XLA Ops:
  7.2 1.3 reshape.139
  8.5 1.2 multiply_reduce_fusion.6
  9.9 0.9 multiply_convert_fusion.1
  10.8 46.0 %all-gather.3.cloned.1.call-done = bf16[384,8192]{1,0:T(8,128)(2,1)} async-done(((bf16[24,8192]{1,0:T(8,128)(2,1)}), bf16[384,8192]{1,0:T(8,128)(2,1)}) %all-gather.3.cloned.1.call-update) | async-done | bytes 6291472 | tf_op jit(solution)/shard_map/all_gather | solution.py:320
  56.9 11.2 %fusion.2 = f32[384,3,256]{0,2,1:T(8,128)S(1)} fusion(bf16[3,8192,256]{2,1,0:T(8,128)(2,1)} %param.9, bf16[384,8192]{1,0:T(8,128)(2,1)} %all-gather.3.cloned.1.call-done), kind=kOutput, calls=%fused_computation.4 | convolution fusion | flops 4831838208 | bytes 20054016 | tf_op jit(solution)/shard_map/nd,cdh->nch/dot_general | solution.py:318
  68.2 0.9 copy-done.5
  69.3 1.0 slice.79
  70.7 0.8 pad_maximum_fusion
  71.8 1.9 iota_compare_fusion
  73.7 0.9 copy.25
  74.7 59.0 %all-gather.5.cloned.1.call-done = bf16[3072,4,128]{2,0,1:T(8,128)(2,1)} async-done(((bf16[384,4,128]{2,0,1:T(8,128)(2,1)}), bf16[3072,4,128]{2,0,1:T(8,128)(2,1)}) %all-gather.5.cloned.1.call-update) | async-done | bytes 3145744 | tf_op jit(solution)/shard_map/all_gather | solution.py:335
  133.7 4.3 %fusion = (f32[384,2]{0,1:T(2,128)S(1)}, f32[2,3072,384]{2,1,0:T(8,128)S(1)}) fusion(pred[384,3072]{0,1:T(8,128)(4,1)} %iota_compare_fusion, bf16[3072,4,128]{2,0,1:T(8,128)(2,1)} %all-gather.5.cloned.1.call-done, f32[384,2,128]{2,0,1:T(8,128)} %copy.25, f32[384,2]{0,1:T(2,128)S(1)} %add_rsqrt_fusion), kind=kOutput, calls=%fused_computation.2 | convolution fusion | flops 611253504 | bytes 14161920 | tf_op jit(solution)/shard_map/rha,kha->rhk/dot_general | solution.py:340
  138.0 2.5 fusion.27
  140.6 4.5 %convolution_convert_fusion = bf16[384,8192]{1,0:T(8,128)(2,1)} fusion(bf16[384,256]{0,1:T(8,128)(2,1)S(1)} %bitcast.150, bf16[256,8192]{1,0:T(8,128)(2,1)S(1)} %copy-done.2), kind=kOutput, calls=%fused_computation | convolution fusion | flops 1613758464 | bytes 10682368 | tf_op jit(solution)/shard_map/dot_general | solution.py:355
  145.1 1.0 copy-done.1
  146.1 1.7 fusion.38
  147.8 63.1 %reduce-scatter.2.cloned.1.call-done = bf16[24,8192]{1,0:T(8,128)(2,1)} async-done(((bf16[384,8192]{1,0:T(8,128)(2,1)}), bf16[24,8192]{1,0:T(8,128)(2,1)}) %reduce-scatter.2.cloned.1.call-update) | async-done | bytes 393232 | tf_op jit(solution)/shard_map/reduce_scatter | solution.py:354
  210.9 0.9 slice.44
  211.9 3.5 %collective-permute-start = (bf16[1,8192]{1,0:T(2,128)(2,1)S(1)}, bf16[1,8192]{1,0:T(2,128)(2,1)S(1)}, u32[]{:S(2)}, u32[]{:S(2)}) collective-permute-start(bf16[1,8192]{1,0:T(2,128)(2,1)S(1)} %slice.44), channel_id=1, source_target_pairs={{0,1},{1,2},{2,3},{3,4},{4,5},{5,6},{6,7},{7,8},{8,9},{9,10},{10,1... | collective-permute-start | bytes 49160 | tf_op jit(solution)/shard_map/ppermute | solution.py:19
  215.4 8.7 %copy.42 = bf16[3072,1024]{1,0:T(8,128)(2,1)} copy(bf16[3072,1024]{0,1:T(8,128)(2,1)} %bitcast.142) | data formatting | bytes 12582912 | tf_op jit(solution)/shard_map/dot_general | solution.py:297
  224.2 1.0 maximum_convert_fusion
  225.1 1.3 reshape.140
  226.4 1.2 multiply_reduce_fusion.5
  227.6 1.1 multiply_convert_fusion.xn_ref
  228.7 4.3 %fusion.40 = f32[24,8,3,8,128]{4,1,3,2,0:T(8,128)S(1)} fusion(bf16[3,8,128,1024,1]{3,2,1,0,4:T(8,128)(2,1)} %bitcast.143, bf16[192,1024]{1,0:T(8,128)(2,1)S(1)} %multiply_convert_fusion.xn_ref), kind=kOutput, calls=%fused_computation.60 | convolution fusion | flops 1207959552 | bytes 9043968 | tf_op jit(solution)/shard_map/dot_general | solution.py:297
  234.7 0.9 multiply_reduce_fusion.2
  236.6 0.9 multiply_reduce_fusion.1
  237.6 1.0 fusion.30
  239.0 0.7 copy-done.3
  239.6 1.3 fusion.18
  240.9 40.5 %reduce_grads.1 = (f32[8,3072]{1,0:T(8,128)S(1)}, f32[8,1024]{1,0:T(8,128)S(1)}) custom-call(bf16[192,1024]{1,0:T(8,128)(2,1)S(1)} %multiply_convert_fusion.xn_ref, bf16[192,3072]{1,0:T(8,128)(2,1)S(1)} %bitcast.139, bf16[192,1024]{1,0:T(8,128)(2,1)S(1)} %get-tuple-element.16.ab_ref, bf16[192,1024]{1,0:T(8,128)(2,1)S(1)} %copy-done.1), custom_call_target="tpu_custom_call" | custom-call | tf_op jit(solution)/shard_map/reduce_grads/pallas_call | solution.py:249
  281.5 0.6 copy.46
  (49 shorter events, 4.9 us)
Async XLA Ops:
  7.2 137.9 %copy-start = (bf16[1,1024,1024]{2,1,0:T(8,128)(2,1)S(1)}, bf16[1,1024,1024]{2,1,0:T(8,128)(2,1)}, u32[]{:S(2)}) copy-start(bf16[1,1024,1024]{2,1,0:T(8,128)(2,1)} %param.12) | copy-start | bytes 6291460
  7.2 49.7 %all-gather.3.cloned.1.call-start = ((), (), s32[]{:S(2)}) async-start(), calls=%async_computation.1 | async-start | bytes 6684672 | tf_op jit(solution)/shard_map/all_gather | solution.py:320
  10.8 122.9 %all-gather.5.cloned.1.call-start = ((), (), s32[]{:S(2)}) async-start(), calls=%async_computation.2 | async-start | bytes 3538944 | tf_op jit(solution)/shard_map/all_gather | solution.py:335
  68.1 1.0 copy-start.5
  71.5 139.4 %reduce-scatter.2.cloned.1.call-start = ((), (), s32[]{:S(2)}) async-start(), calls=%async_computation.3 | async-start | bytes 6684672 | tf_op jit(solution)/shard_map/reduce_scatter | solution.py:354
  74.7 63.4 %copy-start.4 = (pred[384,3072]{0,1:T(8,128)(4,1)S(1)}, pred[384,3072]{0,1:T(8,128)(4,1)}, u32[]{:S(2)}) copy-start(pred[384,3072]{0,1:T(8,128)(4,1)} %iota_compare_fusion) | copy-start | bytes 3538948
  133.7 4.3 %copy-start.8 = (bf16[3072,4,128]{2,0,1:T(8,128)(2,1)S(1)}, bf16[3072,4,128]{2,0,1:T(8,128)(2,1)}, u32[]{:S(2)}) copy-start(bf16[3072,4,128]{2,0,1:T(8,128)(2,1)} %all-gather.5.cloned.1.call-done) | copy-start | bytes 9437188
  138.0 2.5 copy-start.2
  145.1 1.0 copy-start.1
  211.9 12.3 %collective-permute-start = (bf16[1,8192]{1,0:T(2,128)(2,1)S(1)}, bf16[1,8192]{1,0:T(2,128)(2,1)S(1)}, u32[]{:S(2)}, u32[]{:S(2)}) collective-permute-start(bf16[1,8192]{1,0:T(2,128)(2,1)S(1)} %slice.44), channel_id=1, source_target_pairs={{0,1},{1,2},{2,3},{3,4},{4,5},{5,6},{6,7},{7,8},{8,9},{9,10},{10,1... | collective-permute-start | bytes 49160 | tf_op jit(solution)/shard_map/ppermute | solution.py:19
  215.4 8.7 %copy-start.7 = (bf16[24,8192]{1,0:T(8,128)(2,1)S(1)}, bf16[24,8192]{1,0:T(8,128)(2,1)}, u32[]{:S(2)}) copy-start(bf16[24,8192]{1,0:T(8,128)(2,1)} %reduce-scatter.2.cloned.1.call-done) | copy-start | bytes 1179652
  233.0 1.2 copy-start.6
  238.6 1.0 copy-start.3
Sparse Core Ops, SparseCore 0:
  10.9 45.9 all-gather.2
  71.6 62.0 all-gather.4
  145.2 65.6 reduce-scatter.1

commit v3 on v2

--- a/solution.py
+++ b/solution.py
@@ -271,6 +271,181 @@
     )(xn, gq, ab, gb)
 
 
+CHUNK = 512
+LANES = 4096
+
+
+def out_kernel(
+    att_ref, w_ref, out_ref, att2, w2, pbuf, relay, near, psum, pgot, qbuf, qgot, qsum, qlast, fin, other,
+    w_sem, pair_send, pair_recv, p_send, p_recv, q_send, q_recv, att_send, att_recv, fin_send, fin_recv,
+):
+    x, y, z, core = coords()
+    pair = lax.rem(y, 2)
+    partner = device_at(x, y, z, 1 - core)
+    across = device_at(x, y + 1 - 2 * pair, z, core)
+
+    def beside(step):
+        return device_at(lax.rem(x + step, 4), y, z, core)
+
+    greet([partner, across, beside(1), beside(2), beside(3)])
+    depth = att_ref.shape[1]
+    copies = []
+
+    def begin(copy):
+        copy.start()
+        copies.append(copy)
+        return copy
+
+    swap = begin(remote(att_ref, att2.at[:, depth : 2 * depth], att_send, att_recv, partner))
+    order = [c for n in range(4) for c in (4 + n, n)]
+    theirs, mine = {}, {}
+    for c in order:
+        into = pl.ds(c * CHUNK, CHUNK)
+        give = pl.ds(pl.multiple_of((1 - core) * LANES + c * CHUNK, CHUNK), CHUNK)
+        keep = pl.ds(pl.multiple_of(core * LANES + c * CHUNK, CHUNK), CHUNK)
+        theirs[c] = begin(
+            remote(w_ref.at[:, give], w2.at[pl.ds(depth, depth), into], pair_send.at[c], pair_recv.at[c], partner)
+        )
+        mine[c] = pltpu.make_async_copy(w_ref.at[:, keep], w2.at[pl.ds(0, depth), into], w_sem.at[c])
+        mine[c].start()
+    att2[:, 0:depth] = att_ref[...]
+    swap.wait_recv()
+
+    right, left, far = lax.rem(x + 1, 4), lax.rem(x + 3, 4), lax.rem(x + 2, 4)
+    pcopies, qcopies = {}, {}
+    for c in order:
+        mine[c].wait()
+        theirs[c].wait_recv()
+        block = jnp.dot(
+            att2[...], w2[:, c * CHUNK : (c + 1) * CHUNK], preferred_element_type=jnp.float32
+        ).astype(jnp.bfloat16)
+        for row in range(8):
+            piece = block[row * 48 : row * 48 + 48]
+            if c < 4:
+                pbuf[c, row % 4, row // 4] = piece
+            else:
+                qbuf[c - 4, row // 4, row % 4] = piece
+        if c < 4:
+
+            def copy(k, source, target, peer):
+                return remote(source, target, p_send.at[c, k], p_recv.at[c, k], peer)
+
+            pcopies[c] = [
+                copy(0, pbuf.at[c, far, 0], relay.at[c, 0], beside(1)),
+                copy(1, pbuf.at[c, far, 1], relay.at[c, 1], beside(3)),
+                copy(2, pbuf.at[c, right, 1], near.at[c, 0, 1], beside(1)),
+                copy(3, pbuf.at[c, left, 0], near.at[c, 1, 0], beside(3)),
+                copy(4, pbuf.at[c, right, 0], near.at[c, 0, 0], beside(1)),
+                copy(5, pbuf.at[c, left, 1], near.at[c, 1, 1], beside(3)),
+                copy(6, psum.at[c, 1 - pair], pgot.at[c], across),
+            ]
+            for k in range(4):
+                begin(pcopies[c][k])
+        else:
+            n = c - 4
+            qcopies[n] = [remote(qbuf.at[n, 1 - pair], qgot.at[n], q_send.at[n, 0], q_recv.at[n, 0], across)] + [
+                remote(qsum.at[n, lax.rem(x + d, 4)], qlast.at[n, d - 1], q_send.at[n, d], q_recv.at[n, d], beside(d))
+                for d in (1, 2, 3)
+            ]
+            begin(qcopies[n][0])
+
+    def wide(value):
+        return value.astype(jnp.float32)
+
+    def p_relay(n):
+        for k, side in ((0, right), (1, left)):
+            pcopies[n][k].wait_recv()
+            pbuf[n, side, k] = (wide(pbuf[n, side, k]) + wide(relay[n, k])).astype(jnp.bfloat16)
+            begin(pcopies[n][4 + k])
+
+    def p_across(n):
+        for k in range(2, 6):
+            pcopies[n][k].wait_recv()
+        for k in range(2):
+            psum[n, k] = (wide(pbuf[n, x, k]) + wide(near[n, 0, k]) + wide(near[n, 1, k])).astype(jnp.bfloat16)
+        begin(pcopies[n][6])
+
+    def p_end(n):
+        pcopies[n][6].wait_recv()
+        fin[:, n * CHUNK : (n + 1) * CHUNK] = wide(psum[n, pair]) + wide(pgot[n])
+
+    def q_beside(n):
+        qcopies[n][0].wait_recv()
+        for k in range(4):
+            qsum[n, k] = (wide(qbuf[n, pair, k]) + wide(qgot[n, k])).astype(jnp.bfloat16)
+        for k in (2, 1, 3):
+            begin(qcopies[n][k])
+
+    def q_end(n):
+        for k in (1, 2, 3):
+            qcopies[n][k].wait_recv()
+        total = wide(qsum[n, x])
+        for k in range(3):
+            total = total + wide(qlast[n, k])
+        fin[:, (4 + n) * CHUNK : (5 + n) * CHUNK] = total
+
+    p_relay(0)
+    p_relay(1)
+    q_beside(0)
+    p_relay(2)
+    p_relay(3)
+    q_beside(1)
+    p_across(0)
+    p_across(1)
+    q_beside(2)
+    p_across(2)
+    p_across(3)
+    q_end(0)
+    q_end(1)
+    q_beside(3)
+    for n in range(4):
+        p_end(n)
+    q_end(2)
+    q_end(3)
+
+    keep, give = pl.multiple_of(core * 24, 8), pl.multiple_of((1 - core) * 24, 8)
+    end = begin(remote(fin.at[pl.ds(give, 24)], other, fin_send, fin_recv, partner))
+    for b in range(4):
+        out_ref[:, core * 4 + b, :] = fin[pl.ds(keep, 24), b * 1024 : b * 1024 + 1024]
+    end.wait_recv()
+    for b in range(4):
+        out_ref[:, (1 - core) * 4 + b, :] = other[:, b * 1024 : b * 1024 + 1024]
+    for copy in copies:
+        copy.wait_send()
+
+
+def project_out(att, w):
+    rows, depth = att.shape
+    bf, f32 = jnp.bfloat16, jnp.float32
+    vmem = pl.BlockSpec(memory_space=pltpu.VMEM)
+
+    def units(*lead):
+        return pltpu.VMEM((*lead, 48, CHUNK), bf)
+
+    def sems(*shape):
+        return pltpu.SemaphoreType.DMA(shape)
+
+    return pl.pallas_call(
+        out_kernel,
+        name="project_out",
+        out_shape=jax.ShapeDtypeStruct((24, 8, 1024), f32),
+        in_specs=[vmem, pl.BlockSpec(memory_space=pl.ANY)],
+        out_specs=vmem,
+        scratch_shapes=[
+            pltpu.VMEM((rows, 2 * depth), bf),
+            pltpu.VMEM((2 * depth, LANES), bf),
+            units(4, 4, 2), units(4, 2), units(4, 2, 2), units(4, 2), units(4),
+            units(4, 2, 4), units(4, 4), units(4, 4), units(4, 3),
+            pltpu.VMEM((48, LANES), f32),
+            pltpu.VMEM((24, LANES), f32),
+            sems(8), sems(8), sems(8), sems(4, 7), sems(4, 7), sems(4, 4), sems(4, 4),
+            pltpu.SemaphoreType.DMA, pltpu.SemaphoreType.DMA,
+            pltpu.SemaphoreType.DMA, pltpu.SemaphoreType.DMA,
+        ],
+        compiler_params=pltpu.CompilerParams(collective_id=3, has_side_effects=True, vmem_limit_bytes=40 << 20),
+    )(att, w)
+
+
 def rms_norm(values):
     return values * lax.rsqrt(jnp.mean(values * values, axis=-1, keepdims=True) + 1e-06)
 
@@ -351,15 +526,10 @@
     attended = (
         (numerator / denominator[..., None]).reshape(shard_rows, head_width).astype(jnp.bfloat16)
     )
-    patch_out = lax.psum_scatter(
-        jnp.dot(attended, global_out, preferred_element_type=jnp.float32).astype(jnp.bfloat16),
-        "tp",
-        scatter_dimension=0,
-        tiled=True,
-    )
-    earlier_row = from_behind(patch_out[-1:], ("ctx", "tp"), 1)
-    patch_out = jnp.concatenate([earlier_row, patch_out[:-1]], axis=0)
-    context = patch_out.reshape(byte_count, byte_embeds.shape[1])
+    before = from_behind(attended[-1:], "ctx", 1)
+    attended = jnp.concatenate([before, attended[:-1]], axis=0)
+    context = project_out(attended, global_out).reshape(byte_count, byte_embeds.shape[1])
+    context = context.astype(jnp.bfloat16)
     state = local_embeds.astype(jnp.float32) + context.astype(jnp.float32)
     hidden, *factors = local_pass(state, local_qkv, local_out, cotangent)
     grad_qkv, grad_out = reduce_grads(*factors)

time: 290 us -> 244 us (0.84)
  waiting for transfers between devices: 168 us -> 104 us
  Pallas kernels: 40.5 us -> 69.2 us
  matrix products: 33.8 us -> 27.1 us
    reduce_scatter x1 -> x0, waiting for transfers between devices: 63.1 us -> none  [per_device(): lax.psum_scatter(jnp.dot(attended, global_out, preferred_element_type=jnp...]
    pallas_call x0 -> x1, Pallas kernels: none -> 31.9 us  [project_out(): pl.pallas_call(out_kernel, name='project_out', out_shape=jax.ShapeDtypeSt...]
    dot_general x1 -> x0, matrix products: 4.49 us -> none  [per_device(): jnp.dot(attended, global_out, preferred_element_type=jnp.float32)]
    pallas_call x1, Pallas kernels: 40.5 us -> 37.4 us  [reduce_grads(): pl.pallas_call(grads_kernel, name='reduce_grads', out_shape=(jax.ShapeDty...]
  transfers between devices with their start and end apart: 4 -> 3, of which waited for: 3 -> 2; matrix products, arithmetic and copies ran while one was open for 5% -> 5% of each run, Pallas kernels for 0% -> 0%
where the time goes in v3:
time: 244 us; the launch traced here: 243 us
  waiting for transfers between devices  104 us (43%)
  Pallas kernels  69.2 us (28%)
  matrix products  27.1 us (11%)
  local copies, waits for them, and re-layouts  17.2 us (7%)
  between operations  14.4 us (6%)
  other arithmetic  8.57 us (4%)
    all_gather x1, waiting for transfers between devices, per_device(): lax.all_gather(jnp.concatenate([keys_mine, values_mine], axis=1), 'ctx',...  58.3 us
    all_gather x1, waiting for transfers between devices, per_device(): lax.all_gather(normed, 'tp', axis=0, tiled=True)  46 us
    pallas_call x1, Pallas kernels, reduce_grads(): pl.pallas_call(grads_kernel, name='reduce_grads', out_shape=(jax.ShapeDty...  37.4 us
    pallas_call x1, Pallas kernels, project_out(): pl.pallas_call(out_kernel, name='project_out', out_shape=jax.ShapeDtypeSt...  31.9 us
    dot_general x1, matrix products, per_device(): jnp.einsum('nd,cdh->nch', lax.all_gather(normed, 'tp', axis=0, tiled=True...  11.2 us
    dot_general x1, local copies, waits for them, and re-layouts, local_pass(): jnp.dot(normed, local_qkv[layer], preferred_element_type=jnp.float32)  8.67 us
  transfers between devices with their start and end apart: 3, of which 2 were waited for; matrix products, arithmetic and copies ran while one was open for 5% of the time, Pallas kernels for 0%

profile of v3, /device:TPU:1, one launch (start us, length us, event | category | flops | bytes accessed | tf_op | source)
XLA Modules:
  0.0 243.2 jit_solution(14969503768932307636)
XLA Ops:
  7.2 1.3 reshape.142
  8.5 1.2 multiply_reduce_fusion.6
  9.9 0.9 multiply_convert_fusion.1
  10.8 46.0 %all-gather.3.cloned.1.call-done = bf16[384,8192]{1,0:T(8,128)(2,1)} async-done(((bf16[24,8192]{1,0:T(8,128)(2,1)}), bf16[384,8192]{1,0:T(8,128)(2,1)}) %all-gather.3.cloned.1.call-update) | async-done | bytes 6291472 | tf_op jit(solution)/shard_map/all_gather | solution.py:495
  56.9 11.2 %fusion.2 = f32[384,3,256]{0,2,1:T(8,128)S(1)} fusion(bf16[3,8192,256]{2,1,0:T(8,128)(2,1)} %param.9, bf16[384,8192]{1,0:T(8,128)(2,1)} %all-gather.3.cloned.1.call-done), kind=kOutput, calls=%fused_computation.3 | convolution fusion | flops 4831838208 | bytes 20054016 | tf_op jit(solution)/shard_map/nd,cdh->nch/dot_general | solution.py:493
  68.1 1.0 copy-done.6
  69.2 0.9 copy.24
  70.1 1.0 slice.88
  71.3 1.2 multiply_convert_fusion.3
  72.5 0.8 pad_maximum_fusion
  73.4 1.7 fusion.38
  75.1 1.9 iota_compare_fusion
  77.2 58.3 %all-gather.5.cloned.1.call-done = bf16[3072,4,128]{2,0,1:T(8,128)(2,1)} async-done(((bf16[384,4,128]{2,0,1:T(8,128)(2,1)}), bf16[3072,4,128]{2,0,1:T(8,128)(2,1)}) %all-gather.5.cloned.1.call-update) | async-done | bytes 3145744 | tf_op jit(solution)/shard_map/all_gather | solution.py:510
  135.5 4.2 %fusion = (f32[384,2]{0,1:T(2,128)S(1)}, f32[2,3072,384]{2,1,0:T(8,128)S(1)}) fusion(pred[384,3072]{0,1:T(8,128)(4,1)} %iota_compare_fusion, bf16[3072,4,128]{2,0,1:T(8,128)(2,1)} %all-gather.5.cloned.1.call-done, f32[384,2,128]{2,0,1:T(8,128)S(1)} %copy.26, f32[384,2]{0,1:T(2,128)S(1)} %add_rsqrt_fusion), kind=kOutput, calls=%fused_computation.1 | convolution fusion | flops 611253504 | bytes 14161920 | tf_op jit(solution)/shard_map/rha,kha->rhk/dot_general | solution.py:515
  139.7 2.5 %fusion.27 = bf16[384,2,128]{0,2,1:T(8,128)(2,1)S(1)} fusion(bf16[3072,4,128]{2,0,1:T(8,128)(2,1)S(1)} %copy-done.8, f32[2,3072,384]{2,1,0:T(8,128)S(1)} %get-tuple-element.18, pred[384,3072]{0,1:T(8,128)(4,1)S(1)} %copy-done.5, f32[384,2]{0,1:T(2,128)S(1)} %get-tuple-element.17), kind=kOutput, calls=%fused_computation.29 | convolution fusion | flops 611254272 | bytes 13962240 | tf_op jit(solution)/shard_map/rhk,kha->rha/dot_general | solution.py:521
  142.4 2.3 collective-permute-start
  144.8 8.7 %copy.45 = bf16[3072,1024]{1,0:T(8,128)(2,1)} copy(bf16[3072,1024]{0,1:T(8,128)(2,1)} %bitcast.150) | data formatting | bytes 12582912 | tf_op jit(solution)/shard_map/dot_general | solution.py:472
  153.7 2.2 copy-done.1
  155.9 31.9 %project_out.1 = f32[24,8,1024]{2,1,0:T(8,128)S(1)} custom-call(bf16[384,256]{1,0:T(8,128)(2,1)S(1)} %pad_maximum_fusion.1.att_ref, bf16[256,8192]{1,0:T(8,128)(2,1)S(1)} %copy-done.1), custom_call_target="tpu_custom_call" | custom-call | tf_op jit(solution)/shard_map/project_out/pallas_call | solution.py:428
  188.1 2.2 fusion.40
  190.3 0.5 multiply_reduce_fusion.4
  190.8 0.6 select_reduce_fusion
  191.5 0.4 convolution_bitcast_fusion.2
  191.9 0.9 multiply_reduce_fusion.2
  192.9 0.4 fusion.16
  193.3 0.6 convolution_bitcast_fusion
  193.9 0.9 multiply_reduce_fusion.1
  194.9 1.2 fusion.30
  196.4 1.3 fusion.18
  197.8 37.4 %reduce_grads.1 = (f32[8,3072]{1,0:T(8,128)S(1)}, f32[8,1024]{1,0:T(8,128)S(1)}) custom-call(bf16[192,1024]{1,0:T(8,128)(2,1)S(1)} %multiply_convert_fusion.xn_ref, bf16[192,3072]{1,0:T(8,128)(2,1)S(1)} %bitcast.147, bf16[192,1024]{1,0:T(8,128)(2,1)S(1)} %get-tuple-element.16.ab_ref, bf16[192,1024]{1,0:T(8,128)(2,1)S(1)} %copy-done.2), custom_call_target="tpu_custom_call" | custom-call | tf_op jit(solution)/shard_map/reduce_grads/pallas_call | solution.py:249
  235.1 0.6 copy.52
  235.8 0.6 copy.53
  (47 shorter events, 2.0 us)
Async XLA Ops:
  7.2 66.2 %copy-start = (bf16[1,1024,1024]{2,1,0:T(8,128)(2,1)S(1)}, bf16[1,1024,1024]{2,1,0:T(8,128)(2,1)}, u32[]{:S(2)}) copy-start(bf16[1,1024,1024]{2,1,0:T(8,128)(2,1)} %param.12) | copy-start | bytes 6291460
  7.2 49.7 %all-gather.3.cloned.1.call-start = ((), (), s32[]{:S(2)}) async-start(), calls=%async_computation | async-start | bytes 6684672 | tf_op jit(solution)/shard_map/all_gather | solution.py:495
  10.8 124.7 %all-gather.5.cloned.1.call-start = ((), (), s32[]{:S(2)}) async-start(), calls=%async_computation.1 | async-start | bytes 3538944 | tf_op jit(solution)/shard_map/all_gather | solution.py:510
  68.1 1.0 copy-start.6
  69.1 4.2 %copy-start.2 = (bf16[192,1024]{1,0:T(8,128)(2,1)S(1)}, bf16[192,1024]{1,0:T(8,128)(2,1)}, u32[]{:S(2)}) copy-start(bf16[192,1024]{1,0:T(8,128)(2,1)} %gb_ref) | copy-start | bytes 1179652
  135.5 4.2 %copy-start.5 = (pred[384,3072]{0,1:T(8,128)(4,1)S(1)}, pred[384,3072]{0,1:T(8,128)(4,1)}, u32[]{:S(2)}) copy-start(pred[384,3072]{0,1:T(8,128)(4,1)} %iota_compare_fusion) | copy-start | bytes 3538948
  135.5 4.2 %copy-start.8 = (bf16[3072,4,128]{2,0,1:T(8,128)(2,1)S(1)}, bf16[3072,4,128]{2,0,1:T(8,128)(2,1)}, u32[]{:S(2)}) copy-start(bf16[3072,4,128]{2,0,1:T(8,128)(2,1)} %all-gather.5.cloned.1.call-done) | copy-start | bytes 9437188
  142.4 11.2 %collective-permute-start = (bf16[1,256]{1,0:T(2,128)(2,1)S(1)}, bf16[1,256]{1,0:T(2,128)(2,1)S(1)}, u32[]{:S(2)}, u32[]{:S(2)}) collective-permute-start(bf16[1,256]{1,0:T(2,128)(2,1)S(1)} %bitcast.160), channel_id=1, source_target_pairs={{0,16},{16,32},{32,48},{48,64},{64,80},{80,96},{96,112},{1,17},{17... | collective-permute-start | bytes 1544 | tf_op jit(solution)/shard_map/ppermute | solution.py:19
  153.4 34.3 %copy-start.4 = (bf16[192,1024]{1,0:T(8,128)(2,1)S(1)}, bf16[192,1024]{1,0:T(8,128)(2,1)}, u32[]{:S(2)}) copy-start(bf16[192,1024]{1,0:T(8,128)(2,1)} %param.8) | copy-start | bytes 1179652
  153.7 2.2 copy-start.1
  155.8 32.2 %copy-start.3 = (bf16[3072,1024]{1,0:T(8,128)(2,1)S(1)}, bf16[3072,1024]{1,0:T(8,128)(2,1)}, u32[]{:S(2)}) copy-start(bf16[3072,1024]{1,0:T(8,128)(2,1)} %copy.45) | copy-start | bytes 18874372
  190.3 1.2 copy-start.7
Sparse Core Ops, SparseCore 0:
  10.9 45.9 all-gather.2
  73.4 62.0 all-gather.4

commit v4 on v3

--- a/solution.py
+++ b/solution.py
@@ -11,12 +11,6 @@
 HEAD_DIM = 128
 LOCAL_HEADS = 8
 LOCAL_HEAD_DIM = 128
-
-
-def from_behind(value, axis, steps):
-    count = lax.axis_size(axis)
-    initial, last = (max(0, -steps), min(count, count - steps))
-    return lax.ppermute(value, axis, [(source, source + steps) for source in range(initial, last)])
 
 
 MESH = pl.DeviceIdType.MESH
@@ -275,9 +269,129 @@
 LANES = 4096
 
 
+def attend(
+    x, y, z, core, begin, q_ref, k_ref, v_ref, att2, q2, ka, va, acc, tall, back,
+    y_send, y_recv, z_send, z_recv, row_send, row_recv, back_send, back_recv, swap_send, swap_recv,
+):
+    half = lax.div(y, 2)
+    partner = device_at(x, y, z, 1 - core)
+    opposite = device_at(x, lax.rem(y + 2, 4), z, core)
+    rows = q_ref.shape[0]
+    mine = pl.ds(pl.multiple_of(half * HEAD_DIM, HEAD_DIM), HEAD_DIM)
+    its = pl.ds(pl.multiple_of((1 - half) * HEAD_DIM, HEAD_DIM), HEAD_DIM)
+
+    across = [
+        begin(remote(source.at[:, its], target, y_send.at[n], y_recv.at[n], opposite))
+        for n, (source, target) in enumerate(
+            ((k_ref, ka.at[z, half]), (v_ref, va.at[z, half]), (q_ref, q2.at[half]))
+        )
+    ]
+
+    def up(d, kind, which):
+        block = half if which == 0 else 1 - half
+        target = (ka, va)[kind].at[z, block]
+        source = (k_ref, v_ref)[kind].at[:, mine] if which == 0 else target
+        return remote(
+            source, target, z_send.at[d - 1, kind, which], z_recv.at[d - 1, kind, which],
+            device_at(x, y, lax.rem(z + d, 4), core),
+        )
+
+    lifts = {(d, kind, which): up(d, kind, which) for which in (0, 1) for kind in (0, 1) for d in (1, 3, 2)}
+    for (d, kind, which), copy in lifts.items():
+        if which == 0:
+            pl.when(z + d <= 3)(copy.start)
+    ka[z, half] = k_ref[:, mine]
+    va[z, half] = v_ref[:, mine]
+    q2[half] = q_ref[:, mine]
+    for kind in (0, 1):
+        across[kind].wait_recv()
+        for d in (1, 3, 2):
+            pl.when(z + d <= 3)(lifts[d, kind, 1].start)
+    across[2].wait_recv()
+
+    tile = 128
+    tiles = rows // tile
+    scale = 1.0 / math.sqrt(HEAD_DIM)
+
+    def attend_tile(block, n, keys, values, masked, first):
+        s = lax.dot_general(
+            q2[block, n * tile : (n + 1) * tile], keys, (((1,), (1,)), ((), ())), preferred_element_type=jnp.float32
+        )
+        e = jnp.exp(s * scale)
+        if masked:
+            row = n * tile + lax.broadcasted_iota(jnp.int32, e.shape, 0)
+            e = jnp.where(lax.broadcasted_iota(jnp.int32, e.shape, 1) <= row, e, 0.0)
+        sums = jnp.dot(e.astype(jnp.bfloat16), values, preferred_element_type=jnp.float32)
+        at = slice(n * tile, (n + 1) * tile)
+        acc[block, at] = sums if first else acc[block, at] + sums
+
+    def with_ones(values):
+        return jnp.concatenate([values, jnp.ones_like(values)], axis=1)
+
+    for k in (0, 1):
+        keys, values = ka[z, k], with_ones(va[z, k])
+        for block in range(k, 2):
+            for n in range(tiles):
+                attend_tile(block, n, keys, values, block == k, k == 0)
+
+    for d in (1, 3, 2):
+
+        @pl.when(z >= d)
+        def _():
+            for kind in (0, 1):
+                for which in (0, 1):
+                    lifts[d, kind, which].wait_recv()
+            below = lax.rem(z + 4 - d, 4)
+
+            def body(k, carry):
+                keys, values = ka[below, k], with_ones(va[below, k])
+                for block in (0, 1):
+                    for n in range(tiles):
+                        attend_tile(block, n, keys, values, False, False)
+                return carry
+
+            lax.fori_loop(0, 2, body, 0)
+
+    for block in (0, 1):
+        tall[8 + block * rows : 8 + (block + 1) * rows] = acc[block, :, 0:HEAD_DIM] / acc[block, :, HEAD_DIM:]
+    row = remote(
+        tall.at[pl.ds(2 * rows, 8)], tall.at[pl.ds(0, 8)], row_send, row_recv,
+        device_at(x, y, lax.rem(z + 1, 4), core),
+    )
+    pl.when(z < 3)(row.start)
+    pl.when(z > 0)(row.wait_recv)
+
+    @pl.when(z == 0)
+    def _():
+        tall[0:8] = jnp.zeros((8, HEAD_DIM), jnp.float32)
+
+    for part in (0, 1):
+
+        @pl.when(half == part)
+        def _():
+            back[...] = tall[7 + (1 - part) * rows : 7 + (2 - part) * rows].astype(jnp.bfloat16)
+            att2[:, part * HEAD_DIM : (part + 1) * HEAD_DIM] = tall[
+                7 + part * rows : 7 + (part + 1) * rows
+            ].astype(jnp.bfloat16)
+
+    width = 2 * HEAD_DIM
+    far_mine = pl.ds(pl.multiple_of(width + half * HEAD_DIM, HEAD_DIM), HEAD_DIM)
+    far_its = pl.ds(pl.multiple_of(width + (1 - half) * HEAD_DIM, HEAD_DIM), HEAD_DIM)
+    returned = begin(remote(back, att2.at[:, mine], back_send, back_recv, opposite))
+    near = begin(remote(att2.at[:, mine], att2.at[:, far_mine], swap_send.at[0], swap_recv.at[0], partner))
+    returned.wait_recv()
+    last = begin(remote(att2.at[:, its], att2.at[:, far_its], swap_send.at[1], swap_recv.at[1], partner))
+    near.wait_recv()
+    last.wait_recv()
+    pl.when(z < 3)(row.wait_send)
+    for (d, kind, which), copy in lifts.items():
+        pl.when(z + d <= 3)(copy.wait_send)
+
+
 def out_kernel(
-    att_ref, w_ref, out_ref, att2, w2, pbuf, relay, near, psum, pgot, qbuf, qgot, qsum, qlast, fin, other,
-    w_sem, pair_send, pair_recv, p_send, p_recv, q_send, q_recv, att_send, att_recv, fin_send, fin_recv,
+    q_ref, k_ref, v_ref, w_ref, out_ref, q2, ka, va, acc, tall, back, att2, w2, pbuf, relay, near, psum, pgot, qbuf, qgot, qsum, qlast, fin, other,
+    w_sem, pair_send, pair_recv, p_send, p_recv, q_send, q_recv, fin_send, fin_recv,
+    *att_sems,
 ):
     x, y, z, core = coords()
     pair = lax.rem(y, 2)
@@ -287,8 +401,11 @@
     def beside(step):
         return device_at(lax.rem(x + step, 4), y, z, core)
 
-    greet([partner, across, beside(1), beside(2), beside(3)])
-    depth = att_ref.shape[1]
+    greet(
+        [partner, across, beside(1), beside(2), beside(3), device_at(x, lax.rem(y + 2, 4), z, core)]
+        + [device_at(x, y, lax.rem(z + d, 4), core) for d in (1, 2, 3)]
+    )
+    depth = q_ref.shape[1]
     copies = []
 
     def begin(copy):
@@ -296,7 +413,6 @@
         copies.append(copy)
         return copy
 
-    swap = begin(remote(att_ref, att2.at[:, depth : 2 * depth], att_send, att_recv, partner))
     order = [c for n in range(4) for c in (4 + n, n)]
     theirs, mine = {}, {}
     for c in order:
@@ -308,8 +424,9 @@
         )
         mine[c] = pltpu.make_async_copy(w_ref.at[:, keep], w2.at[pl.ds(0, depth), into], w_sem.at[c])
         mine[c].start()
-    att2[:, 0:depth] = att_ref[...]
-    swap.wait_recv()
+    attend(
+        x, y, z, core, begin, q_ref, k_ref, v_ref, att2, q2, ka, va, acc, tall, back, *att_sems
+    )
 
     right, left, far = lax.rem(x + 1, 4), lax.rem(x + 3, 4), lax.rem(x + 2, 4)
     pcopies, qcopies = {}, {}
@@ -414,8 +531,8 @@
         copy.wait_send()
 
 
-def project_out(att, w):
-    rows, depth = att.shape
+def attend_and_project(q, k, v, w):
+    rows, depth = q.shape
     bf, f32 = jnp.bfloat16, jnp.float32
     vmem = pl.BlockSpec(memory_space=pltpu.VMEM)
 
@@ -427,11 +544,17 @@
 
     return pl.pallas_call(
         out_kernel,
-        name="project_out",
+        name="attend_out",
         out_shape=jax.ShapeDtypeStruct((24, 8, 1024), f32),
-        in_specs=[vmem, pl.BlockSpec(memory_space=pl.ANY)],
+        in_specs=[vmem] * 3 + [pl.BlockSpec(memory_space=pl.ANY)],
         out_specs=vmem,
         scratch_shapes=[
+            pltpu.VMEM((2, rows, HEAD_DIM), bf),
+            pltpu.VMEM((4, 2, rows, HEAD_DIM), bf),
+            pltpu.VMEM((4, 2, rows, HEAD_DIM), bf),
+            pltpu.VMEM((2, rows, 2 * HEAD_DIM), f32),
+            pltpu.VMEM((8 + 2 * rows, HEAD_DIM), f32),
+            pltpu.VMEM((rows, HEAD_DIM), bf),
             pltpu.VMEM((rows, 2 * depth), bf),
             pltpu.VMEM((2 * depth, LANES), bf),
             units(4, 4, 2), units(4, 2), units(4, 2, 2), units(4, 2), units(4),
@@ -440,10 +563,12 @@
             pltpu.VMEM((24, LANES), f32),
             sems(8), sems(8), sems(8), sems(4, 7), sems(4, 7), sems(4, 4), sems(4, 4),
             pltpu.SemaphoreType.DMA, pltpu.SemaphoreType.DMA,
+            sems(3), sems(3), sems(3, 2, 2), sems(3, 2, 2),
             pltpu.SemaphoreType.DMA, pltpu.SemaphoreType.DMA,
+            pltpu.SemaphoreType.DMA, pltpu.SemaphoreType.DMA, sems(2), sems(2),
         ],
         compiler_params=pltpu.CompilerParams(collective_id=3, has_side_effects=True, vmem_limit_bytes=40 << 20),
-    )(att, w)
+    )(q, k, v, w)
 
 
 def rms_norm(values):
@@ -506,29 +631,8 @@
         jnp.bfloat16
     )
     values_mine = projected[:, 2].reshape(shard_rows, head_count, HEAD_DIM).astype(jnp.bfloat16)
-    query_pos = lax.axis_index("ctx") * shard_rows + jnp.arange(shard_rows, dtype=jnp.int32)
-    pieces = lax.all_gather(
-        jnp.concatenate([keys_mine, values_mine], axis=1), "ctx", axis=0, tiled=True
-    )
-    key_piece, value_piece = pieces[:, :head_count], pieces[:, head_count:]
-    key_count = key_piece.shape[0]
-    scores = jnp.einsum(
-        "rha,kha->rhk", queries, key_piece, preferred_element_type=jnp.float32
-    ) / math.sqrt(HEAD_DIM)
-    key_pos = jnp.arange(key_count, dtype=jnp.int32)
-    allowed = key_pos[None, None, :] <= query_pos[:, None, None]
-    expo = jnp.where(allowed, jnp.exp(scores), 0.0)
-    numerator = jnp.einsum(
-        "rhk,kha->rha", expo.astype(jnp.bfloat16), value_piece, preferred_element_type=jnp.float32
-    )
-    denominator = jnp.sum(expo, axis=-1)
-    numerator, denominator = (numerator, denominator)
-    attended = (
-        (numerator / denominator[..., None]).reshape(shard_rows, head_width).astype(jnp.bfloat16)
-    )
-    before = from_behind(attended[-1:], "ctx", 1)
-    attended = jnp.concatenate([before, attended[:-1]], axis=0)
-    context = project_out(attended, global_out).reshape(byte_count, byte_embeds.shape[1])
+    flat = [part.reshape(shard_rows, head_width) for part in (queries, keys_mine, values_mine)]
+    context = attend_and_project(*flat, global_out).reshape(byte_count, byte_embeds.shape[1])
     context = context.astype(jnp.bfloat16)
     state = local_embeds.astype(jnp.float32) + context.astype(jnp.float32)
     hidden, *factors = local_pass(state, local_qkv, local_out, cotangent)

time: 244 us -> 194 us (0.80)
  waiting for transfers between devices: 104 us -> 35.6 us
  Pallas kernels: 69.2 us -> 96 us
  matrix products: 27.1 us -> 21.3 us
    all_gather x1 -> x0, waiting for transfers between devices: 58.3 us -> none  [per_device(): lax.all_gather(jnp.concatenate([keys_mine, values_mine], axis=1), 'ctx',...]
    pallas_call x1, Pallas kernels: 31.9 us -> 48.7 us  [attend_and_project(): pl.pallas_call(out_kernel, name='attend_out', out_shape=jax.ShapeDtypeStr...]
    all_gather x1, waiting for transfers between devices: 46 us -> 35.5 us  [per_device(): lax.all_gather(normed, 'tp', axis=0, tiled=True)]
    pallas_call x1, Pallas kernels: 37.4 us -> 47.3 us  [reduce_grads(): pl.pallas_call(grads_kernel, name='reduce_grads', out_shape=(jax.ShapeDty...]
    dot_general x2 -> x0, matrix products: 6.69 us -> none  [the longest x1 4.18 us: per_device(): jnp.einsum('rha,kha->rhk', queries, key_piece, preferred_element_type=jnp...]
    mul x0 -> x4, local copies, waits for them, and re-layouts: none -> 3.01 us  [the longest x2 1.86 us: rms_norm(): values * lax.rsqrt(jnp.mean(values * values, axis=-1, keepdims=True) + 1e...]
  transfers between devices with their start and end apart: 3 -> 1, of which waited for: 2 -> 1; matrix products, arithmetic and copies ran while one was open for 5% -> 5% of each run, Pallas kernels for 0% -> 0%
where the time goes in v4:
time: 194 us; the launch traced here: 193 us
  Pallas kernels  96 us (49%)
  waiting for transfers between devices  35.6 us (18%)
  matrix products  21.3 us (11%)
  local copies, waits for them, and re-layouts  17.6 us (9%)
  between operations  14.3 us (7%)
  other arithmetic  8.27 us (4%)
    pallas_call x1, Pallas kernels, attend_and_project(): pl.pallas_call(out_kernel, name='attend_out', out_shape=jax.ShapeDtypeStr...  48.7 us
    pallas_call x1, Pallas kernels, reduce_grads(): pl.pallas_call(grads_kernel, name='reduce_grads', out_shape=(jax.ShapeDty...  47.3 us
    all_gather x1, waiting for transfers between devices, per_device(): lax.all_gather(normed, 'tp', axis=0, tiled=True)  35.5 us
    dot_general x1, matrix products, per_device(): jnp.einsum('nd,cdh->nch', lax.all_gather(normed, 'tp', axis=0, tiled=True...  9.86 us
    dot_general x1, local copies, waits for them, and re-layouts, local_pass(): jnp.dot(normed, local_qkv[layer], preferred_element_type=jnp.float32)  8.72 us
    dot_general x1, matrix products, local_pass(): jnp.dot(normed, local_qkv[layer], preferred_element_type=jnp.float32)  4.47 us
    unnamed x14, local copies, waits for them, and re-layouts  4.43 us
    reduce_sum x6, other arithmetic, rms_norm(): jnp.mean(values * values, axis=-1, keepdims=True) + 1e-06  3.89 us
  transfers between devices with their start and end apart: 1, of which 1 were waited for; matrix products, arithmetic and copies ran while one was open for 5% of the time, Pallas kernels for 0%

profile of v4, /device:TPU:1, one launch (start us, length us, event | category | flops | bytes accessed | tf_op | source)
XLA Modules:
  0.0 193.2 jit_solution(15004245415663598707)
XLA Ops:
  7.2 1.3 reshape.121
  8.5 1.2 multiply_reduce_fusion.6
  9.9 0.9 multiply_convert_fusion.1
  10.8 8.7 %copy.63 = bf16[3072,1024]{1,0:T(8,128)(2,1)} copy(bf16[3072,1024]{0,1:T(8,128)(2,1)} %bitcast.139) | data formatting | bytes 12582912 | tf_op jit(solution)/shard_map/dot_general | solution.py:597
  19.5 1.8 fusion.24
  21.3 35.5 %all-gather.2.cloned.1.call-done = bf16[384,8192]{1,0:T(8,128)(2,1)} async-done(((bf16[24,8192]{1,0:T(8,128)(2,1)}), bf16[384,8192]{1,0:T(8,128)(2,1)}) %all-gather.2.cloned.1.call-update) | async-done | bytes 6291472 | tf_op jit(solution)/shard_map/all_gather | solution.py:620
  56.9 9.9 %fusion = f32[384,3,256]{2,0,1:T(8,128)S(1)} fusion(bf16[3,8192,256]{2,1,0:T(8,128)(2,1)} %param.9, bf16[384,8192]{1,0:T(8,128)(2,1)} %all-gather.2.cloned.1.call-done), kind=kOutput, calls=%fused_computation | convolution fusion | flops 4831838208 | bytes 20054016 | tf_op jit(solution)/shard_map/nd,cdh->nch/dot_general | solution.py:618
  66.8 1.0 copy-done.4
  67.8 0.9 mul.159
  68.7 1.5 reduce_sum.112
  70.2 0.7 add_rsqrt_fusion.1
  70.9 0.2 mul.164
  71.1 0.5 reduce_sum.113
  71.7 1.4 mul.160
  73.1 0.5 mul.165
  73.5 1.2 fusion.22
  74.7 2.2 %copy-done.1 = bf16[256,8192]{1,0:T(8,128)(2,1)S(1)} copy-done((bf16[256,8192]{1,0:T(8,128)(2,1)S(1)}, bf16[256,8192]{1,0:T(8,128)(2,1)}, u32[]{:S(2)}) %copy-start.1) | copy-done | bytes 4194328
  76.9 48.7 %attend_out.1 = f32[24,8,1024]{2,1,0:T(8,128)S(1)} custom-call(bf16[384,256]{1,0:T(8,128)(2,1)S(1)} %get-tuple-element.14.q_ref, bf16[384,256]{1,0:T(8,128)(2,1)S(1)} %get-tuple-element.13.k_ref, bf16[384,256]{1,0:T(8,128)(2,1)S(1)} %fusion.37.v_ref, bf16[256,8192]{1,0:T(8,128)(2,1)S(1)} %copy-done.1), custom_call_target="tpu_custom_call" | custom-call | tf_op jit(solution)/shard_map/attend_out/pallas_call | solution.py:545
  126.0 4.5 %fusion.26 = f32[24,8,3,8,128]{4,1,3,2,0:T(8,128)S(1)} fusion(bf16[3,8,128,1024,1]{3,2,1,0,4:T(8,128)(2,1)} %bitcast.140, bf16[192,1024]{1,0:T(8,128)(2,1)S(1)} %multiply_convert_fusion.xn_ref), kind=kOutput, calls=%fused_computation.50 | convolution fusion | flops 1207959552 | bytes 9043968 | tf_op jit(solution)/shard_map/dot_general | solution.py:597
  130.5 0.5 multiply_reduce_fusion.4
  131.0 0.6 select_reduce_fusion
  131.7 0.4 convolution_bitcast_fusion.2
  132.1 0.9 multiply_reduce_fusion.2
  133.0 0.4 fusion.9
  133.5 0.6 convolution_bitcast_fusion
  134.1 0.9 multiply_reduce_fusion.1
  135.1 1.0 fusion.14
  136.1 0.2 add_convert_fusion
  136.4 1.3 fusion.11
  137.7 47.3 %reduce_grads.1 = (f32[8,3072]{1,0:T(8,128)S(1)}, f32[8,1024]{1,0:T(8,128)S(1)}) custom-call(bf16[192,1024]{1,0:T(8,128)(2,1)S(1)} %multiply_convert_fusion.xn_ref, bf16[192,3072]{1,0:T(8,128)(2,1)S(1)} %bitcast.136, bf16[192,1024]{1,0:T(8,128)(2,1)S(1)} %get-tuple-element.18.ab_ref, bf16[192,1024]{1,0:T(8,128)(2,1)S(1)} %copy-done.2), custom_call_target="tpu_custom_call" | custom-call | tf_op jit(solution)/shard_map/reduce_grads/pallas_call | solution.py:243
  185.1 0.6 copy.73
  185.7 0.6 copy.74
  (28 shorter events, 1.0 us)
Async XLA Ops:
  7.2 12.4 %copy-start = (bf16[1,1024,1024]{2,1,0:T(8,128)(2,1)S(1)}, bf16[1,1024,1024]{2,1,0:T(8,128)(2,1)}, u32[]{:S(2)}) copy-start(bf16[1,1024,1024]{2,1,0:T(8,128)(2,1)} %param.12) | copy-start | bytes 6291460
  7.2 49.7 %all-gather.2.cloned.1.call-start = ((), (), s32[]{:S(2)}) async-start(), calls=%async_computation | async-start | bytes 6684672 | tf_op jit(solution)/shard_map/all_gather | solution.py:620
  10.8 8.7 %copy-start.2 = (bf16[192,1024]{1,0:T(8,128)(2,1)S(1)}, bf16[192,1024]{1,0:T(8,128)(2,1)}, u32[]{:S(2)}) copy-start(bf16[192,1024]{1,0:T(8,128)(2,1)} %gb_ref) | copy-start | bytes 1179652
  66.7 1.0 copy-start.4
  74.7 2.2 %copy-start.1 = (bf16[256,8192]{1,0:T(8,128)(2,1)S(1)}, bf16[256,8192]{1,0:T(8,128)(2,1)}, u32[]{:S(2)}) copy-start(bf16[256,8192]{1,0:T(8,128)(2,1)} %w_ref.1) | copy-start | bytes 12582916
  76.9 48.7 %copy-start.3 = (bf16[192,1024]{1,0:T(8,128)(2,1)S(1)}, bf16[192,1024]{1,0:T(8,128)(2,1)}, u32[]{:S(2)}) copy-start(bf16[192,1024]{1,0:T(8,128)(2,1)} %param.8) | copy-start | bytes 1179652
  130.5 1.2 copy-start.5
Sparse Core Ops, SparseCore 0:
  10.9 45.9 all-gather.1

commit v5 on v4

--- a/solution.py
+++ b/solution.py
@@ -267,6 +267,208 @@
 
 CHUNK = 512
 LANES = 4096
+
+
+def project_kernel(
+    bytes_ref, w_ref, q_ref, k_ref, v_ref, theirs, wide_rows, xs, ws, acc,
+    swap_send, swap_recv, w_sem, p_send, p_recv, q_send, q_recv, f_send, f_recv,
+):
+    x, y, z, core = coords()
+    pair = lax.rem(y, 2)
+    partner = device_at(x, y, z, 1 - core)
+    across = device_at(x, y + 1 - 2 * pair, z, core)
+
+    def beside(step):
+        return device_at(lax.rem(x + step, 4), y, z, core)
+
+    greet([partner, across, beside(1), beside(2), beside(3)])
+    copies = []
+
+    def begin(copy):
+        copy.start()
+        copies.append(copy)
+        return copy
+
+    swap = begin(remote(bytes_ref, theirs, swap_send, swap_recv, partner))
+    order = [c for n in range(4) for c in (4 + n, n)]
+    mine, its = [core * 8 + c for c in range(8)], [(1 - core) * 8 + c for c in range(8)]
+    loads = {}
+    for c in order:
+        for who, g in enumerate((mine[c], its[c])):
+            load = pltpu.make_async_copy(
+                w_ref.at[:, pl.ds(pl.multiple_of(g * CHUNK, CHUNK), CHUNK), :], ws.at[g], w_sem.at[who, c]
+            )
+            load.start()
+            loads[who, c] = load
+    rows = bytes_ref.shape[0]
+    lane_tiles = bytes_ref.shape[1] // 128
+
+    def spread(source, side):
+        at = pl.ds(pl.multiple_of(side * rows, rows), rows)
+        for n in range(lane_tiles):
+            wide_rows[n, at] = source[:, n * 128 : (n + 1) * 128].astype(jnp.float32)
+
+    spread(bytes_ref, core)
+    acc[...] = jnp.zeros_like(acc)
+    swap.wait_recv()
+    spread(theirs, 1 - core)
+
+    def entries(n, b):
+        return wide_rows[n, pl.ds(b, 48, stride=PATCH), :]
+
+    squares = jnp.zeros((48, 128), jnp.float32)
+    for n in range(lane_tiles):
+        for b in range(PATCH):
+            squares = squares + entries(n, b) * entries(n, b)
+    mean = jnp.sum(squares, axis=-1, keepdims=True) / (PATCH * lane_tiles * 128)
+    scale = lax.rsqrt(mean + 1e-06)
+    for side in (0, 1):
+
+        @pl.when(core == side)
+        def _():
+            for c in range(8):
+                for n in range(4):
+                    normed = entries(c % 2 * 4 + n, side * 4 + c // 2) * scale
+                    xs[side * 8 + c, pair, x, :, n * 128 : (n + 1) * 128] = normed.astype(jnp.bfloat16)
+
+    right, left = lax.rem(x + 1, 4), lax.rem(x + 3, 4)
+    pc, qc = {}, {}
+    for n in range(4):
+        g = mine[n]
+
+        def copy(k, part, peer):
+            return remote(part, part, p_send.at[n, k], p_recv.at[n, k], peer)
+
+        pc[n] = [
+            copy(0, xs.at[g, pair, x], across),
+            copy(1, xs.at[g, :, x], beside(1)),
+            copy(2, xs.at[g, :, x], beside(3)),
+            copy(3, xs.at[g, 0, left], beside(1)),
+            copy(4, xs.at[g, 1, right], beside(3)),
+        ]
+        g = mine[4 + n]
+
+        def copy(k, part, peer):
+            return remote(part, part, q_send.at[n, k], q_recv.at[n, k], peer)
+
+        qc[n] = [copy(0, xs.at[g, pair], across)] + [copy(d, xs.at[g, pair, x], beside(d)) for d in (1, 2, 3)]
+    for n in range(4):
+        begin(pc[n][0])
+        for d in (2, 1, 3):
+            begin(qc[n][d])
+
+    forwards = {
+        c: remote(xs.at[mine[c]], xs.at[mine[c]], f_send.at[c], f_recv.at[c], partner) for c in range(8)
+    }
+
+    def multiply(who, c):
+        loads[who, c].wait()
+        g = (mine, its)[who][c]
+        block = xs[g].reshape(acc.shape[1], CHUNK)
+
+        def body(j, carry):
+            acc[j] += jnp.dot(block, ws[g, j], preferred_element_type=jnp.float32)
+            return carry
+
+        lax.fori_loop(0, 3, body, 0)
+
+    def p_turn(n):
+        pc[n][0].wait_recv()
+        begin(pc[n][1])
+        begin(pc[n][2])
+
+    def q_turn(n):
+        for d in (1, 2, 3):
+            qc[n][d].wait_recv()
+        begin(qc[n][0])
+
+    def p_relay(n):
+        pc[n][1].wait_recv()
+        begin(pc[n][3])
+        pc[n][2].wait_recv()
+        begin(pc[n][4])
+
+    def p_done(n):
+        pc[n][3].wait_recv()
+        pc[n][4].wait_recv()
+        begin(forwards[n])
+        multiply(0, n)
+
+    def q_done(n):
+        qc[n][0].wait_recv()
+        begin(forwards[4 + n])
+        multiply(0, 4 + n)
+
+    def other(c):
+        forwards[c].wait_recv()
+        multiply(1, c)
+
+    p_turn(0)
+    p_turn(1)
+    q_turn(0)
+    p_turn(2)
+    p_turn(3)
+    q_turn(1)
+    q_turn(2)
+    q_turn(3)
+    q_done(0)
+    p_relay(0)
+    other(4)
+    p_relay(1)
+    p_done(0)
+    q_done(1)
+    p_relay(2)
+    other(0)
+    p_done(1)
+    p_relay(3)
+    other(5)
+    other(1)
+    q_done(2)
+    p_done(2)
+    other(6)
+    other(2)
+    p_done(3)
+    q_done(3)
+    other(3)
+    other(7)
+
+    for j, out in enumerate((q_ref, k_ref, v_ref)):
+        for head in range(out.shape[1] // HEAD_DIM):
+            at = slice(head * HEAD_DIM, (head + 1) * HEAD_DIM)
+            value = acc[j, :, at]
+            if j < 2:
+                value = rms_norm(value)
+            out[:, at] = value.astype(jnp.bfloat16)
+    for copy in copies:
+        copy.wait_send()
+
+
+def project_patches(byte_rows, w):
+    bf, f32 = jnp.bfloat16, jnp.float32
+    vmem = pl.BlockSpec(memory_space=pltpu.VMEM)
+    rows, width = byte_rows.shape
+    total, cols = 2 * rows // PATCH * 8, w.shape[2]
+
+    def sems(*shape):
+        return pltpu.SemaphoreType.DMA(shape)
+
+    return pl.pallas_call(
+        project_kernel,
+        name="project_patches",
+        out_shape=[jax.ShapeDtypeStruct((total, cols), bf)] * 3,
+        in_specs=[vmem, pl.BlockSpec(memory_space=pl.ANY)],
+        out_specs=[vmem] * 3,
+        scratch_shapes=[
+            pltpu.VMEM((rows, width), bf),
+            pltpu.VMEM((width // 128, 2 * rows, 128), f32),
+            pltpu.VMEM((16, 2, 4, 48, CHUNK), bf),
+            pltpu.VMEM((16, 3, CHUNK, cols), bf),
+            pltpu.VMEM((3, total, cols), f32),
+            pltpu.SemaphoreType.DMA, pltpu.SemaphoreType.DMA,
+            sems(2, 8), sems(4, 5), sems(4, 5), sems(4, 4), sems(4, 4), sems(8), sems(8),
+        ],
+        compiler_params=pltpu.CompilerParams(collective_id=1, has_side_effects=True, vmem_limit_bytes=44 << 20),
+    )(byte_rows, w)
 
 
 def attend(
@@ -611,27 +813,7 @@
 
 def per_device(byte_embeds, local_embeds, global_qkv, global_out, local_qkv, local_out, cotangent):
     byte_count = byte_embeds.shape[0]
-    patch_count = byte_count // PATCH
-    full_width = PATCH * byte_embeds.shape[1]
-    patch_in = byte_embeds.reshape(patch_count, full_width).astype(jnp.float32)
-    normed = rms_norm(patch_in).astype(jnp.bfloat16)
-    projected = jnp.einsum(
-        "nd,cdh->nch",
-        lax.all_gather(normed, "tp", axis=0, tiled=True),
-        global_qkv,
-        preferred_element_type=jnp.float32,
-    )
-    shard_rows = projected.shape[0]
-    head_width = global_qkv.shape[2]
-    head_count = head_width // HEAD_DIM
-    queries = rms_norm(projected[:, 0].reshape(shard_rows, head_count, HEAD_DIM)).astype(
-        jnp.bfloat16
-    )
-    keys_mine = rms_norm(projected[:, 1].reshape(shard_rows, head_count, HEAD_DIM)).astype(
-        jnp.bfloat16
-    )
-    values_mine = projected[:, 2].reshape(shard_rows, head_count, HEAD_DIM).astype(jnp.bfloat16)
-    flat = [part.reshape(shard_rows, head_width) for part in (queries, keys_mine, values_mine)]
+    flat = project_patches(byte_embeds, global_qkv)
     context = attend_and_project(*flat, global_out).reshape(byte_count, byte_embeds.shape[1])
     context = context.astype(jnp.bfloat16)
     state = local_embeds.astype(jnp.float32) + context.astype(jnp.float32)

time: 194 us -> 162 us (0.84)
  Pallas kernels: 96 us -> 137 us
  waiting for transfers between devices: 35.6 us -> 0 us
  between operations: 14.3 us -> 0.86 us
  matrix products: 21.3 us -> 10.3 us
  local copies, waits for them, and re-layouts: 17.6 us -> 11.4 us
  other arithmetic: 8.27 us -> 2.17 us
    pallas_call x0 -> x1, Pallas kernels: none -> 39.3 us  [project_patches(): pl.pallas_call(project_kernel, name='project_patches', out_shape=[jax.Sha...]
    all_gather x1 -> x0, waiting for transfers between devices: 35.5 us -> none  [per_device(): lax.all_gather(normed, 'tp', axis=0, tiled=True)]
    dot_general x1 -> x0, matrix products: 9.86 us -> none  [per_device(): jnp.einsum('nd,cdh->nch', lax.all_gather(normed, 'tp', axis=0, tiled=True...]
    reduce_sum x6 -> x2, other arithmetic: 3.89 us -> 0.66 us  [rms_norm(): jnp.mean(values * values, axis=-1, keepdims=True) + 1e-06]
    mul x4 -> x0, local copies, waits for them, and re-layouts: 3.01 us -> none  [the longest x2 1.86 us: rms_norm(): values * lax.rsqrt(jnp.mean(values * values, axis=-1, keepdims=True) + 1e...]
    convert_element_type x2 -> x0, other arithmetic: 2.07 us -> none  [the longest x1 1.2 us: per_device(): rms_norm(projected[:, 1].reshape(shard_rows, head_count, HEAD_DIM))]
    unnamed x14, local copies, waits for them, and re-layouts: 4.43 us -> 2.42 us
  transfers between devices with their start and end apart: 1 -> 0, of which waited for: 1 -> 0; matrix products, arithmetic and copies ran while one was open for 5% -> 0% of each run, Pallas kernels for 0% -> 0%
where the time goes in v5:
time: 162 us; the launch traced here: 161 us
  Pallas kernels  137 us (85%)
  local copies, waits for them, and re-layouts  11.4 us (7%)
  matrix products  10.3 us (6%)
  other arithmetic  2.17 us (1%)
    pallas_call x1, Pallas kernels, attend_and_project(): pl.pallas_call(out_kernel, name='attend_out', out_shape=jax.ShapeDtypeStr...  49.6 us
    pallas_call x1, Pallas kernels, reduce_grads(): pl.pallas_call(grads_kernel, name='reduce_grads', out_shape=(jax.ShapeDty...  47.8 us
    pallas_call x1, Pallas kernels, project_patches(): pl.pallas_call(project_kernel, name='project_patches', out_shape=[jax.Sha...  39.3 us
    dot_general x1, local copies, waits for them, and re-layouts, local_pass(): jnp.dot(normed, local_qkv[layer], preferred_element_type=jnp.float32)  8.85 us
    dot_general x1, matrix products, local_pass(): jnp.dot(normed, local_qkv[layer], preferred_element_type=jnp.float32)  4.27 us

profile of v5, /device:TPU:1, one launch (start us, length us, event | category | flops | bytes accessed | tf_op | source)
XLA Modules:
  0.0 161.4 jit_solution(16544843654315220311)
XLA Ops:
  0.6 0.0 copy-start
  0.6 0.0 copy-start.3
  0.7 1.1 copy-done.3
  1.8 39.3 %project_patches.1 = (bf16[384,256]{1,0:T(8,128)(2,1)S(1)}, bf16[384,256]{1,0:T(8,128)(2,1)S(1)}, bf16[384,256]{1,0:T(8,128)(2,1)S(1)}) custom-call(bf16[192,1024]{1,0:T(8,128)(2,1)S(1)} %copy-done.3, bf16[3,8192,256]{2,1,0:T(8,128)(2,1)} %w_ref.2), custom_call_target="tpu_custom_call" | custom-call | tf_op jit(solution)/shard_map/project_patches/pallas_call | solution.py:455
  41.1 0.0 copy-done.1
  41.1 0.0 copy-start.4
  41.1 49.6 %attend_out.1 = f32[24,8,1024]{2,1,0:T(8,128)S(1)} custom-call(bf16[384,256]{1,0:T(8,128)(2,1)S(1)} %get-tuple-element.8.q_ref, bf16[384,256]{1,0:T(8,128)(2,1)S(1)} %get-tuple-element.9.k_ref, bf16[384,256]{1,0:T(8,128)(2,1)S(1)} %get-tuple-element.10.v_ref, bf16[256,8192]{1,0:T(8,128)(2,1)S(1)} %copy-done.1), custom_call_target="tpu_custom_call" | custom-call | tf_op jit(solution)/shard_map/attend_out/pallas_call | solution.py:747
  90.7 0.2 multiply_reduce_fusion.5
  90.9 0.1 multiply_convert_fusion.xn_ref
  91.0 8.9 %copy.21 = bf16[3072,1024]{1,0:T(8,128)(2,1)} copy(bf16[3072,1024]{0,1:T(8,128)(2,1)} %bitcast.115) | data formatting | bytes 12582912 | tf_op jit(solution)/shard_map/dot_general | solution.py:799
  99.9 4.3 %fusion.22 = f32[24,8,3,8,128]{4,1,3,2,0:T(8,128)S(1)} fusion(bf16[3,8,128,1024,1]{3,2,1,0,4:T(8,128)(2,1)} %bitcast.116, bf16[192,1024]{1,0:T(8,128)(2,1)S(1)} %multiply_convert_fusion.xn_ref), kind=kOutput, calls=%fused_computation.41 | convolution fusion | flops 1207959552 | bytes 9043968 | tf_op jit(solution)/shard_map/dot_general | solution.py:799
  104.2 0.0 copy-start.2
  104.2 0.5 multiply_reduce_fusion.4
  104.7 0.6 select_reduce_fusion
  105.4 0.0 copy-done
  105.4 0.0 copy-done.2
  105.4 0.8 fusion.20
  106.2 0.4 convolution_bitcast_fusion.2
  106.7 0.9 multiply_reduce_fusion.2
  107.6 0.4 fusion.7
  108.1 0.6 convolution_bitcast_fusion
  108.7 0.9 multiply_reduce_fusion.1
  109.6 0.1 multiply_multiply_fusion
  109.7 1.0 fusion.12
  110.6 0.2 add_convert_fusion
  110.9 0.0 copy-start.5
  110.9 0.1 copy.15
  111.0 47.8 %reduce_grads.1 = (f32[8,3072]{1,0:T(8,128)S(1)}, f32[8,1024]{1,0:T(8,128)S(1)}) custom-call(bf16[192,1024]{1,0:T(8,128)(2,1)S(1)} %multiply_convert_fusion.xn_ref, bf16[192,3072]{1,0:T(8,128)(2,1)S(1)} %bitcast.112, bf16[192,1024]{1,0:T(8,128)(2,1)S(1)} %get-tuple-element.20.ab_ref, bf16[192,1024]{1,0:T(8,128)(2,1)S(1)} %copy-done.2), custom_call_target="tpu_custom_call" | custom-call | tf_op jit(solution)/shard_map/reduce_grads/pallas_call | solution.py:243
  158.8 0.0 copy-done.5
  158.8 1.3 fusion.9
  160.1 0.6 copy.25
  160.7 0.6 copy.26
  (8 shorter events, 0.1 us)
Async XLA Ops:
  0.6 104.7 %copy-start = (bf16[1,1024,1024]{2,1,0:T(8,128)(2,1)S(1)}, bf16[1,1024,1024]{2,1,0:T(8,128)(2,1)}, u32[]{:S(2)}) copy-start(bf16[1,1024,1024]{2,1,0:T(8,128)(2,1)} %param.12) | copy-start | bytes 6291460
  0.6 1.1 copy-start.3
  1.8 39.3 %copy-start.1 = (bf16[256,8192]{1,0:T(8,128)(2,1)S(1)}, bf16[256,8192]{1,0:T(8,128)(2,1)}, u32[]{:S(2)}) copy-start(bf16[256,8192]{1,0:T(8,128)(2,1)} %w_ref.3) | copy-start | bytes 12582916
  41.1 49.6 %copy-start.4 = (bf16[192,1024]{1,0:T(8,128)(2,1)S(1)}, bf16[192,1024]{1,0:T(8,128)(2,1)}, u32[]{:S(2)}) copy-start(bf16[192,1024]{1,0:T(8,128)(2,1)} %param.8) | copy-start | bytes 1179652
  104.2 1.2 copy-start.2
  110.9 47.9 %copy-start.5 = (bf16[192,1024]{1,0:T(8,128)(2,1)S(1)}, bf16[192,1024]{1,0:T(8,128)(2,1)}, u32[]{:S(2)}) copy-start(bf16[192,1024]{1,0:T(8,128)(2,1)} %param.8) | copy-start | bytes 1179652

commit v6 on v5

--- a/solution.py
+++ b/solution.py
@@ -45,224 +45,8 @@
     )
 
 
-PART_COLS = (640, 640, 768)
-PART_ORDERS = ((0, 1, 2), (1, 2, 0), (2, 0, 1))
-
-
-def grads_kernel(
-    xn_ref, gq_ref, ab_ref, gb_ref, out_q, out_o,
-    xn2, gq2, ab2, gb2,
-    part0, part1, part2, relay0, relay1, relay2, near0, near1, near2,
-    sum0, sum1, sum2, got0, got1, got2, low0, low1, low2, last0, last1, last2,
-    fin, other, pair_send, pair_recv, send1, recv1, send2, recv2, send3, recv3,
-    fin_send, fin_recv,
-):
-    place = coords()
-    core = place[3]
-
-    def peer_along(axis, step):
-        at = list(place)
-        at[axis] = lax.rem(at[axis] + step, 4)
-        return device_at(*at)
-
-    partner = device_at(place[0], place[1], place[2], 1 - core)
-    greet([partner] + [peer_along(axis, step) for axis in range(3) for step in (1, 2, 3)])
-
-    rows = xn_ref.shape[0]
-    qh, oh = gq2.shape[1], gb2.shape[1]
-    mine_q, mine_o = pl.multiple_of(core * qh, qh), pl.multiple_of(core * oh, oh)
-    its_q, its_o = pl.multiple_of((1 - core) * qh, qh), pl.multiple_of((1 - core) * oh, oh)
-    bottom = pl.ds(rows, rows)
-    swaps = [
-        remote(xn_ref, xn2.at[bottom], pair_send.at[0], pair_recv.at[0], partner),
-        remote(gq_ref.at[:, pl.ds(its_q, qh)], gq2.at[bottom], pair_send.at[1], pair_recv.at[1], partner),
-        remote(ab_ref, ab2.at[bottom], pair_send.at[2], pair_recv.at[2], partner),
-        remote(gb_ref.at[:, pl.ds(its_o, oh)], gb2.at[bottom], pair_send.at[3], pair_recv.at[3], partner),
-    ]
-    for swap in swaps:
-        swap.start()
-    top = pl.ds(0, rows)
-    xn2[top] = xn_ref[...]
-    gq2[top] = gq_ref[:, pl.ds(mine_q, qh)]
-    ab2[top] = ab_ref[...]
-    gb2[top] = gb_ref[:, pl.ds(mine_o, oh)]
-
-    parts = (part0, part1, part2)
-    relays, nears = (relay0, relay1, relay2), (near0, near1, near2)
-    sums, gots = (sum0, sum1, sum2), (got0, got1, got2)
-    lows, lasts = (low0, low1, low2), (last0, last1, last2)
-
-    def fill(part, order, left, right, columns, into):
-        width = columns[1] - columns[0]
-        for z in range(4):
-            block = lax.dot_general(
-                left[:, z * 256 : (z + 1) * 256],
-                right[:, columns[0] : columns[1]],
-                (((0,), (0,)), ((), ())),
-                preferred_element_type=jnp.float32,
-            ).astype(jnp.bfloat16)
-            for y in range(4):
-                for x in range(4):
-                    at = (x, y, z)
-                    row = (y * 4 + x) * 16
-                    part[at[order[0]], at[order[1]], at[order[2]], :, into : into + width] = block[
-                        row : row + 16
-                    ]
-
-    first = []
-
-    def stage1(k):
-        order = PART_ORDERS[k]
-        axis = order[0]
-        me = place[axis]
-        right, left, far = lax.rem(me + 1, 4), lax.rem(me + 3, 4), lax.rem(me + 2, 4)
-        to_right, to_left = peer_along(axis, 1), peer_along(axis, 3)
-        part, relay, near = parts[k], relays[k], nears[k]
-        lo, hi = pl.ds(0, 2), pl.ds(2, 2)
-
-        def copy(n, source, target, peer):
-            return remote(source, target, send1.at[k, n], recv1.at[k, n], peer)
-
-        copies = [
-            copy(0, part.at[far, lo], relay.at[0], to_right),
-            copy(1, part.at[far, hi], relay.at[1], to_left),
-            copy(2, part.at[right, hi], near.at[0, hi], to_right),
-            copy(3, part.at[left, lo], near.at[1, lo], to_left),
-            copy(4, part.at[right, lo], near.at[0, lo], to_right),
-            copy(5, part.at[left, hi], near.at[1, hi], to_left),
-        ]
-        for n in range(4):
-            copies[n].start()
-        return copies, (right, left)
-
-    def add_relay(k, copies, sides):
-        part, relay = parts[k], relays[k]
-        for n in range(2):
-            copies[n].wait_recv()
-            for j in range(2):
-                at = 2 * n + j
-                part[sides[n], at] = (
-                    part[sides[n], at].astype(jnp.float32) + relay[n, j].astype(jnp.float32)
-                ).astype(jnp.bfloat16)
-            copies[4 + n].start()
-
-    def stage2(k, copies):
-        order = PART_ORDERS[k]
-        for n in range(2, 6):
-            copies[n].wait_recv()
-        me = place[order[0]]
-        for j in range(4):
-            sums[k][j] = (
-                parts[k][me, j].astype(jnp.float32)
-                + nears[k][0, j].astype(jnp.float32)
-                + nears[k][1, j].astype(jnp.float32)
-            ).astype(jnp.bfloat16)
-        axis = order[1]
-        at = place[axis]
-        sends = []
-        for d in range(1, 4):
-            send = remote(
-                sums[k].at[lax.rem(at + d, 4)], gots[k].at[d - 1],
-                send2.at[k, d - 1], recv2.at[k, d - 1], peer_along(axis, d),
-            )
-            send.start()
-            sends.append(send)
-        return sends
-
-    def stage3(k, copies):
-        order = PART_ORDERS[k]
-        for copy in copies:
-            copy.wait_recv()
-        me = place[order[1]]
-        total = sums[k][me].astype(jnp.float32)
-        for d in range(3):
-            total = total + gots[k][d].astype(jnp.float32)
-        lows[k][...] = total.astype(jnp.bfloat16)
-        axis = order[2]
-        at = place[axis]
-        sends = []
-        for d in range(1, 4):
-            send = remote(
-                lows[k].at[lax.rem(at + d, 4)], lasts[k].at[d - 1],
-                send3.at[k, d - 1], recv3.at[k, d - 1], peer_along(axis, d),
-            )
-            send.start()
-            sends.append(send)
-        return sends
-
-    def finish(k, copies):
-        for copy in copies:
-            copy.wait_recv()
-        me = place[PART_ORDERS[k][2]]
-        total = lows[k][me].astype(jnp.float32)
-        for d in range(3):
-            total = total + lasts[k][d].astype(jnp.float32)
-        start = sum(PART_COLS[:k])
-        fin[:, start : start + PART_COLS[k]] = total
-
-    swaps[0].wait_recv()
-    swaps[1].wait_recv()
-    split = PART_COLS[0] + PART_COLS[1]
-    fill(part0, PART_ORDERS[0], xn2, gq2, (0, PART_COLS[0]), 0)
-    first.append(stage1(0))
-    fill(part1, PART_ORDERS[1], xn2, gq2, (PART_COLS[0], split), 0)
-    first.append(stage1(1))
-    swaps[2].wait_recv()
-    swaps[3].wait_recv()
-    fill(part2, PART_ORDERS[2], xn2, gq2, (split, qh), 0)
-    fill(part2, PART_ORDERS[2], ab2, gb2, (0, oh), qh - split)
-    first.append(stage1(2))
-    for k in range(3):
-        add_relay(k, *first[k])
-    second = [stage2(k, first[k][0]) for k in range(3)]
-    third = [stage3(k, second[k]) for k in range(3)]
-    for k in range(3):
-        finish(k, third[k])
-
-    keep, give = pl.multiple_of(core * 8, 8), pl.multiple_of((1 - core) * 8, 8)
-    end = remote(fin.at[pl.ds(give, 8)], other, fin_send, fin_recv, partner)
-    end.start()
-    out_q[:, pl.ds(mine_q, qh)] = fin[pl.ds(keep, 8), 0:qh]
-    out_o[:, pl.ds(mine_o, oh)] = fin[pl.ds(keep, 8), qh : qh + oh]
-    end.wait_recv()
-    out_q[:, pl.ds(its_q, qh)] = other[:, 0:qh]
-    out_o[:, pl.ds(its_o, oh)] = other[:, qh : qh + oh]
-    for copy in swaps + [c for f in first for c in f[0]] + [c for s in second + third for c in s] + [end]:
-        copy.wait_send()
-
-
-def reduce_grads(xn, gq, ab, gb):
-    rows, width = xn.shape
-    qw, ow = gq.shape[1], gb.shape[1]
-    bf, f32 = jnp.bfloat16, jnp.float32
-    vmem = pl.BlockSpec(memory_space=pltpu.VMEM)
-
-    def each(*lead):
-        return [pltpu.VMEM((*lead, 16, c), bf) for c in PART_COLS]
-
-    return pl.pallas_call(
-        grads_kernel,
-        name="reduce_grads",
-        out_shape=(jax.ShapeDtypeStruct((8, qw), f32), jax.ShapeDtypeStruct((8, ow), f32)),
-        in_specs=[vmem] * 4,
-        out_specs=(vmem, vmem),
-        scratch_shapes=[
-            pltpu.VMEM((2 * rows, width), bf),
-            pltpu.VMEM((2 * rows, qw // 2), bf),
-            pltpu.VMEM((2 * rows, width), bf),
-            pltpu.VMEM((2 * rows, ow // 2), bf),
-            *each(4, 4, 4), *each(2, 2, 4), *each(2, 4, 4),
-            *each(4, 4), *each(3, 4), *each(4), *each(3),
-            pltpu.VMEM((16, (qw + ow) // 2), f32),
-            pltpu.VMEM((8, (qw + ow) // 2), f32),
-            pltpu.SemaphoreType.DMA((4,)), pltpu.SemaphoreType.DMA((4,)),
-            pltpu.SemaphoreType.DMA((3, 6)), pltpu.SemaphoreType.DMA((3, 6)),
-            pltpu.SemaphoreType.DMA((3, 3)), pltpu.SemaphoreType.DMA((3, 3)),
-            pltpu.SemaphoreType.DMA((3, 3)), pltpu.SemaphoreType.DMA((3, 3)),
-            pltpu.SemaphoreType.DMA, pltpu.SemaphoreType.DMA,
-        ],
-        compiler_params=pltpu.CompilerParams(collective_id=5, has_side_effects=True, vmem_limit_bytes=48 << 20),
-    )(xn, gq, ab, gb)
+def rms_norm(values):
+    return values * lax.rsqrt(jnp.mean(values * values, axis=-1, keepdims=True) + 1e-06)
 
 
 CHUNK = 512
@@ -773,52 +557,309 @@
     )(q, k, v, w)
 
 
-def rms_norm(values):
-    return values * lax.rsqrt(jnp.mean(values * values, axis=-1, keepdims=True) + 1e-06)
-
-
-def local_core(qkv_rows):
-    total = qkv_rows.shape[0]
-    groups = total // PATCH
-    width = qkv_rows.shape[1] // 3
-    parts = qkv_rows.reshape(groups, PATCH, 3, LOCAL_HEADS, LOCAL_HEAD_DIM)
-    queries = rms_norm(parts[:, :, 0])
-    keys_all = rms_norm(parts[:, :, 1])
-    values = parts[:, :, 2]
-    scores = jnp.einsum("npha,nqha->nhpq", queries, keys_all) / math.sqrt(LOCAL_HEAD_DIM)
-    causal = jnp.arange(PATCH)[:, None] >= jnp.arange(PATCH)[None, :]
-    weights = jnp.where(causal[None, None], jnp.exp(scores), 0.0)
-    numerator = jnp.einsum("nhpq,nqha->npha", weights, values)
-    denominator = jnp.sum(weights, axis=-1).transpose(0, 2, 1)[..., None]
-    return (numerator / denominator).reshape(total, width)
-
-
-def local_pass(state, local_qkv, local_out, cotangent):
-    layer = 0
-    normed = rms_norm(state).astype(jnp.bfloat16)
-    qkv_rows = jnp.dot(normed, local_qkv[layer], preferred_element_type=jnp.float32)
-    core, core_back = jax.vjp(local_core, qkv_rows)
-    attended = core.astype(jnp.bfloat16)
-    saved = [(state, normed, core_back, attended)]
-    state = state + jnp.dot(attended, local_out[layer], preferred_element_type=jnp.float32)
-    hidden = state.astype(jnp.bfloat16)
-    grad_state = cotangent.astype(jnp.float32)
-    layer = 0
-    before, normed, core_back, attended = saved[layer]
-    grad_round = grad_state.astype(jnp.bfloat16)
-    grad_core = jnp.dot(grad_round, local_out[layer].T, preferred_element_type=jnp.float32)
-    grad_rows = core_back(grad_core)[0].astype(jnp.bfloat16)
-    return hidden, normed, grad_rows, attended, grad_round
+PART_COLS = (640, 640, 768)
+PART_ORDERS = ((0, 1, 2), (1, 2, 0), (2, 0, 1))
+
+
+def rms_scale(values):
+    return lax.rsqrt(jnp.mean(values * values, axis=-1, keepdims=True) + 1e-06)
+
+
+def cross(left, right, left_axis, right_axis):
+    return lax.dot_general(
+        left, right, (((left_axis,), (right_axis,)), ((), ())), preferred_element_type=jnp.float32
+    )
+
+
+SPAN = 96
+
+
+def local_head(h, first, inside, qkv, gcore, gq, ab):
+    rows = slice(first, first + SPAN)
+    bf = jnp.bfloat16
+    width = gcore.shape[1]
+    at = [pl.ds(pl.multiple_of(n * width + h * LOCAL_HEAD_DIM, LOCAL_HEAD_DIM), LOCAL_HEAD_DIM) for n in range(3)]
+    q, k, v = (qkv[rows, part] for part in at)
+    q_scale, k_scale = rms_scale(q), rms_scale(k)
+    qn, kn = q * q_scale, k * k_scale
+    qb, kb, vb = qn.astype(bf), kn.astype(bf), v.astype(bf)
+    scale = 1.0 / math.sqrt(LOCAL_HEAD_DIM)
+    e = jnp.where(inside, jnp.exp(cross(qb, kb, 1, 1) * scale), 0.0)
+    p = e / jnp.sum(e, axis=-1, keepdims=True)
+    pb = p.astype(bf)
+    ab[rows, at[0]] = cross(pb, vb, 1, 0).astype(bf)
+    back = gcore[rows, at[0]].astype(bf)
+    dp = cross(back, vb, 1, 1)
+    ds = (p * (dp - jnp.sum(p * dp, axis=-1, keepdims=True)) * scale).astype(bf)
+
+    def through_rms(grad, normed, factor):
+        return (factor * (grad - normed * jnp.mean(grad * normed, axis=-1, keepdims=True))).astype(bf)
+
+    gq[rows, at[0]] = through_rms(cross(ds, kb, 1, 0), qn, q_scale)
+    gq[rows, at[1]] = through_rms(cross(ds, qb, 0, 0), kn, k_scale)
+    gq[rows, at[2]] = cross(pb, back, 0, 0).astype(bf)
+
+
+def grads_kernel(
+    emb_ref, ctx_ref, wqkv_ref, wout_ref, gb_ref, hid_ref, out_q, out_o,
+    state, qkv, gcore, gq, xt, abt, xn2, gq2, ab2, gb2,
+    part0, part1, part2, relay0, relay1, relay2, near0, near1, near2,
+    sum0, sum1, sum2, got0, got1, got2, low0, low1, low2, last0, last1, last2,
+    fin, other, pair_send, pair_recv, send1, recv1, send2, recv2, send3, recv3,
+    fin_send, fin_recv,
+):
+    place = coords()
+    core = place[3]
+
+    def peer_along(axis, step):
+        at = list(place)
+        at[axis] = lax.rem(at[axis] + step, 4)
+        return device_at(*at)
+
+    partner = device_at(place[0], place[1], place[2], 1 - core)
+    greet([partner] + [peer_along(axis, step) for axis in range(3) for step in (1, 2, 3)])
+
+    rows, width = emb_ref.shape
+    qh, oh = gq2.shape[1], gb2.shape[1]
+    mine_q, mine_o = pl.multiple_of(core * qh, qh), pl.multiple_of(core * oh, oh)
+    its_q, its_o = pl.multiple_of((1 - core) * qh, qh), pl.multiple_of((1 - core) * oh, oh)
+    top, bottom = pl.ds(0, rows), pl.ds(rows, rows)
+    swaps = [
+        remote(xn2.at[top], xn2.at[bottom], pair_send.at[0], pair_recv.at[0], partner),
+        remote(gq.at[:, pl.ds(its_q, qh)], gq2.at[bottom], pair_send.at[1], pair_recv.at[1], partner),
+        remote(ab2.at[top], ab2.at[bottom], pair_send.at[2], pair_recv.at[2], partner),
+        remote(gb_ref.at[:, pl.ds(its_o, oh)], gb2.at[bottom], pair_send.at[3], pair_recv.at[3], partner),
+    ]
+    swaps[3].start()
+    state[...] = emb_ref[...].astype(jnp.float32) + ctx_ref[...].astype(jnp.bfloat16).astype(jnp.float32)
+    normed = (state[...] * rms_scale(state[...])).astype(jnp.bfloat16)
+    xn2[top] = normed
+    swaps[0].start()
+    gb2[top] = gb_ref[:, pl.ds(mine_o, oh)]
+
+    def project(n, carry):
+        at = pl.ds(pl.multiple_of(n * 512, 512), 512)
+        qkv[:, at] = jnp.dot(xn2[top], wqkv_ref[:, at], preferred_element_type=jnp.float32)
+        return carry
+
+    lax.fori_loop(0, 3 * width // 512, project, 0)
+    for n in range(2):
+        at = slice(n * width // 2, (n + 1) * width // 2)
+        gcore[:, at] = cross(gb_ref[...], wout_ref[at], 1, 1)
+    row = lax.broadcasted_iota(jnp.int32, (SPAN, SPAN), 0)
+    column = lax.broadcasted_iota(jnp.int32, (SPAN, SPAN), 1)
+    inside = (column <= row) & (column >= row - lax.rem(row, PATCH))
+
+    def heads(n, carry):
+        for h in (2 * n, 2 * n + 1):
+            for first in range(0, rows, SPAN):
+                local_head(h, first, inside, qkv, gcore, gq, ab2)
+        return carry
+
+    lax.fori_loop(0, LOCAL_HEADS // 2, heads, 0)
+    swaps[1].start()
+    swaps[2].start()
+    gq2[top] = gq[:, pl.ds(mine_q, qh)]
+    xt[0] = xn2[top].T
+    swaps[0].wait_recv()
+    xt[1] = xn2[bottom].T
+
+    parts = (part0, part1, part2)
+    relays, nears = (relay0, relay1, relay2), (near0, near1, near2)
+    sums, gots = (sum0, sum1, sum2), (got0, got1, got2)
+    lows, lasts = (low0, low1, low2), (last0, last1, last2)
+
+    def fill(part, order, left, right, columns, into):
+        span = slice(*columns)
+        for z in range(4):
+            at = slice(z * 256, (z + 1) * 256)
+            block = (
+                jnp.dot(left[0, at], right[top, span], preferred_element_type=jnp.float32)
+                + jnp.dot(left[1, at], right[bottom, span], preferred_element_type=jnp.float32)
+            ).astype(jnp.bfloat16)
+            for y in range(4):
+                for x in range(4):
+                    at = (x, y, z)
+                    row = (y * 4 + x) * 16
+                    part[
+                        at[order[0]], at[order[1]], at[order[2]], :, into : into + columns[1] - columns[0]
+                    ] = block[row : row + 16]
+
+    first = []
+
+    def stage1(k):
+        order = PART_ORDERS[k]
+        axis = order[0]
+        me = place[axis]
+        right, left, far = lax.rem(me + 1, 4), lax.rem(me + 3, 4), lax.rem(me + 2, 4)
+        to_right, to_left = peer_along(axis, 1), peer_along(axis, 3)
+        part, relay, near = parts[k], relays[k], nears[k]
+        lo, hi = pl.ds(0, 2), pl.ds(2, 2)
+
+        def copy(n, source, target, peer):
+            return remote(source, target, send1.at[k, n], recv1.at[k, n], peer)
+
+        copies = [
+            copy(0, part.at[far, lo], relay.at[0], to_right),
+            copy(1, part.at[far, hi], relay.at[1], to_left),
+            copy(2, part.at[right, hi], near.at[0, hi], to_right),
+            copy(3, part.at[left, lo], near.at[1, lo], to_left),
+            copy(4, part.at[right, lo], near.at[0, lo], to_right),
+            copy(5, part.at[left, hi], near.at[1, hi], to_left),
+        ]
+        for n in range(4):
+            copies[n].start()
+        return copies, (right, left)
+
+    def add_relay(k, copies, sides):
+        part, relay = parts[k], relays[k]
+        for n in range(2):
+            copies[n].wait_recv()
+            for j in range(2):
+                at = 2 * n + j
+                part[sides[n], at] = (
+                    part[sides[n], at].astype(jnp.float32) + relay[n, j].astype(jnp.float32)
+                ).astype(jnp.bfloat16)
+            copies[4 + n].start()
+
+    def stage2(k, copies):
+        order = PART_ORDERS[k]
+        for n in range(2, 6):
+            copies[n].wait_recv()
+        me = place[order[0]]
+        for j in range(4):
+            sums[k][j] = (
+                parts[k][me, j].astype(jnp.float32)
+                + nears[k][0, j].astype(jnp.float32)
+                + nears[k][1, j].astype(jnp.float32)
+            ).astype(jnp.bfloat16)
+        axis = order[1]
+        at = place[axis]
+        sends = []
+        for d in range(1, 4):
+            send = remote(
+                sums[k].at[lax.rem(at + d, 4)], gots[k].at[d - 1],
+                send2.at[k, d - 1], recv2.at[k, d - 1], peer_along(axis, d),
+            )
+            send.start()
+            sends.append(send)
+        return sends
+
+    def stage3(k, copies):
+        order = PART_ORDERS[k]
+        for copy in copies:
+            copy.wait_recv()
+        me = place[order[1]]
+        total = sums[k][me].astype(jnp.float32)
+        for d in range(3):
+            total = total + gots[k][d].astype(jnp.float32)
+        lows[k][...] = total.astype(jnp.bfloat16)
+        axis = order[2]
+        at = place[axis]
+        sends = []
+        for d in range(1, 4):
+            send = remote(
+                lows[k].at[lax.rem(at + d, 4)], lasts[k].at[d - 1],
+                send3.at[k, d - 1], recv3.at[k, d - 1], peer_along(axis, d),
+            )
+            send.start()
+            sends.append(send)
+        return sends
+
+    def finish(k, copies):
+        for copy in copies:
+            copy.wait_recv()
+        me = place[PART_ORDERS[k][2]]
+        total = lows[k][me].astype(jnp.float32)
+        for d in range(3):
+            total = total + lasts[k][d].astype(jnp.float32)
+        start = sum(PART_COLS[:k])
+        fin[:, start : start + PART_COLS[k]] = total
+
+    swaps[1].wait_recv()
+    split = PART_COLS[0] + PART_COLS[1]
+    fill(part0, PART_ORDERS[0], xt, gq2, (0, PART_COLS[0]), 0)
+    first.append(stage1(0))
+    fill(part1, PART_ORDERS[1], xt, gq2, (PART_COLS[0], split), 0)
+    first.append(stage1(1))
+    fill(part2, PART_ORDERS[2], xt, gq2, (split, qh), 0)
+    abt[0] = ab2[top].T
+    swaps[2].wait_recv()
+    abt[1] = ab2[bottom].T
+    swaps[3].wait_recv()
+    fill(part2, PART_ORDERS[2], abt, gb2, (0, oh), qh - split)
+    first.append(stage1(2))
+    add_relay(0, *first[0])
+    add_relay(1, *first[1])
+    hid_ref[...] = (
+        state[...] + jnp.dot(ab2[top], wout_ref[...], preferred_element_type=jnp.float32)
+    ).astype(jnp.bfloat16)
+    add_relay(2, *first[2])
+    second = [stage2(k, first[k][0]) for k in range(3)]
+    third = [stage3(k, second[k]) for k in range(3)]
+    for k in range(3):
+        finish(k, third[k])
+
+    keep, give = pl.multiple_of(core * 8, 8), pl.multiple_of((1 - core) * 8, 8)
+    end = remote(fin.at[pl.ds(give, 8)], other, fin_send, fin_recv, partner)
+    end.start()
+    out_q[:, pl.ds(mine_q, qh)] = fin[pl.ds(keep, 8), 0:qh]
+    out_o[:, pl.ds(mine_o, oh)] = fin[pl.ds(keep, 8), qh : qh + oh]
+    end.wait_recv()
+    out_q[:, pl.ds(its_q, qh)] = other[:, 0:qh]
+    out_o[:, pl.ds(its_o, oh)] = other[:, qh : qh + oh]
+    for copy in swaps + [c for f in first for c in f[0]] + [c for s in second + third for c in s] + [end]:
+        copy.wait_send()
+
+
+def local_window(emb, context, w_qkv, w_out, cotangent):
+    rows, width = emb.shape
+    qw, ow = w_qkv.shape[1], w_out.shape[1]
+    bf, f32 = jnp.bfloat16, jnp.float32
+    vmem = pl.BlockSpec(memory_space=pltpu.VMEM)
+
+    def each(*lead):
+        return [pltpu.VMEM((*lead, 16, c), bf) for c in PART_COLS]
+
+    def sems(*shape):
+        return pltpu.SemaphoreType.DMA(shape)
+
+    return pl.pallas_call(
+        grads_kernel,
+        name="local_window",
+        out_shape=(
+            jax.ShapeDtypeStruct((rows, width), bf),
+            jax.ShapeDtypeStruct((8, qw), f32),
+            jax.ShapeDtypeStruct((8, ow), f32),
+        ),
+        in_specs=[vmem] * 5,
+        out_specs=(vmem,) * 3,
+        scratch_shapes=[
+            pltpu.VMEM((rows, width), f32),
+            pltpu.VMEM((rows, qw), f32),
+            pltpu.VMEM((rows, width), f32),
+            pltpu.VMEM((rows, qw), bf),
+            pltpu.VMEM((2, width, rows), bf),
+            pltpu.VMEM((2, width, rows), bf),
+            pltpu.VMEM((2 * rows, width), bf),
+            pltpu.VMEM((2 * rows, qw // 2), bf),
+            pltpu.VMEM((2 * rows, width), bf),
+            pltpu.VMEM((2 * rows, ow // 2), bf),
+            *each(4, 4, 4), *each(2, 2, 4), *each(2, 4, 4),
+            *each(4, 4), *each(3, 4), *each(4), *each(3),
+            pltpu.VMEM((16, (qw + ow) // 2), f32),
+            pltpu.VMEM((8, (qw + ow) // 2), f32),
+            sems(4), sems(4), sems(3, 6), sems(3, 6), sems(3, 3), sems(3, 3), sems(3, 3), sems(3, 3),
+            pltpu.SemaphoreType.DMA, pltpu.SemaphoreType.DMA,
+        ],
+        compiler_params=pltpu.CompilerParams(collective_id=5, has_side_effects=True, vmem_limit_bytes=44 << 20),
+    )(emb, context, w_qkv, w_out, cotangent)
 
 
 def per_device(byte_embeds, local_embeds, global_qkv, global_out, local_qkv, local_out, cotangent):
-    byte_count = byte_embeds.shape[0]
     flat = project_patches(byte_embeds, global_qkv)
-    context = attend_and_project(*flat, global_out).reshape(byte_count, byte_embeds.shape[1])
-    context = context.astype(jnp.bfloat16)
-    state = local_embeds.astype(jnp.float32) + context.astype(jnp.float32)
-    hidden, *factors = local_pass(state, local_qkv, local_out, cotangent)
-    grad_qkv, grad_out = reduce_grads(*factors)
+    context = attend_and_project(*flat, global_out).reshape(local_embeds.shape)
+    hidden, grad_qkv, grad_out = local_window(local_embeds, context, local_qkv[0], local_out[0], cotangent)
     return (hidden, grad_qkv[None], grad_out[None])
 
 

time: 162 us -> 157 us (0.969)
  Pallas kernels: 137 us -> 153 us
  matrix products: 10.3 us -> 0 us
  local copies, waits for them, and re-layouts: 11.4 us -> 3.01 us
  other arithmetic: 2.17 us -> 0 us
    pallas_call x1, Pallas kernels: 47.8 us -> 63.7 us  [local_window(): pl.pallas_call(grads_kernel, name='local_window', out_shape=(jax.ShapeDty...]
    dot_general x9 -> x0, matrix products: 10.3 us -> none  [the longest x1 4.27 us: local_pass(): jnp.dot(normed, local_qkv[layer], preferred_element_type=jnp.float32)]
    dot_general x1 -> x0, local copies, waits for them, and re-layouts: 8.85 us -> none  [local_pass(): jnp.dot(normed, local_qkv[layer], preferred_element_type=jnp.float32)]
where the time goes in v6:
time: 157 us; the launch traced here: 156 us
  Pallas kernels  153 us (97%)
  local copies, waits for them, and re-layouts  3.01 us (2%)
    pallas_call x1, Pallas kernels, local_window(): pl.pallas_call(grads_kernel, name='local_window', out_shape=(jax.ShapeDty...  63.7 us
    pallas_call x1, Pallas kernels, attend_and_project(): pl.pallas_call(out_kernel, name='attend_out', out_shape=jax.ShapeDtypeStr...  49.7 us
    pallas_call x1, Pallas kernels, project_patches(): pl.pallas_call(project_kernel, name='project_patches', out_shape=[jax.Sha...  39.4 us

profile of v6, /device:TPU:1, one launch (start us, length us, event | category | flops | bytes accessed | tf_op | source)
XLA Modules:
  0.0 156.4 jit_solution(17960391213756239379)
XLA Ops:
  0.6 0.0 copy-start.2
  0.6 1.0 copy-done.2
  1.6 0.0 copy-start
  1.6 0.0 copy-start.1
  1.6 0.0 copy-start.3
  1.6 0.0 copy-start.4
  1.6 39.4 %project_patches.1 = (bf16[384,256]{1,0:T(8,128)(2,1)S(1)}, bf16[384,256]{1,0:T(8,128)(2,1)S(1)}, bf16[384,256]{1,0:T(8,128)(2,1)S(1)}) custom-call(bf16[192,1024]{1,0:T(8,128)(2,1)S(1)} %copy-done.2, bf16[3,8192,256]{2,1,0:T(8,128)(2,1)} %w_ref.2), custom_call_target="tpu_custom_call" | custom-call | tf_op jit(solution)/shard_map/project_patches/pallas_call | solution.py:239
  41.0 0.0 copy-done
  41.0 49.7 %attend_out.1 = f32[24,8,1024]{2,1,0:T(8,128)S(1)} custom-call(bf16[384,256]{1,0:T(8,128)(2,1)S(1)} %get-tuple-element.9.q_ref, bf16[384,256]{1,0:T(8,128)(2,1)S(1)} %get-tuple-element.10.k_ref, bf16[384,256]{1,0:T(8,128)(2,1)S(1)} %get-tuple-element.11.v_ref, bf16[256,8192]{1,0:T(8,128)(2,1)S(1)} %copy-done), custom_call_target="tpu_custom_call" | custom-call | tf_op jit(solution)/shard_map/attend_out/pallas_call | solution.py:531
  90.7 0.0 copy-done.1
  90.7 0.0 copy-done.3
  90.7 0.0 copy-done.4
  90.7 63.7 %local_window.1 = (bf16[192,1024]{1,0:T(8,128)(2,1)S(1)}, f32[8,3072]{1,0:T(8,128)S(1)}, f32[8,1024]{1,0:T(8,128)S(1)}) custom-call(bf16[192,1024]{1,0:T(8,128)(2,1)S(1)} %copy-done.3, f32[192,1024]{1,0:T(8,128)S(1)} %bitcast.5, bf16[1024,3072]{1,0:T(8,128)(2,1)} %bitcast.9, bf16[1024,1024]{1,0:T(8,128)(2,1)S(1)} %bitcast.6, bf16[192,1024]{1,0:T(8,128)(2,1)S(1)} %copy-done.4), custom_call_target="tpu_custom_call" | custom-call | tf_op jit(solution)/shard_map/local_window/pallas_call | solution.py:827
  154.4 0.7 copy.13
  155.2 0.6 copy.14
  155.8 0.6 copy.15
Async XLA Ops:
  0.6 1.0 copy-start.2
  1.6 39.4 %copy-start = (bf16[256,8192]{1,0:T(8,128)(2,1)S(1)}, bf16[256,8192]{1,0:T(8,128)(2,1)}, u32[]{:S(2)}) copy-start(bf16[256,8192]{1,0:T(8,128)(2,1)} %w_ref.3) | copy-start | bytes 12582916
  1.6 89.1 %copy-start.1 = (bf16[1,1024,1024]{2,1,0:T(8,128)(2,1)S(1)}, bf16[1,1024,1024]{2,1,0:T(8,128)(2,1)}, u32[]{:S(2)}) copy-start(bf16[1,1024,1024]{2,1,0:T(8,128)(2,1)} %param.12) | copy-start | bytes 6291460
  1.6 89.1 %copy-start.3 = (bf16[192,1024]{1,0:T(8,128)(2,1)S(1)}, bf16[192,1024]{1,0:T(8,128)(2,1)}, u32[]{:S(2)}) copy-start(bf16[192,1024]{1,0:T(8,128)(2,1)} %emb_ref.1) | copy-start | bytes 1179652
  1.6 89.1 %copy-start.4 = (bf16[192,1024]{1,0:T(8,128)(2,1)S(1)}, bf16[192,1024]{1,0:T(8,128)(2,1)}, u32[]{:S(2)}) copy-start(bf16[192,1024]{1,0:T(8,128)(2,1)} %gb_ref.1) | copy-start | bytes 1179652

commit v7 on v6

--- a/solution.py
+++ b/solution.py
@@ -273,27 +273,61 @@
         )
     ]
 
-    def up(d, kind, which):
-        block = half if which == 0 else 1 - half
-        target = (ka, va)[kind].at[z, block]
-        source = (k_ref, v_ref)[kind].at[:, mine] if which == 0 else target
-        return remote(
-            source, target, z_send.at[d - 1, kind, which], z_recv.at[d - 1, kind, which],
-            device_at(x, y, lax.rem(z + d, 4), core),
-        )
-
-    lifts = {(d, kind, which): up(d, kind, which) for which in (0, 1) for kind in (0, 1) for d in (1, 3, 2)}
-    for (d, kind, which), copy in lifts.items():
-        if which == 0:
-            pl.when(z + d <= 3)(copy.start)
+    above, below = device_at(x, y, lax.rem(z + 1, 4), core), device_at(x, y, lax.rem(z + 3, 4), core)
+    stores = (ka, va)
+    jobs = []
+
+    def piece(owner, kind, which):
+        return stores[kind].at[owner, half if which == 0 else 1 - half]
+
+    def job(slot, kind, which, owner, peer, sends, fresh):
+        target = piece(owner, kind, which)
+        source = (k_ref, v_ref)[kind].at[:, mine] if fresh and which == 0 else target
+        made = remote(source, target, z_send.at[slot, kind, which], z_recv.at[slot, kind, which], peer)
+        jobs.append((sends, made))
+        return made
+
+    direct, wrap, transit, relay_k, relay_v = {}, {}, {}, {}, {}
+    for which in (0, 1):
+        for kind in (0, 1):
+            direct[kind, which] = job(0, kind, which, z, above, z < 3, True)
+            wrap[kind, which] = job(1, kind, which, z, below, z == 0, True)
+        transit[which] = job(3, 1, which, z, below, z == 1, True)
+        relay_k[which] = job(2, 0, which, lax.rem(z + 3, 4), above, (z == 1) | (z == 2), False)
+        relay_v[which] = job(2, 1, which, 1 - lax.div(z, 3), below, (z == 0) | (z == 3), False)
+
+    def send_fresh(kind, which):
+        pl.when(z < 3)(direct[kind, which].start)
+        pl.when(z == 0)(wrap[kind, which].start)
+        if kind == 1:
+            pl.when(z == 1)(transit[which].start)
+
+    def send_on(which):
+        @pl.when((z == 1) | (z == 2))
+        def _():
+            direct[0, which].wait_recv()
+            relay_k[which].start()
+
+        @pl.when(z == 3)
+        def _():
+            wrap[1, which].wait_recv()
+            relay_v[which].start()
+
+        @pl.when(z == 0)
+        def _():
+            transit[which].wait_recv()
+            relay_v[which].start()
+
+    send_fresh(0, 0)
+    send_fresh(1, 0)
     ka[z, half] = k_ref[:, mine]
     va[z, half] = v_ref[:, mine]
     q2[half] = q_ref[:, mine]
     for kind in (0, 1):
         across[kind].wait_recv()
-        for d in (1, 3, 2):
-            pl.when(z + d <= 3)(lifts[d, kind, 1].start)
+        send_fresh(kind, 1)
     across[2].wait_recv()
+    send_on(0)
 
     tile = 128
     tiles = rows // tile
@@ -320,23 +354,37 @@
             for n in range(tiles):
                 attend_tile(block, n, keys, values, block == k, k == 0)
 
-    for d in (1, 3, 2):
-
-        @pl.when(z >= d)
-        def _():
-            for kind in (0, 1):
-                for which in (0, 1):
-                    lifts[d, kind, which].wait_recv()
-            below = lax.rem(z + 4 - d, 4)
-
-            def body(k, carry):
-                keys, values = ka[below, k], with_ones(va[below, k])
-                for block in (0, 1):
-                    for n in range(tiles):
-                        attend_tile(block, n, keys, values, False, False)
-                return carry
-
-            lax.fori_loop(0, 2, body, 0)
+    send_on(1)
+
+    def attend_all(owner):
+        def body(k, carry):
+            keys, values = ka[owner, k], with_ones(va[owner, k])
+            for block in (0, 1):
+                for n in range(tiles):
+                    attend_tile(block, n, keys, values, False, False)
+            return carry
+
+        lax.fori_loop(0, 2, body, 0)
+
+    @pl.when(z == 3)
+    def _():
+        for which in (0, 1):
+            wrap[0, which].wait_recv()
+        attend_all(0)
+
+    @pl.when(z >= 1)
+    def _():
+        for which in (0, 1):
+            pl.when(z == 3)(direct[0, which].wait_recv)
+            direct[1, which].wait_recv()
+        attend_all(z - 1)
+
+    @pl.when(z >= 2)
+    def _():
+        for which in (0, 1):
+            relay_k[which].wait_recv()
+            relay_v[which].wait_recv()
+        attend_all(z - 2)
 
     for block in (0, 1):
         tall[8 + block * rows : 8 + (block + 1) * rows] = acc[block, :, 0:HEAD_DIM] / acc[block, :, HEAD_DIM:]
@@ -370,8 +418,8 @@
     near.wait_recv()
     last.wait_recv()
     pl.when(z < 3)(row.wait_send)
-    for (d, kind, which), copy in lifts.items():
-        pl.when(z + d <= 3)(copy.wait_send)
+    for sends, copy in jobs:
+        pl.when(sends)(copy.wait_send)
 
 
 def out_kernel(
@@ -549,7 +597,7 @@
             pltpu.VMEM((24, LANES), f32),
             sems(8), sems(8), sems(8), sems(4, 7), sems(4, 7), sems(4, 4), sems(4, 4),
             pltpu.SemaphoreType.DMA, pltpu.SemaphoreType.DMA,
-            sems(3), sems(3), sems(3, 2, 2), sems(3, 2, 2),
+            sems(3), sems(3), sems(4, 2, 2), sems(4, 2, 2),
             pltpu.SemaphoreType.DMA, pltpu.SemaphoreType.DMA,
             pltpu.SemaphoreType.DMA, pltpu.SemaphoreType.DMA, sems(2), sems(2),
         ],
@@ -651,12 +699,13 @@
     inside = (column <= row) & (column >= row - lax.rem(row, PATCH))
 
     def heads(n, carry):
-        for h in (2 * n, 2 * n + 1):
+        for i in range(8):
+            h = 8 * n + i
             for first in range(0, rows, SPAN):
                 local_head(h, first, inside, qkv, gcore, gq, ab2)
         return carry
 
-    lax.fori_loop(0, LOCAL_HEADS // 2, heads, 0)
+    lax.fori_loop(0, LOCAL_HEADS // 8, heads, 0)
     swaps[1].start()
     swaps[2].start()
     gq2[top] = gq[:, pl.ds(mine_q, qh)]

time: 157 us -> 152 us (0.968)
  Pallas kernels: 153 us -> 148 us
    pallas_call x1, Pallas kernels: 63.7 us -> 60.8 us  [local_window(): pl.pallas_call(grads_kernel, name='local_window', out_shape=(jax.ShapeDty...]
    pallas_call x1, Pallas kernels: 49.7 us -> 47.6 us  [attend_and_project(): pl.pallas_call(out_kernel, name='attend_out', out_shape=jax.ShapeDtypeStr...]
where the time goes in v7:
time: 152 us; the launch traced here: 151 us
  Pallas kernels  148 us (97%)
  local copies, waits for them, and re-layouts  3.01 us (2%)
    pallas_call x1, Pallas kernels, local_window(): pl.pallas_call(grads_kernel, name='local_window', out_shape=(jax.ShapeDty...  60.8 us
    pallas_call x1, Pallas kernels, attend_and_project(): pl.pallas_call(out_kernel, name='attend_out', out_shape=jax.ShapeDtypeStr...  47.6 us
    pallas_call x1, Pallas kernels, project_patches(): pl.pallas_call(project_kernel, name='project_patches', out_shape=[jax.Sha...  39.4 us

profile of v7, /device:TPU:1, one launch (start us, length us, event | category | flops | bytes accessed | tf_op | source)
XLA Modules:
  0.0 151.4 jit_solution(8205431510477921956)
XLA Ops:
  0.6 0.0 copy-start.2
  0.6 1.0 copy-done.2
  1.6 0.0 copy-start
  1.6 0.0 copy-start.1
  1.6 0.0 copy-start.3
  1.6 0.0 copy-start.4
  1.6 39.4 %project_patches.1 = (bf16[384,256]{1,0:T(8,128)(2,1)S(1)}, bf16[384,256]{1,0:T(8,128)(2,1)S(1)}, bf16[384,256]{1,0:T(8,128)(2,1)S(1)}) custom-call(bf16[192,1024]{1,0:T(8,128)(2,1)S(1)} %copy-done.2, bf16[3,8192,256]{2,1,0:T(8,128)(2,1)} %w_ref.2), custom_call_target="tpu_custom_call" | custom-call | tf_op jit(solution)/shard_map/project_patches/pallas_call | solution.py:239
  41.0 0.0 copy-done
  41.0 47.6 %attend_out.1 = f32[24,8,1024]{2,1,0:T(8,128)S(1)} custom-call(bf16[384,256]{1,0:T(8,128)(2,1)S(1)} %get-tuple-element.9.q_ref, bf16[384,256]{1,0:T(8,128)(2,1)S(1)} %get-tuple-element.10.k_ref, bf16[384,256]{1,0:T(8,128)(2,1)S(1)} %get-tuple-element.11.v_ref, bf16[256,8192]{1,0:T(8,128)(2,1)S(1)} %copy-done), custom_call_target="tpu_custom_call" | custom-call | tf_op jit(solution)/shard_map/attend_out/pallas_call | solution.py:579
  88.6 0.0 copy-done.1
  88.6 0.0 copy-done.3
  88.6 0.0 copy-done.4
  88.6 60.8 %local_window.1 = (bf16[192,1024]{1,0:T(8,128)(2,1)S(1)}, f32[8,3072]{1,0:T(8,128)S(1)}, f32[8,1024]{1,0:T(8,128)S(1)}) custom-call(bf16[192,1024]{1,0:T(8,128)(2,1)S(1)} %copy-done.3, f32[192,1024]{1,0:T(8,128)S(1)} %bitcast.5, bf16[1024,3072]{1,0:T(8,128)(2,1)} %bitcast.9, bf16[1024,1024]{1,0:T(8,128)(2,1)S(1)} %bitcast.6, bf16[192,1024]{1,0:T(8,128)(2,1)S(1)} %copy-done.4), custom_call_target="tpu_custom_call" | custom-call | tf_op jit(solution)/shard_map/local_window/pallas_call | solution.py:876
  149.4 0.7 copy.13
  150.2 0.6 copy.14
  150.8 0.6 copy.15
Async XLA Ops:
  0.6 1.0 copy-start.2
  1.6 39.4 %copy-start = (bf16[256,8192]{1,0:T(8,128)(2,1)S(1)}, bf16[256,8192]{1,0:T(8,128)(2,1)}, u32[]{:S(2)}) copy-start(bf16[256,8192]{1,0:T(8,128)(2,1)} %w_ref.3) | copy-start | bytes 12582916
  1.6 87.0 %copy-start.1 = (bf16[1,1024,1024]{2,1,0:T(8,128)(2,1)S(1)}, bf16[1,1024,1024]{2,1,0:T(8,128)(2,1)}, u32[]{:S(2)}) copy-start(bf16[1,1024,1024]{2,1,0:T(8,128)(2,1)} %param.12) | copy-start | bytes 6291460
  1.6 87.0 %copy-start.3 = (bf16[192,1024]{1,0:T(8,128)(2,1)S(1)}, bf16[192,1024]{1,0:T(8,128)(2,1)}, u32[]{:S(2)}) copy-start(bf16[192,1024]{1,0:T(8,128)(2,1)} %emb_ref.1) | copy-start | bytes 1179652
  1.6 87.0 %copy-start.4 = (bf16[192,1024]{1,0:T(8,128)(2,1)S(1)}, bf16[192,1024]{1,0:T(8,128)(2,1)}, u32[]{:S(2)}) copy-start(bf16[192,1024]{1,0:T(8,128)(2,1)} %gb_ref.1) | copy-start | bytes 1179652

commit v8 on v7

--- a/solution.py
+++ b/solution.py
@@ -619,7 +619,7 @@
     )
 
 
-SPAN = 96
+SPAN = 192
 
 
 def local_head(h, first, inside, qkv, gcore, gq, ab):

time: 152 us -> 147 us (0.967)
  Pallas kernels: 148 us -> 143 us
    pallas_call x1, Pallas kernels: 60.8 us -> 56.1 us  [local_window(): pl.pallas_call(grads_kernel, name='local_window', out_shape=(jax.ShapeDty...]
where the time goes in v8:
time: 147 us
  Pallas kernels  143 us (97%)
  local copies, waits for them, and re-layouts  3.01 us (2%)
    pallas_call x1, Pallas kernels, local_window(): pl.pallas_call(grads_kernel, name='local_window', out_shape=(jax.ShapeDty...  56.1 us
    pallas_call x1, Pallas kernels, attend_and_project(): pl.pallas_call(out_kernel, name='attend_out', out_shape=jax.ShapeDtypeStr...  47.8 us
    pallas_call x1, Pallas kernels, project_patches(): pl.pallas_call(project_kernel, name='project_patches', out_shape=[jax.Sha...  39.4 us
    unnamed x13, local copies, waits for them, and re-layouts  3.01 us

profile of v8, /device:TPU:1, one launch (start us, length us, event | category | flops | bytes accessed | tf_op | source)
XLA Modules:
  0.0 146.9 jit_solution(7717345927574448848)
XLA Ops:
  0.6 0.0 copy-start.2
  0.6 1.0 copy-done.2
  1.6 0.0 copy-start
  1.6 0.0 copy-start.1
  1.6 0.0 copy-start.3
  1.6 0.0 copy-start.4
  1.6 39.4 %project_patches.1 = (bf16[384,256]{1,0:T(8,128)(2,1)S(1)}, bf16[384,256]{1,0:T(8,128)(2,1)S(1)}, bf16[384,256]{1,0:T(8,128)(2,1)S(1)}) custom-call(bf16[192,1024]{1,0:T(8,128)(2,1)S(1)} %copy-done.2, bf16[3,8192,256]{2,1,0:T(8,128)(2,1)} %w_ref.2), custom_call_target="tpu_custom_call" | custom-call | tf_op jit(solution)/shard_map/project_patches/pallas_call | solution.py:239
  41.0 0.0 copy-done
  41.0 47.8 %attend_out.1 = f32[24,8,1024]{2,1,0:T(8,128)S(1)} custom-call(bf16[384,256]{1,0:T(8,128)(2,1)S(1)} %get-tuple-element.9.q_ref, bf16[384,256]{1,0:T(8,128)(2,1)S(1)} %get-tuple-element.10.k_ref, bf16[384,256]{1,0:T(8,128)(2,1)S(1)} %get-tuple-element.11.v_ref, bf16[256,8192]{1,0:T(8,128)(2,1)S(1)} %copy-done), custom_call_target="tpu_custom_call" | custom-call | tf_op jit(solution)/shard_map/attend_out/pallas_call | solution.py:579
  88.8 0.0 copy-done.1
  88.8 0.0 copy-done.3
  88.8 0.0 copy-done.4
  88.8 56.1 %local_window.1 = (bf16[192,1024]{1,0:T(8,128)(2,1)S(1)}, f32[8,3072]{1,0:T(8,128)S(1)}, f32[8,1024]{1,0:T(8,128)S(1)}) custom-call(bf16[192,1024]{1,0:T(8,128)(2,1)S(1)} %copy-done.3, f32[192,1024]{1,0:T(8,128)S(1)} %bitcast.5, bf16[1024,3072]{1,0:T(8,128)(2,1)} %bitcast.9, bf16[1024,1024]{1,0:T(8,128)(2,1)S(1)} %bitcast.6, bf16[192,1024]{1,0:T(8,128)(2,1)S(1)} %copy-done.4), custom_call_target="tpu_custom_call" | custom-call | tf_op jit(solution)/shard_map/local_window/pallas_call | solution.py:876
  144.9 0.7 copy.13
  145.6 0.6 copy.14
  146.3 0.6 copy.15
Async XLA Ops:
  0.6 1.0 copy-start.2
  1.6 39.4 %copy-start = (bf16[256,8192]{1,0:T(8,128)(2,1)S(1)}, bf16[256,8192]{1,0:T(8,128)(2,1)}, u32[]{:S(2)}) copy-start(bf16[256,8192]{1,0:T(8,128)(2,1)} %w_ref.3) | copy-start | bytes 12582916
  1.6 87.2 %copy-start.1 = (bf16[1,1024,1024]{2,1,0:T(8,128)(2,1)S(1)}, bf16[1,1024,1024]{2,1,0:T(8,128)(2,1)}, u32[]{:S(2)}) copy-start(bf16[1,1024,1024]{2,1,0:T(8,128)(2,1)} %param.12) | copy-start | bytes 6291460
  1.6 87.2 %copy-start.3 = (bf16[192,1024]{1,0:T(8,128)(2,1)S(1)}, bf16[192,1024]{1,0:T(8,128)(2,1)}, u32[]{:S(2)}) copy-start(bf16[192,1024]{1,0:T(8,128)(2,1)} %emb_ref.1) | copy-start | bytes 1179652
  1.6 87.2 %copy-start.4 = (bf16[192,1024]{1,0:T(8,128)(2,1)S(1)}, bf16[192,1024]{1,0:T(8,128)(2,1)}, u32[]{:S(2)}) copy-start(bf16[192,1024]{1,0:T(8,128)(2,1)} %gb_ref.1) | copy-start | bytes 1179652

commit v9 on v8

--- a/solution.py
+++ b/solution.py
@@ -1,3 +1,4 @@
+import functools
 import math
 
 import jax
@@ -53,9 +54,9 @@
 LANES = 4096
 
 
-def project_kernel(
-    bytes_ref, w_ref, q_ref, k_ref, v_ref, theirs, wide_rows, xs, ws, acc,
-    swap_send, swap_recv, w_sem, p_send, p_recv, q_send, q_recv, f_send, f_recv,
+def project_stage(
+    bytes_ref, w_ref, q_ref, k_ref, v_ref, ours, theirs, wide_rows, xs, ws, acc,
+    own_sem, swap_send, swap_recv, w_sem, p_send, p_recv, q_send, q_recv, f_send, f_recv,
 ):
     x, y, z, core = coords()
     pair = lax.rem(y, 2)
@@ -65,7 +66,13 @@
     def beside(step):
         return device_at(lax.rem(x + step, 4), y, z, core)
 
-    greet([partner, across, beside(1), beside(2), beside(3)])
+    own = pltpu.make_async_copy(bytes_ref, ours, own_sem)
+    own.start()
+    greet(
+        [partner] + [device_at(lax.rem(x + d, 4), y, z, core) for d in (1, 2, 3)]
+        + [device_at(x, lax.rem(y + d, 4), z, core) for d in (1, 2, 3)]
+        + [device_at(x, y, lax.rem(z + d, 4), core) for d in (1, 2, 3)]
+    )
     copies = []
 
     def begin(copy):
@@ -84,15 +91,16 @@
             )
             load.start()
             loads[who, c] = load
-    rows = bytes_ref.shape[0]
-    lane_tiles = bytes_ref.shape[1] // 128
+    rows = ours.shape[0]
+    lane_tiles = ours.shape[1] // 128
 
     def spread(source, side):
         at = pl.ds(pl.multiple_of(side * rows, rows), rows)
         for n in range(lane_tiles):
             wide_rows[n, at] = source[:, n * 128 : (n + 1) * 128].astype(jnp.float32)
 
-    spread(bytes_ref, core)
+    own.wait()
+    spread(ours, core)
     acc[...] = jnp.zeros_like(acc)
     swap.wait_recv()
     spread(theirs, 1 - core)
@@ -176,7 +184,8 @@
         pc[n][3].wait_recv()
         pc[n][4].wait_recv()
         begin(forwards[n])
-        multiply(0, n)
+        if n < 3:
+            multiply(0, n)
 
     def q_done(n):
         qc[n][0].wait_recv()
@@ -195,24 +204,25 @@
     q_turn(1)
     q_turn(2)
     q_turn(3)
+    p_relay(0)
     q_done(0)
-    p_relay(0)
+    p_relay(1)
     other(4)
-    p_relay(1)
     p_done(0)
+    p_relay(2)
     q_done(1)
-    p_relay(2)
     other(0)
+    p_relay(3)
     p_done(1)
-    p_relay(3)
     other(5)
+    q_done(2)
     other(1)
-    q_done(2)
     p_done(2)
     other(6)
-    other(2)
     p_done(3)
     q_done(3)
+    multiply(0, 3)
+    other(2)
     other(3)
     other(7)
 
@@ -223,40 +233,11 @@
             if j < 2:
                 value = rms_norm(value)
             out[:, at] = value.astype(jnp.bfloat16)
-    for copy in copies:
-        copy.wait_send()
-
-
-def project_patches(byte_rows, w):
-    bf, f32 = jnp.bfloat16, jnp.float32
-    vmem = pl.BlockSpec(memory_space=pltpu.VMEM)
-    rows, width = byte_rows.shape
-    total, cols = 2 * rows // PATCH * 8, w.shape[2]
-
-    def sems(*shape):
-        return pltpu.SemaphoreType.DMA(shape)
-
-    return pl.pallas_call(
-        project_kernel,
-        name="project_patches",
-        out_shape=[jax.ShapeDtypeStruct((total, cols), bf)] * 3,
-        in_specs=[vmem, pl.BlockSpec(memory_space=pl.ANY)],
-        out_specs=[vmem] * 3,
-        scratch_shapes=[
-            pltpu.VMEM((rows, width), bf),
-            pltpu.VMEM((width // 128, 2 * rows, 128), f32),
-            pltpu.VMEM((16, 2, 4, 48, CHUNK), bf),
-            pltpu.VMEM((16, 3, CHUNK, cols), bf),
-            pltpu.VMEM((3, total, cols), f32),
-            pltpu.SemaphoreType.DMA, pltpu.SemaphoreType.DMA,
-            sems(2, 8), sems(4, 5), sems(4, 5), sems(4, 4), sems(4, 4), sems(8), sems(8),
-        ],
-        compiler_params=pltpu.CompilerParams(collective_id=1, has_side_effects=True, vmem_limit_bytes=44 << 20),
-    )(byte_rows, w)
+    return copies
 
 
 def attend(
-    x, y, z, core, begin, q_ref, k_ref, v_ref, att2, q2, ka, va, acc, tall, back,
+    x, y, z, core, begin, meanwhile, q_ref, k_ref, v_ref, att2, q2, ka, va, acc, tall, back,
     y_send, y_recv, z_send, z_recv, row_send, row_recv, back_send, back_recv, swap_send, swap_recv,
 ):
     half = lax.div(y, 2)
@@ -413,6 +394,7 @@
     far_its = pl.ds(pl.multiple_of(width + (1 - half) * HEAD_DIM, HEAD_DIM), HEAD_DIM)
     returned = begin(remote(back, att2.at[:, mine], back_send, back_recv, opposite))
     near = begin(remote(att2.at[:, mine], att2.at[:, far_mine], swap_send.at[0], swap_recv.at[0], partner))
+    meanwhile()
     returned.wait_recv()
     last = begin(remote(att2.at[:, its], att2.at[:, far_its], swap_send.at[1], swap_recv.at[1], partner))
     near.wait_recv()
@@ -422,8 +404,8 @@
         pl.when(sends)(copy.wait_send)
 
 
-def out_kernel(
-    q_ref, k_ref, v_ref, w_ref, out_ref, q2, ka, va, acc, tall, back, att2, w2, pbuf, relay, near, psum, pgot, qbuf, qgot, qsum, qlast, fin, other,
+def output_stage(
+    meanwhile, q_ref, k_ref, v_ref, w_ref, out_ref, q2, ka, va, acc, tall, back, att2, w2, pbuf, relay, near, psum, pgot, qbuf, qgot, qsum, qlast, fin, other,
     w_sem, pair_send, pair_recv, p_send, p_recv, q_send, q_recv, fin_send, fin_recv,
     *att_sems,
 ):
@@ -435,10 +417,6 @@
     def beside(step):
         return device_at(lax.rem(x + step, 4), y, z, core)
 
-    greet(
-        [partner, across, beside(1), beside(2), beside(3), device_at(x, lax.rem(y + 2, 4), z, core)]
-        + [device_at(x, y, lax.rem(z + d, 4), core) for d in (1, 2, 3)]
-    )
     depth = q_ref.shape[1]
     copies = []
 
@@ -459,7 +437,7 @@
         mine[c] = pltpu.make_async_copy(w_ref.at[:, keep], w2.at[pl.ds(0, depth), into], w_sem.at[c])
         mine[c].start()
     attend(
-        x, y, z, core, begin, q_ref, k_ref, v_ref, att2, q2, ka, va, acc, tall, back, *att_sems
+        x, y, z, core, begin, meanwhile, q_ref, k_ref, v_ref, att2, q2, ka, va, acc, tall, back, *att_sems
     )
 
     right, left, far = lax.rem(x + 1, 4), lax.rem(x + 3, 4), lax.rem(x + 2, 4)
@@ -561,48 +539,7 @@
     end.wait_recv()
     for b in range(4):
         out_ref[:, (1 - core) * 4 + b, :] = other[:, b * 1024 : b * 1024 + 1024]
-    for copy in copies:
-        copy.wait_send()
-
-
-def attend_and_project(q, k, v, w):
-    rows, depth = q.shape
-    bf, f32 = jnp.bfloat16, jnp.float32
-    vmem = pl.BlockSpec(memory_space=pltpu.VMEM)
-
-    def units(*lead):
-        return pltpu.VMEM((*lead, 48, CHUNK), bf)
-
-    def sems(*shape):
-        return pltpu.SemaphoreType.DMA(shape)
-
-    return pl.pallas_call(
-        out_kernel,
-        name="attend_out",
-        out_shape=jax.ShapeDtypeStruct((24, 8, 1024), f32),
-        in_specs=[vmem] * 3 + [pl.BlockSpec(memory_space=pl.ANY)],
-        out_specs=vmem,
-        scratch_shapes=[
-            pltpu.VMEM((2, rows, HEAD_DIM), bf),
-            pltpu.VMEM((4, 2, rows, HEAD_DIM), bf),
-            pltpu.VMEM((4, 2, rows, HEAD_DIM), bf),
-            pltpu.VMEM((2, rows, 2 * HEAD_DIM), f32),
-            pltpu.VMEM((8 + 2 * rows, HEAD_DIM), f32),
-            pltpu.VMEM((rows, HEAD_DIM), bf),
-            pltpu.VMEM((rows, 2 * depth), bf),
-            pltpu.VMEM((2 * depth, LANES), bf),
-            units(4, 4, 2), units(4, 2), units(4, 2, 2), units(4, 2), units(4),
-            units(4, 2, 4), units(4, 4), units(4, 4), units(4, 3),
-            pltpu.VMEM((48, LANES), f32),
-            pltpu.VMEM((24, LANES), f32),
-            sems(8), sems(8), sems(8), sems(4, 7), sems(4, 7), sems(4, 4), sems(4, 4),
-            pltpu.SemaphoreType.DMA, pltpu.SemaphoreType.DMA,
-            sems(3), sems(3), sems(4, 2, 2), sems(4, 2, 2),
-            pltpu.SemaphoreType.DMA, pltpu.SemaphoreType.DMA,
-            pltpu.SemaphoreType.DMA, pltpu.SemaphoreType.DMA, sems(2), sems(2),
-        ],
-        compiler_params=pltpu.CompilerParams(collective_id=3, has_side_effects=True, vmem_limit_bytes=40 << 20),
-    )(q, k, v, w)
+    return copies
 
 
 PART_COLS = (640, 640, 768)
@@ -622,11 +559,13 @@
 SPAN = 192
 
 
-def local_head(h, first, inside, qkv, gcore, gq, ab):
+def local_head(group, i, first, inside, qkv, gcore, gq, ab):
     rows = slice(first, first + SPAN)
     bf = jnp.bfloat16
     width = gcore.shape[1]
+    h = group * (LOCAL_HEADS // 2) + i
     at = [pl.ds(pl.multiple_of(n * width + h * LOCAL_HEAD_DIM, LOCAL_HEAD_DIM), LOCAL_HEAD_DIM) for n in range(3)]
+    into = [slice(n * width // 2 + i * LOCAL_HEAD_DIM, n * width // 2 + (i + 1) * LOCAL_HEAD_DIM) for n in range(3)]
     q, k, v = (qkv[rows, part] for part in at)
     q_scale, k_scale = rms_scale(q), rms_scale(k)
     qn, kn = q * q_scale, k * k_scale
@@ -643,13 +582,13 @@
     def through_rms(grad, normed, factor):
         return (factor * (grad - normed * jnp.mean(grad * normed, axis=-1, keepdims=True))).astype(bf)
 
-    gq[rows, at[0]] = through_rms(cross(ds, kb, 1, 0), qn, q_scale)
-    gq[rows, at[1]] = through_rms(cross(ds, qb, 0, 0), kn, k_scale)
-    gq[rows, at[2]] = cross(pb, back, 0, 0).astype(bf)
-
-
-def grads_kernel(
-    emb_ref, ctx_ref, wqkv_ref, wout_ref, gb_ref, hid_ref, out_q, out_o,
+    gq[group, rows, into[0]] = through_rms(cross(ds, kb, 1, 0), qn, q_scale)
+    gq[group, rows, into[1]] = through_rms(cross(ds, qb, 0, 0), kn, k_scale)
+    gq[group, rows, into[2]] = cross(pb, back, 0, 0).astype(bf)
+
+
+def local_stage(
+    emb_ref, ctx_ref, weights, gb_ref, hid_ref, out_q, out_o,
     state, qkv, gcore, gq, xt, abt, xn2, gq2, ab2, gb2,
     part0, part1, part2, relay0, relay1, relay2, near0, near1, near2,
     sum0, sum1, sum2, got0, got1, got2, low0, low1, low2, last0, last1, last2,
@@ -665,53 +604,54 @@
         return device_at(*at)
 
     partner = device_at(place[0], place[1], place[2], 1 - core)
-    greet([partner] + [peer_along(axis, step) for axis in range(3) for step in (1, 2, 3)])
-
     rows, width = emb_ref.shape
     qh, oh = gq2.shape[1], gb2.shape[1]
-    mine_q, mine_o = pl.multiple_of(core * qh, qh), pl.multiple_of(core * oh, oh)
-    its_q, its_o = pl.multiple_of((1 - core) * qh, qh), pl.multiple_of((1 - core) * oh, oh)
+    mine_o, its_o = pl.multiple_of(core * oh, oh), pl.multiple_of((1 - core) * oh, oh)
     top, bottom = pl.ds(0, rows), pl.ds(rows, rows)
     swaps = [
         remote(xn2.at[top], xn2.at[bottom], pair_send.at[0], pair_recv.at[0], partner),
-        remote(gq.at[:, pl.ds(its_q, qh)], gq2.at[bottom], pair_send.at[1], pair_recv.at[1], partner),
+        remote(gq.at[1 - core], gq2.at[bottom], pair_send.at[1], pair_recv.at[1], partner),
         remote(ab2.at[top], ab2.at[bottom], pair_send.at[2], pair_recv.at[2], partner),
         remote(gb_ref.at[:, pl.ds(its_o, oh)], gb2.at[bottom], pair_send.at[3], pair_recv.at[3], partner),
     ]
     swaps[3].start()
-    state[...] = emb_ref[...].astype(jnp.float32) + ctx_ref[...].astype(jnp.bfloat16).astype(jnp.float32)
+    state[...] = emb_ref[...].astype(jnp.float32) + ctx_ref[...].reshape(rows, width).astype(jnp.bfloat16).astype(jnp.float32)
     normed = (state[...] * rms_scale(state[...])).astype(jnp.bfloat16)
     xn2[top] = normed
     swaps[0].start()
     gb2[top] = gb_ref[:, pl.ds(mine_o, oh)]
 
+    def product(left, n, first):
+        blocks = [n, first + n]
+        return sum(
+            jnp.dot(
+                left[top, r * 512 : (r + 1) * 512], weights[lax.div(at, 3), lax.rem(at, 3)],
+                preferred_element_type=jnp.float32,
+            )
+            for r, at in enumerate(blocks)
+        )
+
     def project(n, carry):
-        at = pl.ds(pl.multiple_of(n * 512, 512), 512)
-        qkv[:, at] = jnp.dot(xn2[top], wqkv_ref[:, at], preferred_element_type=jnp.float32)
+        qkv[:, pl.ds(pl.multiple_of(n * 256, 256), 256)] = product(xn2, n, 12)
         return carry
 
-    lax.fori_loop(0, 3 * width // 512, project, 0)
-    for n in range(2):
-        at = slice(n * width // 2, (n + 1) * width // 2)
-        gcore[:, at] = cross(gb_ref[...], wout_ref[at], 1, 1)
+    lax.fori_loop(0, 3 * width // 256, project, 0)
     row = lax.broadcasted_iota(jnp.int32, (SPAN, SPAN), 0)
     column = lax.broadcasted_iota(jnp.int32, (SPAN, SPAN), 1)
     inside = (column <= row) & (column >= row - lax.rem(row, PATCH))
 
-    def heads(n, carry):
-        for i in range(8):
-            h = 8 * n + i
+    for group in (1 - core, core):
+        for i in range(LOCAL_HEADS // 2):
             for first in range(0, rows, SPAN):
-                local_head(h, first, inside, qkv, gcore, gq, ab2)
-        return carry
-
-    lax.fori_loop(0, LOCAL_HEADS // 8, heads, 0)
-    swaps[1].start()
+                local_head(group, i, first, inside, qkv, gcore, gq, ab2)
+        if group is not core:
+            swaps[1].start()
     swaps[2].start()
-    gq2[top] = gq[:, pl.ds(mine_q, qh)]
+    gq2[top] = gq[core]
     xt[0] = xn2[top].T
     swaps[0].wait_recv()
     xt[1] = xn2[bottom].T
+    abt[0] = ab2[top].T
 
     parts = (part0, part1, part2)
     relays, nears = (relay0, relay1, relay2), (near0, near1, near2)
@@ -832,7 +772,6 @@
     fill(part1, PART_ORDERS[1], xt, gq2, (PART_COLS[0], split), 0)
     first.append(stage1(1))
     fill(part2, PART_ORDERS[2], xt, gq2, (split, qh), 0)
-    abt[0] = ab2[top].T
     swaps[2].wait_recv()
     abt[1] = ab2[bottom].T
     swaps[3].wait_recv()
@@ -840,9 +779,16 @@
     first.append(stage1(2))
     add_relay(0, *first[0])
     add_relay(1, *first[1])
-    hid_ref[...] = (
-        state[...] + jnp.dot(ab2[top], wout_ref[...], preferred_element_type=jnp.float32)
-    ).astype(jnp.bfloat16)
+    for c in range(4):
+        at = slice(c * 256, (c + 1) * 256)
+        moved = sum(
+            jnp.dot(
+                ab2[top, r * 512 : (r + 1) * 512], weights[(24 + r * 4 + c) // 3, (24 + r * 4 + c) % 3],
+                preferred_element_type=jnp.float32,
+            )
+            for r in range(2)
+        )
+        hid_ref[:, at] = (state[:, at] + moved).astype(jnp.bfloat16)
     add_relay(2, *first[2])
     second = [stage2(k, first[k][0]) for k in range(3)]
     third = [stage3(k, second[k]) for k in range(3)]
@@ -852,42 +798,113 @@
     keep, give = pl.multiple_of(core * 8, 8), pl.multiple_of((1 - core) * 8, 8)
     end = remote(fin.at[pl.ds(give, 8)], other, fin_send, fin_recv, partner)
     end.start()
-    out_q[:, pl.ds(mine_q, qh)] = fin[pl.ds(keep, 8), 0:qh]
+    third_of = qh // 3
+    for n in range(3):
+        at = pl.ds(pl.multiple_of(n * width + core * third_of, third_of), third_of)
+        out_q[:, at] = fin[pl.ds(keep, 8), n * third_of : (n + 1) * third_of]
     out_o[:, pl.ds(mine_o, oh)] = fin[pl.ds(keep, 8), qh : qh + oh]
     end.wait_recv()
-    out_q[:, pl.ds(its_q, qh)] = other[:, 0:qh]
+    for n in range(3):
+        at = pl.ds(pl.multiple_of(n * width + (1 - core) * third_of, third_of), third_of)
+        out_q[:, at] = other[:, n * third_of : (n + 1) * third_of]
     out_o[:, pl.ds(its_o, oh)] = other[:, qh : qh + oh]
     for copy in swaps + [c for f in first for c in f[0]] + [c for s in second + third for c in s] + [end]:
         copy.wait_send()
 
 
-def local_window(emb, context, w_qkv, w_out, cotangent):
-    rows, width = emb.shape
+def window_kernel(counts, *refs):
+    byte_embeds, local_embeds, global_qkv, global_out, local_qkv, local_out, cotangent = refs[:7]
+    hidden, grad_qkv, grad_out = refs[7:10]
+    q, k, v, context, emb, cot, in_sems = refs[10:17]
+    stages, at = [], 17
+    for count in counts:
+        stages.append(refs[at : at + count])
+        at += count
+    for_project, for_output, for_local = stages
+    sent = project_stage(byte_embeds, global_qkv, q, k, v, *for_project)
+    weights = for_project[4]
+    loads = [
+        pltpu.make_async_copy(local_embeds, emb, in_sems.at[32]),
+        pltpu.make_async_copy(cotangent, cot, in_sems.at[33]),
+    ]
+    for source, blocks, first in ((local_qkv, 12, 0), (local_out, 4, 24)):
+        for r in range(2):
+            for c in range(blocks):
+                n = first + r * blocks + c
+                part = source.at[r * 512 : (r + 1) * 512, c * 256 : (c + 1) * 256]
+                loads.append(pltpu.make_async_copy(part, weights.at[n // 3, n % 3], in_sems.at[n]))
+    for load in loads:
+        load.start()
+    gcore = for_local[2]
+
+    def meanwhile():
+        for load in loads:
+            load.wait()
+        for r in range(2):
+            gcore[:, r * 512 : (r + 1) * 512] = sum(
+                cross(cot[:, c * 256 : (c + 1) * 256], weights[(24 + r * 4 + c) // 3, (24 + r * 4 + c) % 3], 1, 1)
+                for c in range(4)
+            )
+
+    sent += output_stage(meanwhile, q, k, v, global_out, context, *for_output)
+    local_stage(emb, context, weights, cot, hidden, grad_qkv, grad_out, *for_local)
+    for copy in sent:
+        copy.wait_send()
+
+
+def window(byte_rows, emb, w, w_global_out, w_qkv, w_out, cotangent):
+    bf, f32 = jnp.bfloat16, jnp.float32
+    rows, width = byte_rows.shape
+    total, cols = 2 * rows // PATCH * 8, w.shape[2]
     qw, ow = w_qkv.shape[1], w_out.shape[1]
-    bf, f32 = jnp.bfloat16, jnp.float32
-    vmem = pl.BlockSpec(memory_space=pltpu.VMEM)
+
+    def sems(*shape):
+        return pltpu.SemaphoreType.DMA(shape)
+
+    def units(*lead):
+        return pltpu.VMEM((*lead, 48, CHUNK), bf)
 
     def each(*lead):
         return [pltpu.VMEM((*lead, 16, c), bf) for c in PART_COLS]
 
-    def sems(*shape):
-        return pltpu.SemaphoreType.DMA(shape)
-
-    return pl.pallas_call(
-        grads_kernel,
-        name="local_window",
-        out_shape=(
-            jax.ShapeDtypeStruct((rows, width), bf),
-            jax.ShapeDtypeStruct((8, qw), f32),
-            jax.ShapeDtypeStruct((8, ow), f32),
-        ),
-        in_specs=[vmem] * 5,
-        out_specs=(vmem,) * 3,
-        scratch_shapes=[
+    parts = [
+        [
+
+            pltpu.VMEM((rows, width), bf),
+            pltpu.VMEM((rows, width), bf),
+            pltpu.VMEM((width // 128, 2 * rows, 128), f32),
+            pltpu.VMEM((16, 2, 4, 48, CHUNK), bf),
+            pltpu.VMEM((16, 3, CHUNK, cols), bf),
+            pltpu.VMEM((3, total, cols), f32),
+            pltpu.SemaphoreType.DMA, pltpu.SemaphoreType.DMA, pltpu.SemaphoreType.DMA,
+            sems(2, 8), sems(4, 5), sems(4, 5), sems(4, 4), sems(4, 4), sems(8), sems(8),
+        ],
+        [
+
+            pltpu.VMEM((2, total, HEAD_DIM), bf),
+            pltpu.VMEM((4, 2, total, HEAD_DIM), bf),
+            pltpu.VMEM((4, 2, total, HEAD_DIM), bf),
+            pltpu.VMEM((2, total, 2 * HEAD_DIM), f32),
+            pltpu.VMEM((8 + 2 * total, HEAD_DIM), f32),
+            pltpu.VMEM((total, HEAD_DIM), bf),
+            pltpu.VMEM((total, 2 * cols), bf),
+            pltpu.VMEM((2 * cols, LANES), bf),
+            units(4, 4, 2), units(4, 2), units(4, 2, 2), units(4, 2), units(4),
+            units(4, 2, 4), units(4, 4), units(4, 4), units(4, 3),
+            pltpu.VMEM((48, LANES), f32),
+            pltpu.VMEM((24, LANES), f32),
+            sems(8), sems(8), sems(8), sems(4, 7), sems(4, 7), sems(4, 4), sems(4, 4),
+            pltpu.SemaphoreType.DMA, pltpu.SemaphoreType.DMA,
+            sems(3), sems(3), sems(4, 2, 2), sems(4, 2, 2),
+            pltpu.SemaphoreType.DMA, pltpu.SemaphoreType.DMA,
+            pltpu.SemaphoreType.DMA, pltpu.SemaphoreType.DMA, sems(2), sems(2),
+        ],
+        [
+
             pltpu.VMEM((rows, width), f32),
             pltpu.VMEM((rows, qw), f32),
             pltpu.VMEM((rows, width), f32),
-            pltpu.VMEM((rows, qw), bf),
+            pltpu.VMEM((2, rows, qw // 2), bf),
             pltpu.VMEM((2, width, rows), bf),
             pltpu.VMEM((2, width, rows), bf),
             pltpu.VMEM((2 * rows, width), bf),
@@ -901,14 +918,33 @@
             sems(4), sems(4), sems(3, 6), sems(3, 6), sems(3, 3), sems(3, 3), sems(3, 3), sems(3, 3),
             pltpu.SemaphoreType.DMA, pltpu.SemaphoreType.DMA,
         ],
-        compiler_params=pltpu.CompilerParams(collective_id=5, has_side_effects=True, vmem_limit_bytes=44 << 20),
-    )(emb, context, w_qkv, w_out, cotangent)
+    ]
+    inner = [pltpu.VMEM((total, cols), bf)] * 3 + [
+        pltpu.VMEM((rows // PATCH, PATCH, width), f32),
+        pltpu.VMEM((rows, width), bf),
+        pltpu.VMEM((rows, width), bf),
+        sems(34),
+    ]
+    vmem = pl.BlockSpec(memory_space=pltpu.VMEM)
+    return pl.pallas_call(
+        functools.partial(window_kernel, [len(part) for part in parts]),
+        name="window",
+        out_shape=(
+            jax.ShapeDtypeStruct((rows, width), bf),
+            jax.ShapeDtypeStruct((8, qw), f32),
+            jax.ShapeDtypeStruct((8, ow), f32),
+        ),
+        in_specs=[pl.BlockSpec(memory_space=pl.ANY)] * 7,
+        out_specs=(vmem,) * 3,
+        scratch_shapes=inner + [shape for part in parts for shape in part],
+        compiler_params=pltpu.CompilerParams(collective_id=1, has_side_effects=True, vmem_limit_bytes=67043328),
+    )(byte_rows, emb, w, w_global_out, w_qkv, w_out, cotangent)
 
 
 def per_device(byte_embeds, local_embeds, global_qkv, global_out, local_qkv, local_out, cotangent):
-    flat = project_patches(byte_embeds, global_qkv)
-    context = attend_and_project(*flat, global_out).reshape(local_embeds.shape)
-    hidden, grad_qkv, grad_out = local_window(local_embeds, context, local_qkv[0], local_out[0], cotangent)
+    hidden, grad_qkv, grad_out = window(
+        byte_embeds, local_embeds, global_qkv, global_out, local_qkv[0], local_out[0], cotangent
+    )
     return (hidden, grad_qkv[None], grad_out[None])
 
 

time: 147 us -> 143 us (0.973)
  Pallas kernels: 143 us -> 137 us
  local copies, waits for them, and re-layouts: 3.01 us -> 4.68 us
    pallas_call x3 -> x1, Pallas kernels: 143 us -> 137 us  [window(): pl.pallas_call(functools.partial(window_kernel, [len(part) for part in pa...]
    unnamed x13 -> x3, local copies, waits for them, and re-layouts: 3.01 us -> 4.68 us
where the time goes in v9:
time: 143 us
  Pallas kernels  137 us (96%)
  local copies, waits for them, and re-layouts  4.68 us (3%)
    pallas_call x1, Pallas kernels, window(): pl.pallas_call(functools.partial(window_kernel, [len(part) for part in pa...  137 us
    unnamed x3, local copies, waits for them, and re-layouts  4.68 us

profile of v9, /device:TPU:1, one launch (start us, length us, event | category | flops | bytes accessed | tf_op | source)
XLA Modules:
  0.0 142.8 jit_solution(11156376953338201157)
XLA Ops:
  0.6 137.4 %window.1 = (bf16[192,1024]{1,0:T(8,128)(2,1)}, f32[8,3072]{1,0:T(8,128)}, f32[8,1024]{1,0:T(8,128)}) custom-call(bf16[192,1024]{1,0:T(8,128)(2,1)} %refs_0_.1, bf16[192,1024]{1,0:T(8,128)(2,1)} %refs_1_.1, bf16[3,8192,256]{2,1,0:T(8,128)(2,1)} %refs_2_.1, bf16[256,8192]{1,0:T(8,128)(2,1)} %refs_3_.1, bf16[1024,3072]{1,0:T(8,128)(2,1)} %bitcast.4, ...), custom_call_target="tpu_custom_call" | custom-call | tf_op jit(solution)/shard_map/window/pallas_call | solution.py:929
  138.1 1.8 %copy.13 = bf16[192,1024]{1,0:T(8,128)(2,1)} copy(bf16[192,1024]{1,0:T(8,128)(2,1)} %get-tuple-element.12) | data formatting | bytes 786432
  139.9 1.5 %copy.14 = f32[1,8,3072]{2,1,0:T(8,128)} copy(f32[1,8,3072]{2,1,0:T(8,128)} %bitcast.6) | data formatting | bytes 196608
  141.4 1.4 copy.15

commit v10 on v9

--- a/solution.py
+++ b/solution.py
@@ -542,7 +542,7 @@
     return copies
 
 
-PART_COLS = (640, 640, 768)
+PART_COLS = (768, 640, 640)
 PART_ORDERS = ((0, 1, 2), (1, 2, 0), (2, 0, 1))
 
 
@@ -779,6 +779,7 @@
     first.append(stage1(2))
     add_relay(0, *first[0])
     add_relay(1, *first[1])
+    add_relay(2, *first[2])
     for c in range(4):
         at = slice(c * 256, (c + 1) * 256)
         moved = sum(
@@ -789,7 +790,6 @@
             for r in range(2)
         )
         hid_ref[:, at] = (state[:, at] + moved).astype(jnp.bfloat16)
-    add_relay(2, *first[2])
     second = [stage2(k, first[k][0]) for k in range(3)]
     third = [stage3(k, second[k]) for k in range(3)]
     for k in range(3):

time: 143 us -> 139 us (0.972)
  Pallas kernels: 137 us -> 133 us
    pallas_call x1, Pallas kernels: 137 us -> 133 us  [window(): pl.pallas_call(functools.partial(window_kernel, [len(part) for part in pa...]
where the time goes in v10:
time: 139 us; the launch traced here: 138 us
  Pallas kernels  133 us (96%)
  local copies, waits for them, and re-layouts  4.68 us (3%)
    pallas_call x1, Pallas kernels, window(): pl.pallas_call(functools.partial(window_kernel, [len(part) for part in pa...  133 us
    unnamed x3, local copies, waits for them, and re-layouts  4.68 us

profile of v10, /device:TPU:1, one launch (start us, length us, event | category | flops | bytes accessed | tf_op | source)
XLA Modules:
  0.0 138.5 jit_solution(4653562909919036728)
XLA Ops:
  0.6 133.2 %window.1 = (bf16[192,1024]{1,0:T(8,128)(2,1)}, f32[8,3072]{1,0:T(8,128)}, f32[8,1024]{1,0:T(8,128)}) custom-call(bf16[192,1024]{1,0:T(8,128)(2,1)} %refs_0_.1, bf16[192,1024]{1,0:T(8,128)(2,1)} %refs_1_.1, bf16[3,8192,256]{2,1,0:T(8,128)(2,1)} %refs_2_.1, bf16[256,8192]{1,0:T(8,128)(2,1)} %refs_3_.1, bf16[1024,3072]{1,0:T(8,128)(2,1)} %bitcast.4, ...), custom_call_target="tpu_custom_call" | custom-call | tf_op jit(solution)/shard_map/window/pallas_call | solution.py:929
  133.8 1.8 %copy.13 = bf16[192,1024]{1,0:T(8,128)(2,1)} copy(bf16[192,1024]{1,0:T(8,128)(2,1)} %get-tuple-element.12) | data formatting | bytes 786432
  135.6 1.5 %copy.14 = f32[1,8,3072]{2,1,0:T(8,128)} copy(f32[1,8,3072]{2,1,0:T(8,128)} %bitcast.6) | data formatting | bytes 196608
  137.1 1.4 copy.15
